TPU v7x, 32 devices: a whole 2x2x4 slice. The times are simulated.
32 devices in a mesh: stream: 2 (over core), batch: 16 (over z, y, x).
Axes of the slice: x: 2, y: 2, z: 4, core: 2. Of those that a mesh axis runs over, the one named last changes fastest.
Arguments:
- inputs: bfloat16 [2, 16, 1024, 768], P('stream', 'batch'), may hold values from -6 to 6
- lengths: int32 [16], P('batch'), may hold values from 128 to 1024, as said below
- cotangent: bfloat16 [2, 16, 1024, 768], P('stream', 'batch'), may hold values from -6 to 6
- qkv_weight: bfloat16 [768, 2304], replicated, may hold values from -0.21875 to 0.21875
- out_weight: bfloat16 [768, 768], replicated, may hold values from -2 to 2
- up_weight: bfloat16 [768, 3072], replicated, may hold values from -0.21875 to 0.21875
- down_weight: bfloat16 [3072, 768], replicated, may hold values from -0.109375 to 0.109375
- attn_gain: float32 [768], replicated, may hold values from 0.5 to 1.5
- mlp_gain: float32 [768], replicated, may hold values from 0.5 to 1.5
Outputs:
- outputs: bfloat16 [2, 16, 1024, 768], P('stream', 'batch')
- input_grad: bfloat16 [2, 16, 1024, 768], P('stream', 'batch')
- qkv_grad: float32 [768, 2304], P(('stream', 'batch'))
- out_grad: float32 [768, 768], P(('stream', 'batch'))
- up_grad: float32 [768, 3072], P(None, ('stream', 'batch'))
- down_grad: float32 [3072, 768], P(('stream', 'batch'))
- attn_gain_grad: float32 [768], replicated
- mlp_gain_grad: float32 [768], replicated
- rms: float32 [3], replicated
Inputs may be any that keep to these rules, and one draw needn't show every extreme that they name: `lengths`: each length is a multiple of 16; some row has length 1024.
All inputs are finite; a program needn't handle non-finite values.
Results may differ from a plain program's by a relative error of at most 0.014.
Values may be sent and summed in bfloat16 or wider, within the bound.
No kernel may reach another device: no remote copies, remote signals or barrier semaphores. Data moves between devices by JAX's collectives and lax.ppermute only.
A program may use at most 384 MiB of HBM per device.

v0:
```python
import functools

import jax
import jax.numpy as jnp
import numpy as np
from jax import lax
from jax.experimental import pallas as pl
from jax.experimental.pallas import tpu as pltpu
from jax.sharding import PartitionSpec as P

f32 = jnp.float32
bf16 = jnp.bfloat16

HD = 64
BLK = 16
EPS = 1e-06
NEG = -1e30
PW = 2 * HD
T = 128
R = 256
FC = 512
SCALE = HD**-0.5
BIG = 60
GROUPS = 3

SMEM = pl.BlockSpec(memory_space=pltpu.SMEM)


def params(mib):
    return pltpu.CompilerParams(vmem_limit_bytes=mib << 20)


def shape(dims, dtype):
    return jax.ShapeDtypeStruct(dims, dtype)


def nn(a, b):
    return jnp.dot(a, b, preferred_element_type=f32)


def nt(a, b):
    return lax.dot_general(a, b, (((1,), (1,)), ((), ())), preferred_element_type=f32)


def tn(a, b):
    return lax.dot_general(a, b, (((0,), (0,)), ((), ())), preferred_element_type=f32)


def whole(dims):
    return pl.BlockSpec(dims, lambda *_: (0,) * len(dims), pipeline_mode=pl.Buffered(1))


def inv_rms(v):
    return lax.rsqrt(jnp.mean(v * v, axis=-1, keepdims=True) + EPS)


def norm_back(v, gain, grad):
    r = inv_rms(v)
    unit = v * r
    scaled = grad * gain
    inner = jnp.mean(scaled * unit, axis=-1, keepdims=True)
    return r * (scaled - unit * inner), grad * unit


def rotary_tables(length):
    half = HD // 2
    freqs = np.exp(-np.log(10000.0) * np.arange(half) / half).astype(np.float32)
    angles = (np.arange(length, dtype=np.float32)[:, None] * freqs[None, :]).astype(np.float64)
    return np.cos(angles).astype(np.float32), np.sin(angles).astype(np.float32)


def rotated(v, cosine, signed, sign):
    first = lax.broadcasted_iota(jnp.int32, (1, PW), 1) % HD < HD // 2
    outs = []
    for c in range(0, v.shape[1], PW):
        part = v[:, c : c + PW]
        partner = jnp.where(first, pltpu.roll(part, PW - HD // 2, 1), pltpu.roll(part, HD // 2, 1))
        outs.append(part * cosine + partner * (signed * sign))
    return outs[0] if len(outs) == 1 else jnp.concatenate(outs, axis=1)


def token_weight(start, length, rows):
    return lax.broadcasted_iota(jnp.int32, (rows, 1), 0) + start < length


def row_sum(v):
    return jnp.sum(v, axis=0, keepdims=True)


def project_kernel(info, x, gain, wq, wk, wv, cosine, signed, q, k, v, h1t, sums):
    at = pl.program_id(0)

    @pl.when(at == 0)
    def _():
        sums[...] = jnp.zeros_like(sums)

    value = x[...].astype(f32)
    h1 = (value * inv_rms(value) * gain[...]).astype(bf16)
    q[...] = rotated(nn(h1, wq[...]), cosine[...], signed[...], 1.0).astype(bf16)
    k[...] = rotated(nn(h1, wk[...]), cosine[...], signed[...], 1.0).astype(bf16)
    v[...] = nn(h1, wv[...]).astype(bf16)
    h1t[...] = h1.T
    weight = token_weight(at * R, info[1], R)
    sums[0:1, :] += row_sum(jnp.where(weight, value * value, 0.0))


def project(info, x, gain, weight, tables):
    seq, width = x.shape
    rows = pl.BlockSpec((R, width), lambda i: (i, 0))
    table = pl.BlockSpec((R, PW), lambda i: (i, 0))
    third = lambda c: pl.BlockSpec((width, width), lambda i: (0, c), pipeline_mode=pl.Buffered(1))
    return pl.pallas_call(
        project_kernel,
        grid=(seq // R,),
        in_specs=[SMEM, rows, whole((1, width)), third(0), third(1), third(2), table, table],
        out_specs=[rows, rows, rows, pl.BlockSpec((width, R), lambda i: (0, i)), whole((8, width))],
        out_shape=[shape((seq, width), bf16)] * 3 + [shape((width, seq), bf16), shape((8, width), f32)],
        compiler_params=params(BIG),
        cost_estimate=pl.CostEstimate(
            flops=2 * seq * width * 3 * width, bytes_accessed=12 * seq * width, transcendentals=0
        ),
        name="project",
    )(info, x, gain, weight, weight, weight, *tables)


def stacked(tile, low):
    zero = jnp.zeros_like(tile)
    return jnp.concatenate([jnp.where(low, tile, zero), jnp.where(low, zero, tile)], axis=0)


def unstacked(tile_t):
    half = lax.broadcasted_iota(jnp.int32, (PW, 1), 0) < HD
    return jnp.where(half, tile_t[:, :T], tile_t[:, T:])


def chunks_of(i):
    out, j = [], 0
    while j < i:
        n = 2 if i - j >= 2 else 1
        out.append((j * T, n * T))
        j += n
    return out


def edge_masks(noisy):
    row = lax.broadcasted_iota(jnp.int32, (T, 2 * T), 0) // BLK
    col = (lax.broadcasted_iota(jnp.int32, (T, 2 * T), 1) % T) // BLK
    own = jnp.logical_or(row == col, jnp.logical_and(row < col, noisy == 0))
    other = jnp.logical_and(row < col, noisy == 1)
    return own, other


def masked(s, start, length):
    pos = lax.broadcasted_iota(jnp.int32, s.shape, 0) + start
    return jnp.where(pos < length, s, NEG)


def over_rows(op, v):
    return op(v.reshape(v.shape[0] // 8, 8, v.shape[1]), axis=0)


def attend_pair(noisy, length, q, ko, vo, kc, vc, store, lse, vo_t, vc_t, scores):
    seq = q.shape[0]
    low = lax.broadcasted_iota(jnp.int32, (1, PW), 1) < HD
    own_mask, other_mask = edge_masks(noisy)
    vo_t[...] = vo[...].T
    vc_t[...] = vc[...].T
    for i in range(seq // T):
        at = pl.ds(i * T, T)
        q2 = stacked(q[at, :] * bf16(SCALE), low)
        buf = scores.at[i % 2]
        edge = nt(jnp.concatenate([ko[at, :], kc[at, :]], 0), q2)
        own = masked(jnp.where(own_mask, edge[:T], NEG), i * T, length)
        other = masked(jnp.where(other_mask, edge[T:], NEG), i * T, length)
        buf[pl.ds(0, T), :] = own
        buf[pl.ds(T, T), :] = other
        top = over_rows(jnp.max, jnp.maximum(own, other))
        for start, size in chunks_of(i):
            s = masked(nt(kc[pl.ds(start, size), :], q2), start, length)
            buf[pl.ds(2 * T + start, size), :] = s
            top = jnp.maximum(top, over_rows(jnp.max, s))
        top = jnp.max(top, axis=0, keepdims=True)
        p = jnp.exp(buf[pl.ds(0, 2 * T), :] - top)
        total = over_rows(jnp.sum, p)
        acc = nn(jnp.concatenate([vo_t[:, at], vc_t[:, at]], 1), p.astype(bf16))
        for start, size in chunks_of(i):
            p = jnp.exp(buf[pl.ds(2 * T + start, size), :] - top)
            total = total + over_rows(jnp.sum, p)
            acc = acc + nn(vc_t[:, pl.ds(start, size)], p.astype(bf16))
        total = row_sum(total)
        lse[0, pl.ds(i, 1), :] = top + jnp.log(total)
        store(at, unstacked(acc / total))


def turned_back(v, cosine, sine):
    quarter = HD // 2
    a, b, c, d = (v[i * quarter : (i + 1) * quarter] for i in range(4))
    return jnp.concatenate(
        [a * cosine + b * sine, b * cosine - a * sine, c * cosine + d * sine, d * cosine - c * sine]
    )


def attend_back_kernel(
    info, q, ko, vo, kc, vc, o, do, lse, cosine, sine, dq, keep, send, ko_t, kc_t, dko, dvo, dkc, dvc
):
    noisy, length = info[0], info[1]
    seq = q.shape[0]
    low = lax.broadcasted_iota(jnp.int32, (1, PW), 1) < HD
    own_mask, other_mask = edge_masks(noisy)
    ko_t[...] = ko[...].T
    kc_t[...] = kc[...].T
    for i in range(seq // T):
        at = pl.ds(i * T, T)
        q2 = stacked(q[at, :] * bf16(SCALE), low)
        do2 = stacked(do[at, :], low)
        prod = (do[at, :].astype(f32) * o[at, :].astype(f32)).T
        delta = jnp.concatenate([row_sum(prod[:HD]), row_sum(prod[HD:])], 1)
        norm = lse[0, pl.ds(i, 1), :]
        s = nt(jnp.concatenate([ko[at, :], kc[at, :]], 0), q2)
        own = masked(jnp.where(own_mask, s[:T], NEG), i * T, length)
        other = masked(jnp.where(other_mask, s[T:], NEG), i * T, length)
        p = jnp.exp(jnp.concatenate([own, other], 0) - norm)
        dp = nt(jnp.concatenate([vo[at, :], vc[at, :]], 0), do2)
        ds = (p * (dp - delta)).astype(bf16)
        dv = nn(p.astype(bf16), do2)
        dk = nn(ds, q2)
        dvo[at, :] = dv[:T]
        dko[at, :] = dk[:T]
        dvc[at, :] = dv[T:]
        dkc[at, :] = dk[T:]
        dq_t = nn(jnp.concatenate([ko_t[:, at], kc_t[:, at]], 1), ds)
        for start, size in chunks_of(i):
            rows = pl.ds(start, size)
            p = jnp.exp(masked(nt(kc[rows, :], q2), start, length) - norm)
            ds = (p * (nt(vc[rows, :], do2) - delta)).astype(bf16)
            dvc[rows, :] += nn(p.astype(bf16), do2)
            dkc[rows, :] += nn(ds, q2)
            dq_t = dq_t + nn(kc_t[:, rows], ds)
        dq[at, :] = (turned_back(unstacked(dq_t), cosine[:, at], sine[:, at]) * SCALE).T.astype(bf16)
    clean = (1 - noisy).astype(f32)
    for at, own, other in ((0, dko, dkc), (1, dvo, dvc)):
        keep[at] = (own[...] + clean * other[...]).astype(bf16)
        send[at] = other[...].astype(bf16)


def attend_back(info, first, pairs, q, ko, vo, kc, vc, o, do, lse, cosine, sine):
    seq = q.shape[0]
    width = pairs * PW
    source = pl.BlockSpec((seq, PW), lambda h: (0, first + h))
    both = pl.BlockSpec((2, seq, PW), lambda h: (0, 0, h))
    lines = pl.BlockSpec((1, seq // T, 2 * T), lambda h: (first + h, 0, 0))
    table = whole((HD // 2, seq))
    return pl.pallas_call(
        attend_back_kernel,
        grid=(pairs,),
        in_specs=[SMEM] + [source] * 7 + [lines, table, table],
        out_specs=[pl.BlockSpec((seq, PW), lambda h: (0, h)), both, both],
        out_shape=[shape((seq, width), bf16)] + [shape((2, seq, width), bf16)] * 2,
        scratch_shapes=[pltpu.VMEM((PW, seq), bf16)] * 2 + [pltpu.VMEM((seq, PW), f32)] * 4,
        compiler_params=params(BIG),
        cost_estimate=pl.CostEstimate(
            flops=8 * seq * seq * width, bytes_accessed=30 * seq * width, transcendentals=seq * seq * 8
        ),
        name="attend_back",
    )(info, q, ko, vo, kc, vc, o, do, lse, cosine, sine)


C0 = 0.7978845608028654
C1 = C0 * 0.044715


def layer_kernel(
    plan, info, x, received, gain1, gain2, wk, wv, cosine, signed, q, ko, vo, wo_any, dy_any, w1_any, w2_any,
    kc_out, vc_out, o_out, lse, out, dx2, do, up_send, up_keep, down_send, down_keep, g_send, g_keep, sums,
    kc, vc, vo_t, vc_t, scores, o, o_t, x2, h2, m, dh, act, du, acc, wo, dy, w1, w2, sem_a, sem_1, sem_2,
):
    step = pl.program_id(0)
    noisy, length = info[0], info[1]
    tiles, pairs, chunks = plan
    at_attend, at_join = tiles, tiles + pairs
    at_feed, at_middle = at_join + tiles, at_join + tiles + chunks
    seq = q.shape[0]

    def fetch(c):
        place = lax.rem(c + (chunks // 2) * (1 - noisy), chunks) * FC
        place = pl.multiple_of(place, FC)
        return (
            pltpu.make_async_copy(w1_any.at[:, pl.ds(place, FC)], w1.at[c], sem_1.at[c]),
            pltpu.make_async_copy(w2_any.at[pl.ds(place, FC), :], w2.at[c], sem_2.at[c]),
        )

    copies = (
        pltpu.make_async_copy(wo_any, wo, sem_a.at[0]),
        pltpu.make_async_copy(dy_any, dy, sem_a.at[1]),
    )

    @pl.when(step == 0)
    def _():
        for copy in copies:
            copy.start()
        for c in range(chunks):
            for copy in fetch(c):
                copy.start()
        sums[...] = jnp.zeros_like(sums)
        acc[...] = jnp.zeros_like(acc)

    @pl.when(step < at_attend)
    def _():
        rows = pl.ds(pl.multiple_of(step * R, R), R)
        value = jnp.where(noisy == 1, received[...].astype(f32), x[...].astype(f32))
        h1 = (value * inv_rms(value) * gain1[...]).astype(bf16)
        k = rotated(nn(h1, wk[...]), cosine[...], signed[...], 1.0).astype(bf16)
        v = nn(h1, wv[...]).astype(bf16)
        kc_out[...] = k
        vc_out[...] = v
        for p in range(pairs):
            kc[p, rows, :] = k[:, p * PW : (p + 1) * PW]
            vc[p, rows, :] = v[:, p * PW : (p + 1) * PW]

    @pl.when(jnp.logical_and(step >= at_attend, step < at_join))
    def _():
        p = step - at_attend
        lanes = pl.ds(pl.multiple_of(p * PW, PW), PW)

        def store(at, tile_t):
            o_t[lanes, at] = tile_t.astype(bf16)
            tile = tile_t.T.astype(bf16)
            o[at, lanes] = tile
            o_out[at, :] = tile

        attend_pair(noisy, length, q, ko, vo, kc.at[p], vc.at[p], store, lse, vo_t, vc_t, scores)

    @pl.when(step == at_join)
    def _():
        for copy in copies:
            copy.wait()

    @pl.when(jnp.logical_and(step >= at_join, step < at_feed))
    def _():
        start = pl.multiple_of((step - at_join) * R, R)
        rows = pl.ds(start, R)
        branch = nn(o[rows, :], wo[...])
        value = x[...].astype(f32) + branch
        x2[rows, :] = value
        h2[rows, :] = (value * inv_rms(value) * gain2[...]).astype(bf16)
        m[rows, :] = jnp.zeros_like(value)
        dh[rows, :] = jnp.zeros_like(value)
        weight = token_weight(start, length, R)
        sums[0:1, :] += row_sum(jnp.where(weight, branch * branch, 0.0))

    @pl.when(jnp.logical_and(step >= at_feed, step < at_middle))
    def _():
        c = step - at_feed
        for copy in fetch(c):
            copy.wait()
        up, down = w1.at[c], w2.at[c]
        for t in range(0, seq, R):
            rows = pl.ds(t, R)
            u = nn(h2[rows, :], up[...])
            da = nt(dy[rows, :], down[...])
            sq = u * u
            half = 0.5 * jnp.tanh(u * (C0 + C1 * sq)) + 0.5
            low = (u * half).astype(bf16)
            slope = half + u * (2.0 * half * (1.0 - half)) * (C0 + 3.0 * C1 * sq)
            back = (da * slope).astype(bf16)
            act[rows, :] = low
            du[rows, :] = back
            m[rows, :] += nn(low, down[...])
            dh[rows, :] += nt(back, up[...])
        down_grad = tn(act[...], dy[...]).astype(bf16)
        up_grad = tn(du[...], h2[...]).astype(bf16)

        @pl.when(c < chunks // 2)
        def _():
            down_send[...] = down_grad
            up_send[...] = up_grad

        @pl.when(c >= chunks // 2)
        def _():
            down_keep[...] = down_grad
            up_keep[...] = up_grad

    @pl.when(step >= at_middle)
    def _():
        start = pl.multiple_of((step - at_middle) * R, R)
        rows = pl.ds(start, R)
        value = x2[rows, :]
        mixed = m[rows, :]
        out[...] = (value + mixed).astype(bf16)
        weight = token_weight(start, length, R)
        sums[1:2, :] += row_sum(jnp.where(weight, mixed * mixed, 0.0))
        grad, gain_terms = norm_back(value, gain2[...], dh[rows, :])
        sums[2:3, :] += row_sum(gain_terms)
        grad = grad + dy[rows, :].astype(f32)
        dx2[...] = grad
        da = grad.astype(bf16)
        do[...] = nt(da, wo[...]).astype(bf16)
        acc[...] += nn(o_t[:, rows], da)

    @pl.when(step == at_middle + tiles - 1)
    def _():
        half = acc.shape[0] // 2
        mine = pl.multiple_of(noisy * half, half)
        g_keep[...] = acc[pl.ds(mine, half), :].astype(bf16)
        g_send[...] = acc[pl.ds(half - mine, half), :].astype(bf16)


def layer(info, x, received, gain1, gain2, wqkv, tables, q, ko, vo, wo, dy, w1, w2):
    seq, width = x.shape
    hidden = w1.shape[1]
    tiles, pairs, chunks = seq // R, width // PW, hidden // FC
    at_join = tiles + pairs
    at_feed, at_middle = at_join + tiles, at_join + tiles + chunks
    clip = lambda i, count: jnp.clip(i, 0, count - 1)
    early = lambda i: (clip(i, tiles), 0)
    late = lambda i: (clip(i - at_middle, tiles), 0)
    pair = lambda i: (0, clip(i - tiles, pairs))
    rows = (R, width)
    third = lambda c: pl.BlockSpec((width, width), lambda i: (0, c), pipeline_mode=pl.Buffered(1))
    table = pl.BlockSpec((R, PW), early)
    anywhere = pl.BlockSpec(memory_space=pl.ANY)
    head = pl.BlockSpec((seq, PW), pair)
    send = pl.BlockSpec((FC, width), lambda i: (clip(i - at_feed, chunks // 2), 0))
    keep = pl.BlockSpec((FC, width), lambda i: (clip(i - at_feed - chunks // 2, chunks // 2), 0))
    half = whole((width // 2, width))
    both = lambda i: (jnp.where(i < tiles, i, clip(i - at_join, tiles)), 0)
    vmem = pltpu.VMEM
    return pl.pallas_call(
        functools.partial(layer_kernel, (tiles, pairs, chunks)),
        grid=(at_middle + tiles,),
        in_specs=[SMEM, pl.BlockSpec(rows, both), pl.BlockSpec(rows, early), whole((1, width)), whole((1, width))]
        + [third(1), third(2), table, table, head, head, head]
        + [anywhere] * 4,
        out_specs=[pl.BlockSpec(rows, early)] * 2
        + [head, pl.BlockSpec((1, seq // T, 2 * T), lambda i: (clip(i - tiles, pairs), 0, 0))]
        + [pl.BlockSpec(rows, late)] * 3
        + [send, keep, send, keep, half, half, whole((8, width))],
        out_shape=[shape((seq, width), bf16)] * 3
        + [shape((pairs, seq // T, 2 * T), f32)]
        + [shape((seq, width), bf16), shape((seq, width), f32), shape((seq, width), bf16)]
        + [shape((hidden // 2, width), bf16)] * 4
        + [shape((width // 2, width), bf16)] * 2
        + [shape((8, width), f32)],
        scratch_shapes=[vmem((pairs, seq, PW), bf16)] * 2
        + [vmem((PW, seq), bf16)] * 2
        + [vmem((2, seq + T, 2 * T), f32), vmem((seq, width), bf16), vmem((width, seq), bf16)]
        + [vmem((seq, width), f32), vmem((seq, width), bf16)]
        + [vmem((seq, width), f32)] * 2
        + [vmem((seq, FC), bf16)] * 2
        + [vmem((width, width), f32), vmem((width, width), bf16), vmem((seq, width), bf16)]
        + [vmem((chunks, width, FC), bf16), vmem((chunks, FC, width), bf16)]
        + [pltpu.SemaphoreType.DMA((n,)) for n in (2, chunks, chunks)],
        compiler_params=params(BIG),
        cost_estimate=pl.CostEstimate(
            flops=seq * width * (12 * hidden + 12 * width + 4 * seq),
            bytes_accessed=60 * seq * width,
            transcendentals=seq * hidden + seq * seq * 8,
        ),
        name="layer",
    )(info, x, received, gain1, gain2, wqkv, wqkv, *tables, q, ko, vo, wo, dy, w1, w2)


def weigh_kernel(info, dq, keep, got, cosine, signed, h1t, dkv, g_send, g_keep):
    half = h1t.shape[0] // 2
    mine = pl.multiple_of(info[0] * half, half)
    dk = keep[0].astype(f32) + got[0].astype(f32)
    dk = rotated(dk, cosine[...], signed[...], -1.0).astype(bf16)
    dv = (keep[1].astype(f32) + got[1].astype(f32)).astype(bf16)
    dkv[0] = dk
    dkv[1] = dv
    grads = jnp.concatenate([dq[...], dk, dv], axis=1)
    for out, start in ((g_send, half - mine), (g_keep, mine)):
        total = nn(h1t[pl.ds(start, half), :], grads).astype(bf16)
        for i in range(3):
            out[i] = total[:, i * PW : (i + 1) * PW]


def weigh(info, piece, got, tables, h1t):
    dq, keep = piece
    seq, width = dq.shape
    tall = h1t.shape[0]
    both = pl.BlockSpec((2, seq, PW), lambda h: (0, 0, h))
    table = whole((seq, PW))
    half = pl.BlockSpec((3, tall // 2, PW), lambda h: (0, 0, h))
    return pl.pallas_call(
        weigh_kernel,
        grid=(width // PW,),
        in_specs=[SMEM, pl.BlockSpec((seq, PW), lambda h: (0, h)), both, both, table, table, whole((tall, seq))],
        out_specs=[both, half, half],
        out_shape=[shape((2, seq, width), bf16)] + [shape((3, tall // 2, width), bf16)] * 2,
        compiler_params=params(BIG),
        cost_estimate=pl.CostEstimate(
            flops=6 * seq * width * tall, bytes_accessed=16 * seq * width, transcendentals=0
        ),
        name="weigh",
    )(info, dq, keep, got, *tables, h1t)


def finish_kernel(parts, x, dx2, wqkv, gain, *refs):
    dx, sums = refs[-2:]

    @pl.when(pl.program_id(0) == 0)
    def _():
        sums[...] = jnp.zeros_like(sums)

    dqs, dkvs = refs[:parts], refs[parts : 2 * parts]
    grads = [r[...] for r in dqs] + [r[0] for r in dkvs] + [r[1] for r in dkvs]
    dh = nt(jnp.concatenate(grads, axis=1), wqkv[...])
    grad, gain_terms = norm_back(x[...].astype(f32), gain[...], dh)
    sums[0:1, :] += row_sum(gain_terms)
    dx[...] = (dx2[...] + grad).astype(bf16)


def finish(x, dx2, dqs, dkvs, weight, gain):
    seq, width = x.shape
    rows = pl.BlockSpec((R, width), lambda i: (i, 0))
    return pl.pallas_call(
        functools.partial(finish_kernel, len(dqs)),
        grid=(seq // R,),
        in_specs=[rows, rows, whole(weight.shape), whole((1, width))]
        + [pl.BlockSpec((R, a.shape[1]), lambda i: (i, 0)) for a in dqs]
        + [pl.BlockSpec((2, R, a.shape[2]), lambda i: (0, i, 0)) for a in dkvs],
        out_specs=[rows, whole((8, width))],
        out_shape=[shape((seq, width), bf16), shape((8, width), f32)],
        compiler_params=params(BIG),
        cost_estimate=pl.CostEstimate(
            flops=6 * seq * width * width, bytes_accessed=20 * seq * width, transcendentals=0
        ),
        name="finish",
    )(x, dx2, weight, gain, *dqs, *dkvs)


def bit_orders(count):
    bits = [1 << i for i in range(count.bit_length() - 1)]
    if len(bits) == 4:
        x, y, z, far = bits
        return [(x, y, z, far), (y, x, z, far), (z, x, far, y)]
    return [tuple(bits[g:] + bits[:g]) for g in range(GROUPS)]


def exchange(value, axis, bit):
    size = lax.axis_size(axis)
    return lax.ppermute(value, axis, [(i, i ^ bit) for i in range(size)])


def distance(order, place):
    out = 0
    for i, bit in enumerate(order):
        out = out + ((place >> (len(order) - 1 - i)) & 1) * bit
    return out


def start_kernel(orders, wheres, me, *refs):
    arrays = len(wheres)
    ins, outs = refs[: 2 * arrays], refs[2 * arrays :]
    half = outs[0].shape[0]
    for g, order in enumerate(orders):
        for side in range(2):

            def one(r, carry, g=g, order=order, side=side):
                part = me[0] ^ distance(order, r + side * half)
                row = 0
                for kept, got, where in zip(ins[::2], ins[1::2], wheres, strict=True):
                    place = where(part, g)
                    size = kept.shape[1]
                    total = kept[place].astype(f32) + got[place].astype(f32)
                    outs[g * 2 + side][r, row : row + size, :] = total.astype(bf16)
                    row += size
                return carry

            lax.fori_loop(0, half, one, 0)


def start_sum(me, kept, got, wheres, orders):
    count = 1 << len(orders[0])
    half = count // 2
    rows = sum(a.shape[1] for a in kept)
    width = kept[0].shape[2]
    cols = width // 3
    block = lambda a: pl.BlockSpec((a.shape[0], a.shape[1], cols), lambda c: (0, 0, c))
    out = pl.BlockSpec((half, rows, cols), lambda c: (0, 0, c))
    args = [a for pair in zip(kept, got, strict=True) for a in pair]
    outs = pl.pallas_call(
        functools.partial(start_kernel, orders, wheres),
        grid=(width // cols,),
        in_specs=[SMEM] + [block(a) for a in args],
        out_specs=[out] * (2 * GROUPS),
        out_shape=[shape((half, rows, width), bf16)] * (2 * GROUPS),
        compiler_params=params(BIG),
        cost_estimate=pl.CostEstimate(
            flops=0, bytes_accessed=6 * GROUPS * count * rows * width, transcendentals=0
        ),
        name="start_sum",
    )(me, *args)
    return outs[0::2], outs[1::2]


def step_kernel(*refs):
    for g in range(GROUPS):
        low, high, got_low, got_high = refs[4 * g : 4 * g + 4]
        keep, send = refs[4 * GROUPS + 2 * g : 4 * GROUPS + 2 * g + 2]
        keep[...] = (low[...].astype(f32) + got_low[...].astype(f32)).astype(bf16)
        send[...] = (high[...].astype(f32) + got_high[...].astype(f32)).astype(bf16)


def step_sum(kept, got):
    count, rows, width = kept[0].shape
    half = count // 2
    steps = min(half, 2)
    block = (half // steps, rows, width)
    low = pl.BlockSpec(block, lambda r: (r, 0, 0))
    high = pl.BlockSpec(block, lambda r: (r + steps, 0, 0))
    args = []
    for a, b in zip(kept, got, strict=True):
        args += [a, a, b, b]
    outs = pl.pallas_call(
        step_kernel,
        grid=(steps,),
        in_specs=[low, high, low, high] * GROUPS,
        out_specs=[low, low] * GROUPS,
        out_shape=[shape((half, rows, width), bf16)] * (2 * GROUPS),
        cost_estimate=pl.CostEstimate(
            flops=0, bytes_accessed=6 * GROUPS * count * rows * width, transcendentals=0
        ),
        name="step_sum",
    )(*args)
    return outs[0::2], outs[1::2]


def after(value, *earlier):
    return lax.optimization_barrier((value, earlier))[0]


def sum_parts(me, kept, got, wheres):
    orders = bit_orders(lax.axis_size("batch"))
    keep, send = start_sum(me, kept, got, wheres, orders)
    for i in range(len(orders[0])):
        got = [exchange(s, "batch", order[i]) for s, order in zip(send, orders, strict=True)]
        earlier = yield send[0]
        if earlier is not None:
            keep = after(keep, earlier)
        if i < len(orders[0]) - 1:
            keep, send = step_sum(keep, got)
    yield [a[0].astype(f32) + b[0].astype(f32) for a, b in zip(keep, got, strict=True)]


def finished(steps, earlier):
    out = steps.send(earlier)
    while not isinstance(out, list):
        out = steps.send(None)
    return out


def sum_all(value):
    value = value + exchange(value, "stream", 1)
    for order in bit_orders(lax.axis_size("batch"))[0]:
        value = value + exchange(value, "batch", order)
    return value


def on_device(
    inputs, lengths, cotangent, qkv_weight, out_weight, up_weight, down_weight, attn_gain, mlp_gain
):
    seq, width = inputs.shape[2:]
    x = inputs[0, 0]
    dy = cotangent[0, 0]
    count = lax.axis_size("batch")
    stream = lax.axis_index("stream").astype(jnp.int32)
    me = lax.axis_index("batch").astype(jnp.int32).reshape(1)
    info = jnp.stack([stream, lengths[0]])
    gain1, gain2 = attn_gain.reshape(1, width), mlp_gain.reshape(1, width)
    cosine, sine = rotary_tables(seq)
    tables = (
        jnp.asarray(np.concatenate([cosine] * 4, axis=1)),
        jnp.asarray(np.concatenate([-sine, sine] * 2, axis=1)),
    )
    tables_t = (jnp.asarray(cosine.T), jnp.asarray(sine.T))

    received = lax.ppermute(x, "stream", [(0, 1)])
    q, ko, vo, h1t, sums_x = project(info, x, gain1, qkv_weight, tables)
    (
        kc, vc, o, lse, outputs, dx2, do,
        up_send, up_keep, down_send, down_keep, out_send, out_keep, sums_m,
    ) = layer(
        info, x, received, gain1, gain2, qkv_weight, tables, q, ko, vo, out_weight, dy, up_weight, down_weight
    )
    down_got, up_got, out_got = (exchange(a, "stream", 1) for a in (down_send, up_send, out_send))

    def by_rows(array):
        return array.reshape(count * GROUPS, array.shape[0] // (count * GROUPS), width)

    heads = (q, ko, vo, kc, vc, o, do, lse, *tables_t)
    pairs = width // PW // 2
    dq1, keep1, send1 = attend_back(info, 0, pairs, *heads)
    got1 = lax.ppermute(send1, "stream", [(1, 0)])
    early = sum_parts(
        me,
        [by_rows(after(a, dq1)) for a in (down_keep, up_keep, out_keep)],
        [by_rows(a) for a in (down_got, up_got, out_got)],
        [lambda part, g: part * GROUPS + g] * 3,
    )
    token = next(early)
    dq2, keep2, send2 = attend_back(info, pairs, pairs, q, ko, vo, kc, vc, o, after(do, token), lse, *tables_t)
    got2 = lax.ppermute(send2, "stream", [(1, 0)])
    dkv1, qkv_send1, qkv_keep1 = weigh(info, (dq1, after(keep1, dq2)), got1, tables, h1t)
    qkv_got1 = exchange(qkv_send1, "stream", 1)
    token = early.send(dkv1)
    dkv2, qkv_send2, qkv_keep2 = weigh(info, (dq2, after(keep2, token)), got2, tables, h1t)
    qkv_got2 = exchange(qkv_send2, "stream", 1)
    dx, sums_h = finish(x, dx2, [dq1, dq2], [dkv1, dkv2], qkv_weight, gain1)

    tall = width // (2 * count)
    split = lambda a: a.reshape(GROUPS * count, tall, a.shape[2])
    late = sum_parts(
        me,
        [split(after(a, dx)) for a in (qkv_keep1, qkv_keep2)],
        [split(a) for a in (qkv_got1, qkv_got2)],
        [lambda part, g: g * count + part] * 2,
    )
    token = next(late)
    early.send(token)
    late.send(None)
    early = finished(early, None)
    late = finished(late, None)
    small = jnp.concatenate(
        [
            sums_x[:1],
            sums_m[:3],
            sums_h[:1],
            jnp.full((1, width), lengths[0].astype(f32)),
            jnp.zeros((2, width), f32),
        ]
    )
    small = sum_all(small)

    qkv_grad = jnp.concatenate([part for e in late for part in (e[:tall], e[tall:])], axis=1)
    tall = down_keep.shape[0] // (count * GROUPS)
    down_grad = jnp.concatenate([e[:tall] for e in early])
    up_grad = jnp.concatenate([e[tall : 2 * tall] for e in early]).T
    out_grad = jnp.concatenate([e[2 * tall :] for e in early])
    squares = jnp.sum(small[:3], axis=1)
    rms = jnp.sqrt(squares / (small[5, 0] * width))
    return (
        outputs[None, None],
        dx[None, None],
        qkv_grad,
        out_grad,
        up_grad,
        down_grad,
        small[4],
        small[3],
        rms,
    )


def solution(mesh):
    rows = P("stream", "batch", None, None)
    both = ("stream", "batch")
    return jax.shard_map(
        on_device,
        mesh=mesh,
        in_specs=(rows, P("batch"), rows, P(), P(), P(), P(), P(), P()),
        out_specs=(rows, rows, P(both, None), P(both, None), P(None, both), P(both, None), P(), P(), P()),
        check_vma=False,
    )
```

profile of v0, /device:TPU:0, one launch (start us, length us, event | category | flops | bytes accessed | tf_op | source)
XLA Modules:
  0.0 288.8 jit_solution(14016255031754092019)
XLA Ops:
  0.6 2.5 collective-permute-start
  6.9 9.3 %project.1 = (bf16[1024,768]{1,0:T(8,128)(2,1)}, bf16[1024,768]{1,0:T(8,128)(2,1)}, bf16[1024,768]{1,0:T(8,128)(2,1)}, bf16[768,1024]{1,0:T(8,128)(2,1)}, f32[8,768]{1,0:T(8,128)}) custom-call(s32[2]{0:T(128)} %pad_add_fusion.info, bf16[1024,768]{1,0:T(8,128)(2,1)} %bitcast.73, f32[1,768]{1,0:T(1,128)} %reshape.93.gain.gain1, bf16[768,2304]{1,0:T(8,128)(2,1)} %wqkv.1, ...), custom_call_target="tpu_custom_call" | custom-call | flops 3623878656 | bytes 9437184 | tf_op jit(solution)/shard_map/project/pallas_call | solution.py:112
  17.3 80.1 %layer.1 = (bf16[1024,768]{1,0:T(8,128)(2,1)}, bf16[1024,768]{1,0:T(8,128)(2,1)}, bf16[1024,768]{1,0:T(8,128)(2,1)}, f32[6,8,256]{2,1,0:T(8,128)}, bf16[1024,768...) custom-call(s32[2]{0:T(128)} %pad_add_fusion.info, ...), custom_call_target="tpu_custom_call" | custom-call | flops 39460012032 | bytes 47185920 | tf_op jit(solution)/shard_map/layer/pallas_call | solution.py:428
  98.1 19.9 %attend_back.2 = (bf16[1024,384]{1,0:T(8,128)(2,1)}, bf16[2,1024,384]{2,1,0:T(8,128)(2,1)}, bf16[2,1024,384]{2,1,0:T(8,128)(2,1)}) custom-call(s32[2]{0:T(128)} %pad_add_fusion.info, bf16[1024,768]{1,0:T(8,128)(2,1)} %get-tuple-element.104.q, bf16[1024,768]{1,0:T(8,128)(2,1)} %get-tuple-element.105.ko, bf16[1024,768]{1,0:T(8,128)(2,1)} %get-tuple-element.106.vo, ...), custom_call_target="tpu_custom_call" | custom-call | flops 3221225472 | bytes 11796480 | tf_op jit(solution)/shard_map/attend_back/pallas_call | solution.py:253
  120.9 8.3 %start_sum.2 = (bf16[8,72,768]{2,1,0:T(8,128)(2,1)}, bf16[8,72,768]{2,1,0:T(8,128)(2,1)}, bf16[8,72,768]{2,1,0:T(8,128)(2,1)}, bf16[8,72,768]{2,1,0:T(8,128)(2,1...) custom-call(s32[1]{0:T(128)} %bitcast.4.me, bf16[48,32,768]{2,1,0:T(8,128)(2,1)} %bitcast.63, ...), custom_call_target="tpu_custom_call" | custom-call | bytes 15925248 | tf_op jit(solution)/shard_map/start_sum/pallas_call | solution.py:583
  129.2 19.9 %attend_back.3 = (bf16[1024,384]{1,0:T(8,128)(2,1)}, bf16[2,1024,384]{2,1,0:T(8,128)(2,1)}, bf16[2,1024,384]{2,1,0:T(8,128)(2,1)}) custom-call(s32[2]{0:T(128)} %pad_add_fusion.info, bf16[1024,768]{1,0:T(8,128)(2,1)} %get-tuple-element.104.q, bf16[1024,768]{1,0:T(8,128)(2,1)} %get-tuple-element.105.ko, bf16[1024,768]{1,0:T(8,128)(2,1)} %get-tuple-element.106.vo, ...), custom_call_target="tpu_custom_call" | custom-call | flops 3221225472 | bytes 11796480 | tf_op jit(solution)/shard_map/attend_back/pallas_call | solution.py:253
  150.4 2.4 collective-permute-start.6
  155.9 7.1 %weigh.2 = (bf16[2,1024,384]{2,1,0:T(8,128)(2,1)}, bf16[3,384,384]{2,1,0:T(8,128)(2,1)}, bf16[3,384,384]{2,1,0:T(8,128)(2,1)}) custom-call(s32[2]{0:T(128)} %pad_add_fusion.info, bf16[1024,384]{1,0:T(8,128)(2,1)} %get-tuple-element.114.dq.refs_0_, bf16[2,1024,384]{2,1,0:T(8,128)(2,1)} %get-tuple-element.128.keep, ...), custom_call_target="tpu_custom_call" | custom-call | flops 1811939328 | bytes 6291456 | tf_op jit(solution)/shard_map/weigh/pallas_call | solution.py:485
  163.0 2.5 collective-permute-start.9
  165.5 5.4 %collective-permute-done.6.refs_6_.refs_7_ = bf16[8,72,768]{2,1,0:T(8,128)(2,1)S(1)} collective-permute-done((bf16[8,72,768]{2,1,0:T(8,128)(2,1)}, bf16[8,72,768]{2,1,0:T(8,128)(2,1)S(1)}, u32[]{:S(2)}, u32[]{:S(2)}) %collective-permute-start.6) | collective-permute-done | bytes 884768 | tf_op jit(solution)/shard_map/ppermute | solution.py:543
  170.8 2.6 collective-permute-done.7.refs_10_.refs_11_
  176.2 4.0 %step_sum.6 = (bf16[4,72,768]{2,1,0:T(8,128)(2,1)}, bf16[4,72,768]{2,1,0:T(8,128)(2,1)}, bf16[4,72,768]{2,1,0:T(8,128)(2,1)}, bf16[4,72,768]{2,1,0:T(8,128)(2,1)...) custom-call(bf16[8,72,768]{2,1,0:T(8,128)(2,1)} %get-tuple-element.136.refs_0_.refs_1_, ...), custom_call_target="tpu_custom_call" | custom-call | bytes 7962624 | tf_op jit(solution)/shard_map/step_sum/pallas_call | solution.py:616
  180.2 6.9 %weigh.3 = (bf16[2,1024,384]{2,1,0:T(8,128)(2,1)}, bf16[3,384,384]{2,1,0:T(8,128)(2,1)}, bf16[3,384,384]{2,1,0:T(8,128)(2,1)}) custom-call(s32[2]{0:T(128)} %pad_add_fusion.info, bf16[1024,384]{1,0:T(8,128)(2,1)} %get-tuple-element.126.dq.refs_1_, bf16[2,1024,384]{2,1,0:T(8,128)(2,1)} %get-tuple-element.142.keep, ...), custom_call_target="tpu_custom_call" | custom-call | flops 1811939328 | bytes 6291456 | tf_op jit(solution)/shard_map/weigh/pallas_call | solution.py:485
  192.0 9.3 %finish.1 = (bf16[1024,768]{1,0:T(8,128)(2,1)}, f32[8,768]{1,0:T(8,128)}) custom-call(bf16[1024,768]{1,0:T(8,128)(2,1)} %bitcast.75, f32[1024,768]{1,0:T(8,128)} %get-tuple-element.108.dx2, bf16[768,2304]{1,0:T(8,128)(2,1)} %wqkv.1, f32[1,768]{1,0:T(1,128)} %reshape.93.gain.gain1, bf16[1024,384]{1,0:T(8,128)(2,1)} %get-tuple-element.114.dq.refs_0_, ...), custom_call_target="tpu_custom_call" | custom-call | flops 3623878656 | bytes 15728640 | tf_op jit(solution)/shard_map/finish/pallas_call | solution.py:517
  203.3 4.7 %start_sum.3 = (bf16[8,48,384]{2,1,0:T(8,128)(2,1)}, bf16[8,48,384]{2,1,0:T(8,128)(2,1)}, bf16[8,48,384]{2,1,0:T(8,128)(2,1)}, bf16[8,48,384]{2,1,0:T(8,128)(2,1...) custom-call(s32[1]{0:T(128)} %bitcast.4.me, bf16[48,24,384]{2,1,0:T(8,128)(2,1)} %bitcast.65, ...), custom_call_target="tpu_custom_call" | custom-call | bytes 5308416 | tf_op jit(solution)/shard_map/start_sum/pallas_call | solution.py:583
  208.1 2.5 collective-permute-done.25.refs_10_.refs_11_
  212.1 2.7 step_sum.10
  217.3 2.3 collective-permute-done.33
  220.2 3.3 %collective-permute-done.34 = f32[8,768]{1,0:T(8,128)S(1)} collective-permute-done((f32[8,768]{1,0:T(8,128)S(1)}, f32[8,768]{1,0:T(8,128)S(1)}, u32[]{:S(2)}, u32[]{:S(2)}) %collective-permute-start.34) | collective-permute-done | bytes 24608 | tf_op jit(solution)/shard_map/ppermute | solution.py:543
  224.6 2.8 collective-permute-done.35
  227.5 2.5 collective-permute-start.36
  229.9 2.3 collective-permute-done.36
  236.1 2.8 collective-permute-start.28
  240.9 5.0 %collective-permute-done.27.refs_6_.refs_7_ = bf16[2,72,768]{2,1,0:T(8,128)(2,1)S(1)} collective-permute-done((bf16[2,72,768]{2,1,0:T(8,128)(2,1)}, bf16[2,72,768]{2,1,0:T(8,128)(2,1)S(1)}, u32[]{:S(2)}, u32[]{:S(2)}) %collective-permute-start.27) | collective-permute-done | bytes 221216 | tf_op jit(solution)/shard_map/ppermute | solution.py:543
  246.6 2.2 step_sum.11
  248.9 2.9 collective-permute-start.29
  253.8 2.4 step_sum.7
  265.3 1.8 step_sum.8
  267.2 3.0 %collective-permute-start.17 = (bf16[2,48,384]{2,1,0:T(8,128)(2,1)}, bf16[2,48,384]{2,1,0:T(8,128)(2,1)S(1)}, u32[]{:S(2)}, u32[]{:S(2)}) collective-permute-start(bf16[2,48,384]{2,1,0:T(8,128)(2,1)} %get-tuple-element.165), channel_id=1, source_target_pairs={{0,4},{1,5},{2,6},{3,7},{4,0},{5,1},{6,2},{7,3},{8,12},{9,13},{10,... | collective-permute-start | bytes 221192 | tf_op jit(solution)/shard_map/ppermute | solution.py:543
  270.3 2.6 collective-permute-start.19
  278.1 2.7 collective-permute-start.20
  284.0 2.5 collective-permute-done.21
  (157 shorter events, 55.3 us)
Async XLA Ops:
  0.6 15.5 %collective-permute-start = (bf16[1024,768]{1,0:T(8,128)(2,1)}, bf16[1024,768]{1,0:T(8,128)(2,1)S(1)}, u32[]{:S(2)}, u32[]{:S(2)}) collective-permute-start(bf16[1024,768]{1,0:T(8,128)(2,1)} %bitcast.72), channel_id=1, source_target_pairs={{0,16},{1,17},{2,18},{3,19},{4,20},{5,21},{6,22},{7,23},{8,24},{9,... | collective-permute-start | bytes 4718600 | tf_op jit(solution)/shard_map/ppermute | solution.py:679
  97.4 21.9 %collective-permute-start.1 = (bf16[1536,768]{1,0:T(8,128)(2,1)}, bf16[1536,768]{1,0:T(8,128)(2,1)S(1)}, u32[]{:S(2)}, u32[]{:S(2)}) collective-permute-start(bf16[1536,768]{1,0:T(8,128)(2,1)} %get-tuple-element.117), channel_id=1, source_target_pairs={{0,16},{16,0},{1,17},{17,1},{2,18},{18,2},{3,19},{19,3},{4,20},{20... | collective-permute-start | bytes 7077896 | tf_op jit(solution)/shard_map/ppermute | solution.py:543
  97.5 21.8 %collective-permute-start.2 = (bf16[1536,768]{1,0:T(8,128)(2,1)}, bf16[1536,768]{1,0:T(8,128)(2,1)}, u32[]{:S(2)}, u32[]{:S(2)}) collective-permute-start(bf16[1536,768]{1,0:T(8,128)(2,1)} %get-tuple-element.120), channel_id=1, source_target_pairs={{0,16},{16,0},{1,17},{17,1},{2,18},{18,2},{3,19},{19,3},{4,20},{20... | collective-permute-start | bytes 7077896 | tf_op jit(solution)/shard_map/ppermute | solution.py:543
  98.0 21.3 %collective-permute-start.3 = (bf16[384,768]{1,0:T(8,128)(2,1)}, bf16[384,768]{1,0:T(8,128)(2,1)S(1)}, u32[]{:S(2)}, u32[]{:S(2)}) collective-permute-start(bf16[384,768]{1,0:T(8,128)(2,1)} %get-tuple-element.123), channel_id=1, source_target_pairs={{0,16},{16,0},{1,17},{17,1},{2,18},{18,2},{3,19},{19,3},{4,20},{20... | collective-permute-start | bytes 1769480 | tf_op jit(solution)/shard_map/ppermute | solution.py:543
  118.0 38.0 %collective-permute-start.4 = (bf16[2,1024,384]{2,1,0:T(8,128)(2,1)}, bf16[2,1024,384]{2,1,0:T(8,128)(2,1)}, u32[]{:S(2)}, u32[]{:S(2)}) collective-permute-start(bf16[2,1024,384]{2,1,0:T(8,128)(2,1)} %get-tuple-element.129), channel_id=1, source_target_pairs={{16,0},{17,1},{18,2},{19,3},{20,4},{21,5},{22,6},{23,7},{24,8},{25... | collective-permute-start | bytes 4718600 | tf_op jit(solution)/shard_map/ppermute | solution.py:695
  149.1 31.0 %collective-permute-start.8 = (bf16[2,1024,384]{2,1,0:T(8,128)(2,1)}, bf16[2,1024,384]{2,1,0:T(8,128)(2,1)}, u32[]{:S(2)}, u32[]{:S(2)}) collective-permute-start(bf16[2,1024,384]{2,1,0:T(8,128)(2,1)} %get-tuple-element.143), channel_id=1, source_target_pairs={{16,0},{17,1},{18,2},{19,3},{20,4},{21,5},{22,6},{23,7},{24,8},{25... | collective-permute-start | bytes 4718600 | tf_op jit(solution)/shard_map/ppermute | solution.py:704
  150.4 20.4 %collective-permute-start.6 = (bf16[8,72,768]{2,1,0:T(8,128)(2,1)}, bf16[8,72,768]{2,1,0:T(8,128)(2,1)S(1)}, u32[]{:S(2)}, u32[]{:S(2)}) collective-permute-start(bf16[8,72,768]{2,1,0:T(8,128)(2,1)} %get-tuple-element.138), channel_id=1, source_target_pairs={{0,2},{1,3},{2,0},{3,1},{4,6},{5,7},{6,4},{7,5},{8,10},{9,11},{10,... | collective-permute-start | bytes 2654216 | tf_op jit(solution)/shard_map/ppermute | solution.py:543
  152.8 20.6 %collective-permute-start.7 = (bf16[8,72,768]{2,1,0:T(8,128)(2,1)}, bf16[8,72,768]{2,1,0:T(8,128)(2,1)S(1)}, u32[]{:S(2)}, u32[]{:S(2)}) collective-permute-start(bf16[8,72,768]{2,1,0:T(8,128)(2,1)} %get-tuple-element.140), channel_id=1, source_target_pairs={{0,4},{1,5},{2,6},{3,7},{4,0},{5,1},{6,2},{7,3},{8,12},{9,13},{10,... | collective-permute-start | bytes 2654216 | tf_op jit(solution)/shard_map/ppermute | solution.py:543
  154.4 20.9 %collective-permute-start.5 = (bf16[8,72,768]{2,1,0:T(8,128)(2,1)}, bf16[8,72,768]{2,1,0:T(8,128)(2,1)S(1)}, u32[]{:S(2)}, u32[]{:S(2)}) collective-permute-start(bf16[8,72,768]{2,1,0:T(8,128)(2,1)} %get-tuple-element.124), channel_id=1, source_target_pairs={{0,1},{1,0},{2,3},{3,2},{4,5},{5,4},{6,7},{7,6},{8,9},{9,8},{10,11... | collective-permute-start | bytes 2654216 | tf_op jit(solution)/shard_map/ppermute | solution.py:543
  163.0 39.1 %collective-permute-start.9 = (bf16[3,384,384]{2,1,0:T(8,128)(2,1)}, bf16[3,384,384]{2,1,0:T(8,128)(2,1)S(1)}, u32[]{:S(2)}, u32[]{:S(2)}) collective-permute-start(bf16[3,384,384]{2,1,0:T(8,128)(2,1)} %get-tuple-element.148), channel_id=1, source_target_pairs={{0,16},{16,0},{1,17},{17,1},{2,18},{18,2},{3,19},{19,3},{4,20},{20... | collective-permute-start | bytes 2654216 | tf_op jit(solution)/shard_map/ppermute | solution.py:543
  187.0 15.2 %collective-permute-start.10 = (bf16[3,384,384]{2,1,0:T(8,128)(2,1)}, bf16[3,384,384]{2,1,0:T(8,128)(2,1)S(1)}, u32[]{:S(2)}, u32[]{:S(2)}) collective-permute-start(bf16[3,384,384]{2,1,0:T(8,128)(2,1)} %get-tuple-element.151), channel_id=1, source_target_pairs={{0,16},{16,0},{1,17},{17,1},{2,18},{18,2},{3,19},{19,3},{4,20},{20... | collective-permute-start | bytes 2654216 | tf_op jit(solution)/shard_map/ppermute | solution.py:543
  188.7 19.4 %collective-permute-start.24 = (bf16[4,72,768]{2,1,0:T(8,128)(2,1)}, bf16[4,72,768]{2,1,0:T(8,128)(2,1)S(1)}, u32[]{:S(2)}, u32[]{:S(2)}) collective-permute-start(bf16[4,72,768]{2,1,0:T(8,128)(2,1)} %get-tuple-element.181), channel_id=1, source_target_pairs={{0,1},{1,0},{2,3},{3,2},{4,5},{5,4},{6,7},{7,6},{8,9},{9,8},{10,11... | collective-permute-start | bytes 1327112 | tf_op jit(solution)/shard_map/ppermute | solution.py:543
  190.2 20.3 %collective-permute-start.25 = (bf16[4,72,768]{2,1,0:T(8,128)(2,1)}, bf16[4,72,768]{2,1,0:T(8,128)(2,1)S(1)}, u32[]{:S(2)}, u32[]{:S(2)}) collective-permute-start(bf16[4,72,768]{2,1,0:T(8,128)(2,1)} %get-tuple-element.183), channel_id=1, source_target_pairs={{0,1},{1,0},{2,3},{3,2},{4,5},{5,4},{6,7},{7,6},{8,9},{9,8},{10,11... | collective-permute-start | bytes 1327112 | tf_op jit(solution)/shard_map/ppermute | solution.py:543
  190.7 19.8 %collective-permute-start.23 = (bf16[4,72,768]{2,1,0:T(8,128)(2,1)}, bf16[4,72,768]{2,1,0:T(8,128)(2,1)S(1)}, u32[]{:S(2)}, u32[]{:S(2)}) collective-permute-start(bf16[4,72,768]{2,1,0:T(8,128)(2,1)} %get-tuple-element.141), channel_id=1, source_target_pairs={{0,2},{1,3},{2,0},{3,1},{4,6},{5,7},{6,4},{7,5},{8,10},{9,11},{10,... | collective-permute-start | bytes 1327112 | tf_op jit(solution)/shard_map/ppermute | solution.py:543
  202.1 13.6 %collective-permute-start.32 = (f32[8,768]{1,0:T(8,128)S(1)}, f32[8,768]{1,0:T(8,128)S(1)}, u32[]{:S(2)}, u32[]{:S(2)}) collective-permute-start(f32[8,768]{1,0:T(8,128)S(1)} %concatenate.19), channel_id=1, source_target_pairs={{0,16},{16,0},{1,17},{17,1},{2,18},{18,2},{3,19},{19,3},{4,20},{20... | collective-permute-start | bytes 73736 | tf_op jit(solution)/shard_map/ppermute | solution.py:543
  214.8 24.6 %collective-permute-start.26 = (bf16[2,72,768]{2,1,0:T(8,128)(2,1)}, bf16[2,72,768]{2,1,0:T(8,128)(2,1)S(1)}, u32[]{:S(2)}, u32[]{:S(2)}) collective-permute-start(bf16[2,72,768]{2,1,0:T(8,128)(2,1)} %get-tuple-element.185), channel_id=1, source_target_pairs={{0,4},{1,5},{2,6},{3,7},{4,0},{5,1},{6,2},{7,3},{8,12},{9,13},{10,... | collective-permute-start | bytes 663560 | tf_op jit(solution)/shard_map/ppermute | solution.py:543
  233.5 19.4 %collective-permute-start.11 = (bf16[8,48,384]{2,1,0:T(8,128)(2,1)S(1)}, bf16[8,48,384]{2,1,0:T(8,128)(2,1)S(1)}, u32[]{:S(2)}, u32[]{:S(2)}) collective-permute-start(bf16[8,48,384]{2,1,0:T(8,128)(2,1)S(1)} %copy-done.28), channel_id=1, source_target_pairs={{0,1},{1,0},{2,3},{3,2},{4,5},{5,4},{6,7},{7,6},{8,9},{9,8},{10,11... | collective-permute-start | bytes 884744 | tf_op jit(solution)/shard_map/ppermute | solution.py:543
  235.2 10.7 %collective-permute-start.27 = (bf16[2,72,768]{2,1,0:T(8,128)(2,1)}, bf16[2,72,768]{2,1,0:T(8,128)(2,1)S(1)}, u32[]{:S(2)}, u32[]{:S(2)}) collective-permute-start(bf16[2,72,768]{2,1,0:T(8,128)(2,1)} %get-tuple-element.187), channel_id=1, source_target_pairs={{0,4},{1,5},{2,6},{3,7},{4,0},{5,1},{6,2},{7,3},{8,12},{9,13},{10,... | collective-permute-start | bytes 663560 | tf_op jit(solution)/shard_map/ppermute | solution.py:543
  236.1 9.8 %collective-permute-start.28 = (bf16[2,72,768]{2,1,0:T(8,128)(2,1)}, bf16[2,72,768]{2,1,0:T(8,128)(2,1)S(1)}, u32[]{:S(2)}, u32[]{:S(2)}) collective-permute-start(bf16[2,72,768]{2,1,0:T(8,128)(2,1)} %get-tuple-element.189), channel_id=1, source_target_pairs={{0,8},{1,9},{2,10},{3,11},{4,12},{5,13},{6,14},{7,15},{8,0},{9,1},... | collective-permute-start | bytes 663560 | tf_op jit(solution)/shard_map/ppermute | solution.py:543
  238.9 13.5 %collective-permute-start.12 = (bf16[8,48,384]{2,1,0:T(8,128)(2,1)S(1)}, bf16[8,48,384]{2,1,0:T(8,128)(2,1)S(1)}, u32[]{:S(2)}, u32[]{:S(2)}) collective-permute-start(bf16[8,48,384]{2,1,0:T(8,128)(2,1)S(1)} %copy-done.30), channel_id=1, source_target_pairs={{0,2},{1,3},{2,0},{3,1},{4,6},{5,7},{6,4},{7,5},{8,10},{9,11},{10,... | collective-permute-start | bytes 884744 | tf_op jit(solution)/shard_map/ppermute | solution.py:543
  239.4 13.5 %collective-permute-start.13 = (bf16[8,48,384]{2,1,0:T(8,128)(2,1)S(1)}, bf16[8,48,384]{2,1,0:T(8,128)(2,1)S(1)}, u32[]{:S(2)}, u32[]{:S(2)}) collective-permute-start(bf16[8,48,384]{2,1,0:T(8,128)(2,1)S(1)} %copy-done.29), channel_id=1, source_target_pairs={{0,4},{1,5},{2,6},{3,7},{4,0},{5,1},{6,2},{7,3},{8,12},{9,13},{10,... | collective-permute-start | bytes 884744 | tf_op jit(solution)/shard_map/ppermute | solution.py:543
  248.9 9.7 %collective-permute-start.29 = (bf16[1,72,768]{2,1,0:T(8,128)(2,1)}, bf16[1,72,768]{2,1,0:T(8,128)(2,1)S(1)}, u32[]{:S(2)}, u32[]{:S(2)}) collective-permute-start(bf16[1,72,768]{2,1,0:T(8,128)(2,1)} %get-tuple-element.191), channel_id=1, source_target_pairs={{0,8},{1,9},{2,10},{3,11},{4,12},{5,13},{6,14},{7,15},{8,0},{9,1},... | collective-permute-start | bytes 331784 | tf_op jit(solution)/shard_map/ppermute | solution.py:543
  252.3 7.5 %collective-permute-start.30 = (bf16[1,72,768]{2,1,0:T(8,128)(2,1)}, bf16[1,72,768]{2,1,0:T(8,128)(2,1)S(1)}, u32[]{:S(2)}, u32[]{:S(2)}) collective-permute-start(bf16[1,72,768]{2,1,0:T(8,128)(2,1)} %get-tuple-element.193), channel_id=1, source_target_pairs={{0,8},{1,9},{2,10},{3,11},{4,12},{5,13},{6,14},{7,15},{8,0},{9,1},... | collective-permute-start | bytes 331784 | tf_op jit(solution)/shard_map/ppermute | solution.py:543
  252.4 7.5 %collective-permute-start.31 = (bf16[1,72,768]{2,1,0:T(8,128)(2,1)}, bf16[1,72,768]{2,1,0:T(8,128)(2,1)S(1)}, u32[]{:S(2)}, u32[]{:S(2)}) collective-permute-start(bf16[1,72,768]{2,1,0:T(8,128)(2,1)} %get-tuple-element.195), channel_id=1, source_target_pairs={{0,2},{1,3},{2,0},{3,1},{4,6},{5,7},{6,4},{7,5},{8,10},{9,11},{10,... | collective-permute-start | bytes 331784 | tf_op jit(solution)/shard_map/ppermute | solution.py:543
  256.2 5.4 %collective-permute-start.14 = (bf16[4,48,384]{2,1,0:T(8,128)(2,1)}, bf16[4,48,384]{2,1,0:T(8,128)(2,1)S(1)}, u32[]{:S(2)}, u32[]{:S(2)}) collective-permute-start(bf16[4,48,384]{2,1,0:T(8,128)(2,1)} %get-tuple-element.159), channel_id=1, source_target_pairs={{0,2},{1,3},{2,0},{3,1},{4,6},{5,7},{6,4},{7,5},{8,10},{9,11},{10,... | collective-permute-start | bytes 442376 | tf_op jit(solution)/shard_map/ppermute | solution.py:543
  257.7 5.4 %collective-permute-start.15 = (bf16[4,48,384]{2,1,0:T(8,128)(2,1)}, bf16[4,48,384]{2,1,0:T(8,128)(2,1)S(1)}, u32[]{:S(2)}, u32[]{:S(2)}) collective-permute-start(bf16[4,48,384]{2,1,0:T(8,128)(2,1)} %get-tuple-element.161), channel_id=1, source_target_pairs={{0,1},{1,0},{2,3},{3,2},{4,5},{5,4},{6,7},{7,6},{8,9},{9,8},{10,11... | collective-permute-start | bytes 442376 | tf_op jit(solution)/shard_map/ppermute | solution.py:543
  258.6 6.1 %collective-permute-start.16 = (bf16[4,48,384]{2,1,0:T(8,128)(2,1)}, bf16[4,48,384]{2,1,0:T(8,128)(2,1)S(1)}, u32[]{:S(2)}, u32[]{:S(2)}) collective-permute-start(bf16[4,48,384]{2,1,0:T(8,128)(2,1)} %get-tuple-element.163), channel_id=1, source_target_pairs={{0,1},{1,0},{2,3},{3,2},{4,5},{5,4},{6,7},{7,6},{8,9},{9,8},{10,11... | collective-permute-start | bytes 442376 | tf_op jit(solution)/shard_map/ppermute | solution.py:543
  267.2 6.6 %collective-permute-start.17 = (bf16[2,48,384]{2,1,0:T(8,128)(2,1)}, bf16[2,48,384]{2,1,0:T(8,128)(2,1)S(1)}, u32[]{:S(2)}, u32[]{:S(2)}) collective-permute-start(bf16[2,48,384]{2,1,0:T(8,128)(2,1)} %get-tuple-element.165), channel_id=1, source_target_pairs={{0,4},{1,5},{2,6},{3,7},{4,0},{5,1},{6,2},{7,3},{8,12},{9,13},{10,... | collective-permute-start | bytes 221192 | tf_op jit(solution)/shard_map/ppermute | solution.py:543
  270.3 5.5 %collective-permute-start.19 = (bf16[2,48,384]{2,1,0:T(8,128)(2,1)}, bf16[2,48,384]{2,1,0:T(8,128)(2,1)S(1)}, u32[]{:S(2)}, u32[]{:S(2)}) collective-permute-start(bf16[2,48,384]{2,1,0:T(8,128)(2,1)} %get-tuple-element.169), channel_id=1, source_target_pairs={{0,8},{1,9},{2,10},{3,11},{4,12},{5,13},{6,14},{7,15},{8,0},{9,1},... | collective-permute-start | bytes 221192 | tf_op jit(solution)/shard_map/ppermute | solution.py:543
  278.1 5.1 %collective-permute-start.20 = (bf16[1,48,384]{2,1,0:T(8,128)(2,1)}, bf16[1,48,384]{2,1,0:T(8,128)(2,1)S(1)}, u32[]{:S(2)}, u32[]{:S(2)}) collective-permute-start(bf16[1,48,384]{2,1,0:T(8,128)(2,1)} %get-tuple-element.171), channel_id=1, source_target_pairs={{0,8},{1,9},{2,10},{3,11},{4,12},{5,13},{6,14},{7,15},{8,0},{9,1},... | collective-permute-start | bytes 110600 | tf_op jit(solution)/shard_map/ppermute | solution.py:543
  281.4 5.1 %collective-permute-start.21 = (bf16[1,48,384]{2,1,0:T(8,128)(2,1)}, bf16[1,48,384]{2,1,0:T(8,128)(2,1)S(1)}, u32[]{:S(2)}, u32[]{:S(2)}) collective-permute-start(bf16[1,48,384]{2,1,0:T(8,128)(2,1)} %get-tuple-element.173), channel_id=1, source_target_pairs={{0,8},{1,9},{2,10},{3,11},{4,12},{5,13},{6,14},{7,15},{8,0},{9,1},... | collective-permute-start | bytes 110600 | tf_op jit(solution)/shard_map/ppermute | solution.py:543
  281.7 5.6 %collective-permute-start.22 = (bf16[1,48,384]{2,1,0:T(8,128)(2,1)}, bf16[1,48,384]{2,1,0:T(8,128)(2,1)S(1)}, u32[]{:S(2)}, u32[]{:S(2)}) collective-permute-start(bf16[1,48,384]{2,1,0:T(8,128)(2,1)} %get-tuple-element.175), channel_id=1, source_target_pairs={{0,2},{1,3},{2,0},{3,1},{4,6},{5,7},{6,4},{7,5},{8,10},{9,11},{10,... | collective-permute-start | bytes 110600 | tf_op jit(solution)/shard_map/ppermute | solution.py:543
  (36 other events, 173.0 us)
where the time goes:
time: 290 us; the launch traced here: 289 us
  Pallas kernels  180 us (62%)
  starting transfers between devices  47.7 us (16%)
  waiting for transfers between devices  38.1 us (13%)
  local copies, waits for them, and re-layouts  15.1 us (5%)
  other arithmetic  5.15 us (2%)
    pallas_call x1, Pallas kernels, layer(): pl.pallas_call(functools.partial(layer_kernel, (tiles, pairs, chunks)), g...  80.1 us
    ppermute x34, starting transfers between devices, exchange(): return lax.ppermute(value, axis, [(i, i ^ bit) for i in range(size)])  42.7 us
    pallas_call x2, Pallas kernels, attend_back(): pl.pallas_call(attend_back_kernel, grid=(pairs,), in_specs=[SMEM] + [sour...  39.8 us
    ppermute x34, waiting for transfers between devices, exchange(): return lax.ppermute(value, axis, [(i, i ^ bit) for i in range(size)])  38.1 us
    pallas_call x6, Pallas kernels, step_sum(): pl.pallas_call(step_kernel, grid=(steps,), in_specs=[low, high, low, high...  14.8 us
    pallas_call x2, Pallas kernels, weigh(): pl.pallas_call(weigh_kernel, grid=(width // PW,), in_specs=[SMEM, pl.Bloc...  13.9 us
    pallas_call x2, Pallas kernels, start_sum(): pl.pallas_call(functools.partial(start_kernel, orders, wheres), grid=(wid...  13 us
    unnamed x67, local copies, waits for them, and re-layouts  9.86 us
  transfers between devices with their start and end apart: 37, of which 16 were waited for; matrix products, arithmetic and copies ran while one was open for 3% of the time, Pallas kernels for 33%

commit v1 on v0

--- a/solution.py
+++ b/solution.py
@@ -23,6 +23,9 @@
 BIG = 60
 GROUPS = 3
 
+COST = pl.CostEstimate(flops=1 << 20, bytes_accessed=1 << 16, transcendentals=0)
+LONG = pl.CostEstimate(flops=1 << 35, bytes_accessed=1 << 26, transcendentals=0)
+
 SMEM = pl.BlockSpec(memory_space=pltpu.SMEM)
 
 
@@ -32,6 +35,10 @@
 
 def shape(dims, dtype):
     return jax.ShapeDtypeStruct(dims, dtype)
+
+
+def pinned(*arrays):
+    return [pltpu.with_memory_space_constraint(a, pltpu.HBM) for a in arrays]
 
 
 def nn(a, b):
@@ -116,11 +123,9 @@
         out_specs=[rows, rows, rows, pl.BlockSpec((width, R), lambda i: (0, i)), whole((8, width))],
         out_shape=[shape((seq, width), bf16)] * 3 + [shape((width, seq), bf16), shape((8, width), f32)],
         compiler_params=params(BIG),
-        cost_estimate=pl.CostEstimate(
-            flops=2 * seq * width * 3 * width, bytes_accessed=12 * seq * width, transcendentals=0
-        ),
+        cost_estimate=LONG,
         name="project",
-    )(info, x, gain, weight, weight, weight, *tables)
+    )(info, *pinned(x), gain, *pinned(weight, weight, weight, *tables))
 
 
 def stacked(tile, low):
@@ -257,12 +262,10 @@
         out_specs=[pl.BlockSpec((seq, PW), lambda h: (0, h)), both, both],
         out_shape=[shape((seq, width), bf16)] + [shape((2, seq, width), bf16)] * 2,
         scratch_shapes=[pltpu.VMEM((PW, seq), bf16)] * 2 + [pltpu.VMEM((seq, PW), f32)] * 4,
-        compiler_params=params(BIG),
-        cost_estimate=pl.CostEstimate(
-            flops=8 * seq * seq * width, bytes_accessed=30 * seq * width, transcendentals=seq * seq * 8
-        ),
+        compiler_params=params(24),
+        cost_estimate=LONG,
         name="attend_back",
-    )(info, q, ko, vo, kc, vc, o, do, lse, cosine, sine)
+    )(info, *pinned(q, ko, vo, kc, vc, o, do), lse, cosine, sine)
 
 
 C0 = 0.7978845608028654
@@ -451,13 +454,9 @@
         + [vmem((chunks, width, FC), bf16), vmem((chunks, FC, width), bf16)]
         + [pltpu.SemaphoreType.DMA((n,)) for n in (2, chunks, chunks)],
         compiler_params=params(BIG),
-        cost_estimate=pl.CostEstimate(
-            flops=seq * width * (12 * hidden + 12 * width + 4 * seq),
-            bytes_accessed=60 * seq * width,
-            transcendentals=seq * hidden + seq * seq * 8,
-        ),
+        cost_estimate=LONG,
         name="layer",
-    )(info, x, received, gain1, gain2, wqkv, wqkv, *tables, q, ko, vo, wo, dy, w1, w2)
+    )(info, *pinned(x, received), gain1, gain2, *pinned(wqkv, wqkv, *tables, q, ko, vo, wo, dy, w1, w2))
 
 
 def weigh_kernel(info, dq, keep, got, cosine, signed, h1t, dkv, g_send, g_keep):
@@ -488,12 +487,10 @@
         in_specs=[SMEM, pl.BlockSpec((seq, PW), lambda h: (0, h)), both, both, table, table, whole((tall, seq))],
         out_specs=[both, half, half],
         out_shape=[shape((2, seq, width), bf16)] + [shape((3, tall // 2, width), bf16)] * 2,
-        compiler_params=params(BIG),
-        cost_estimate=pl.CostEstimate(
-            flops=6 * seq * width * tall, bytes_accessed=16 * seq * width, transcendentals=0
-        ),
+        compiler_params=params(24),
+        cost_estimate=LONG,
         name="weigh",
-    )(info, dq, keep, got, *tables, h1t)
+    )(info, *pinned(dq, keep), got, *pinned(*tables, h1t))
 
 
 def finish_kernel(parts, x, dx2, wqkv, gain, *refs):
@@ -522,12 +519,10 @@
         + [pl.BlockSpec((2, R, a.shape[2]), lambda i: (0, i, 0)) for a in dkvs],
         out_specs=[rows, whole((8, width))],
         out_shape=[shape((seq, width), bf16), shape((8, width), f32)],
-        compiler_params=params(BIG),
-        cost_estimate=pl.CostEstimate(
-            flops=6 * seq * width * width, bytes_accessed=20 * seq * width, transcendentals=0
-        ),
+        compiler_params=params(24),
+        cost_estimate=LONG,
         name="finish",
-    )(x, dx2, weight, gain, *dqs, *dkvs)
+    )(*pinned(x, dx2, weight), gain, *pinned(*dqs, *dkvs))
 
 
 def bit_orders(count):
@@ -586,76 +581,110 @@
         in_specs=[SMEM] + [block(a) for a in args],
         out_specs=[out] * (2 * GROUPS),
         out_shape=[shape((half, rows, width), bf16)] * (2 * GROUPS),
-        compiler_params=params(BIG),
-        cost_estimate=pl.CostEstimate(
-            flops=0, bytes_accessed=6 * GROUPS * count * rows * width, transcendentals=0
-        ),
+        compiler_params=params(30),
+        cost_estimate=COST,
         name="start_sum",
     )(me, *args)
     return outs[0::2], outs[1::2]
 
 
+IN_VMEM = pl.BlockSpec(memory_space=pltpu.VMEM)
+
+
 def step_kernel(*refs):
+    half = refs[0].shape[0] // 2
+    kept, got = refs[:GROUPS], refs[GROUPS : 2 * GROUPS]
+    outs = refs[len(refs) - 2 * GROUPS - len(refs) % 2 :]
     for g in range(GROUPS):
-        low, high, got_low, got_high = refs[4 * g : 4 * g + 4]
-        keep, send = refs[4 * GROUPS + 2 * g : 4 * GROUPS + 2 * g + 2]
-        keep[...] = (low[...].astype(f32) + got_low[...].astype(f32)).astype(bf16)
-        send[...] = (high[...].astype(f32) + got_high[...].astype(f32)).astype(bf16)
-
-
-def step_sum(kept, got):
+        total = (kept[g][...].astype(f32) + got[g][...].astype(f32)).astype(bf16)
+        outs[2 * g][...] = total[:half]
+        outs[2 * g + 1][...] = total[half:]
+    if len(refs) % 2:
+        outs[-1][...] = refs[2 * GROUPS][...] + refs[2 * GROUPS + 1][...]
+
+
+def step_sum(kept, got, small):
     count, rows, width = kept[0].shape
-    half = count // 2
-    steps = min(half, 2)
-    block = (half // steps, rows, width)
-    low = pl.BlockSpec(block, lambda r: (r, 0, 0))
-    high = pl.BlockSpec(block, lambda r: (r + steps, 0, 0))
-    args = []
-    for a, b in zip(kept, got, strict=True):
-        args += [a, a, b, b]
+    args = [*kept, *got, *small]
     outs = pl.pallas_call(
         step_kernel,
-        grid=(steps,),
-        in_specs=[low, high, low, high] * GROUPS,
-        out_specs=[low, low] * GROUPS,
-        out_shape=[shape((half, rows, width), bf16)] * (2 * GROUPS),
-        cost_estimate=pl.CostEstimate(
-            flops=0, bytes_accessed=6 * GROUPS * count * rows * width, transcendentals=0
-        ),
+        in_specs=[IN_VMEM] * len(args),
+        out_specs=[IN_VMEM] * (2 * GROUPS + len(small) // 2),
+        out_shape=[shape((count // 2, rows, width), bf16)] * (2 * GROUPS)
+        + [shape(a.shape, f32) for a in small[:1]],
+        compiler_params=params(16),
+        cost_estimate=COST,
         name="step_sum",
     )(*args)
-    return outs[0::2], outs[1::2]
+    return outs[0 : 2 * GROUPS : 2], outs[1 : 2 * GROUPS : 2], list(outs[2 * GROUPS :])
+
+
+def feed_end_kernel(*refs):
+    ins, (down, up, out) = refs[: 2 * GROUPS], refs[2 * GROUPS :]
+    tall, few = down.shape[0] // GROUPS, out.shape[0] // GROUPS
+    ups = []
+    for g in range(GROUPS):
+        total = ins[g][0].astype(f32) + ins[GROUPS + g][0].astype(f32)
+        down[g * tall : (g + 1) * tall, :] = total[:tall]
+        ups.append(total[tall : 2 * tall])
+        out[g * few : (g + 1) * few, :] = total[2 * tall :]
+    up[...] = jnp.concatenate(ups, axis=0).T
+
+
+def feed_end(kept, got, tall, few):
+    width = kept[0].shape[2]
+    return pl.pallas_call(
+        feed_end_kernel,
+        in_specs=[IN_VMEM] * (2 * GROUPS),
+        out_specs=[IN_VMEM] * 3,
+        out_shape=[shape((tall, width), f32), shape((width, tall), f32), shape((few, width), f32)],
+        compiler_params=params(16),
+        cost_estimate=COST,
+        name="feed_end",
+    )(*kept, *got)
+
+
+def qkv_end_kernel(*refs):
+    ins, small, (out, sums) = refs[: 2 * GROUPS], refs[2 * GROUPS : 2 * GROUPS + 2], refs[2 * GROUPS + 2 :]
+    tall = out.shape[0]
+    cols = ins[0].shape[2]
+    for g in range(GROUPS):
+        total = ins[g][0].astype(f32) + ins[GROUPS + g][0].astype(f32)
+        for part in range(total.shape[0] // tall):
+            at = (2 * g + part) * cols
+            out[:, at : at + cols] = total[part * tall : (part + 1) * tall]
+    sums[...] = small[0][...] + small[1][...]
+
+
+def qkv_end(kept, got, small, tall, wide):
+    return pl.pallas_call(
+        qkv_end_kernel,
+        in_specs=[IN_VMEM] * (2 * GROUPS + 2),
+        out_specs=[IN_VMEM] * 2,
+        out_shape=[shape((tall, wide), f32), shape(small[0].shape, f32)],
+        compiler_params=params(16),
+        cost_estimate=COST,
+        name="qkv_end",
+    )(*kept, *got, *small)
 
 
 def after(value, *earlier):
     return lax.optimization_barrier((value, earlier))[0]
 
 
-def sum_parts(me, kept, got, wheres):
+def sum_parts(me, kept, got, wheres, small):
     orders = bit_orders(lax.axis_size("batch"))
     keep, send = start_sum(me, kept, got, wheres, orders)
     for i in range(len(orders[0])):
         got = [exchange(s, "batch", order[i]) for s, order in zip(send, orders, strict=True)]
+        small = [small[0], exchange(small[0], "batch", orders[0][i])] if small else []
+        if i == len(orders[0]) - 1:
+            break
         earlier = yield send[0]
         if earlier is not None:
-            keep = after(keep, earlier)
-        if i < len(orders[0]) - 1:
-            keep, send = step_sum(keep, got)
-    yield [a[0].astype(f32) + b[0].astype(f32) for a, b in zip(keep, got, strict=True)]
-
-
-def finished(steps, earlier):
-    out = steps.send(earlier)
-    while not isinstance(out, list):
-        out = steps.send(None)
-    return out
-
-
-def sum_all(value):
-    value = value + exchange(value, "stream", 1)
-    for order in bit_orders(lax.axis_size("batch"))[0]:
-        value = value + exchange(value, "batch", order)
-    return value
+            keep = after(list(keep), earlier)
+        keep, send, small = step_sum(keep, got, small)
+    yield keep, got, small
 
 
 def on_device(
@@ -698,30 +727,19 @@
         [by_rows(after(a, dq1)) for a in (down_keep, up_keep, out_keep)],
         [by_rows(a) for a in (down_got, up_got, out_got)],
         [lambda part, g: part * GROUPS + g] * 3,
+        [],
     )
     token = next(early)
     dq2, keep2, send2 = attend_back(info, pairs, pairs, q, ko, vo, kc, vc, o, after(do, token), lse, *tables_t)
     got2 = lax.ppermute(send2, "stream", [(1, 0)])
-    dkv1, qkv_send1, qkv_keep1 = weigh(info, (dq1, after(keep1, dq2)), got1, tables, h1t)
+    token = early.send(dq2)
+    dkv1, qkv_send1, qkv_keep1 = weigh(info, (dq1, after(keep1, token)), got1, tables, h1t)
     qkv_got1 = exchange(qkv_send1, "stream", 1)
-    token = early.send(dkv1)
-    dkv2, qkv_send2, qkv_keep2 = weigh(info, (dq2, after(keep2, token)), got2, tables, h1t)
+    dkv2, qkv_send2, qkv_keep2 = weigh(info, (dq2, after(keep2, dkv1)), got2, tables, h1t)
     qkv_got2 = exchange(qkv_send2, "stream", 1)
-    dx, sums_h = finish(x, dx2, [dq1, dq2], [dkv1, dkv2], qkv_weight, gain1)
-
-    tall = width // (2 * count)
-    split = lambda a: a.reshape(GROUPS * count, tall, a.shape[2])
-    late = sum_parts(
-        me,
-        [split(after(a, dx)) for a in (qkv_keep1, qkv_keep2)],
-        [split(a) for a in (qkv_got1, qkv_got2)],
-        [lambda part, g: g * count + part] * 2,
-    )
-    token = next(late)
-    early.send(token)
-    late.send(None)
-    early = finished(early, None)
-    late = finished(late, None)
+    token = early.send(dkv2)
+    dx, sums_h = finish(after(x, token), dx2, [dq1, dq2], [dkv1, dkv2], qkv_weight, gain1)
+
     small = jnp.concatenate(
         [
             sums_x[:1],
@@ -731,13 +749,30 @@
             jnp.zeros((2, width), f32),
         ]
     )
-    small = sum_all(small)
-
-    qkv_grad = jnp.concatenate([part for e in late for part in (e[:tall], e[tall:])], axis=1)
-    tall = down_keep.shape[0] // (count * GROUPS)
-    down_grad = jnp.concatenate([e[:tall] for e in early])
-    up_grad = jnp.concatenate([e[tall : 2 * tall] for e in early]).T
-    out_grad = jnp.concatenate([e[2 * tall :] for e in early])
+    small_got = exchange(small, "stream", 1)
+    tall = width // (2 * count)
+    split = lambda a: a.reshape(GROUPS * count, tall, a.shape[2])
+    late = sum_parts(
+        me,
+        [split(after(a, small)) for a in (qkv_keep1, qkv_keep2)],
+        [split(a) for a in (qkv_got1, qkv_got2)],
+        [lambda part, g: g * count + part] * 2,
+        [small + small_got],
+    )
+    token = next(late)
+    token = early.send(token)
+    out = late.send(token if isinstance(token, jax.Array) else None)
+    ends = token
+    while not isinstance(ends, tuple):
+        ends = early.send(out)
+        if not isinstance(out, tuple):
+            out = late.send(None if isinstance(ends, tuple) else ends)
+    while not isinstance(out, tuple):
+        out = late.send(None)
+    up_cols = down_keep.shape[0] // count
+    down_grad, up_grad, out_grad = feed_end(ends[0], ends[1], up_cols, tall)
+    qkv_grad, small = qkv_end(*out, tall, 3 * width)
+
     squares = jnp.sum(small[:3], axis=1)
     rms = jnp.sqrt(squares / (small[5, 0] * width))
     return (

time: 290 us -> 255 us (0.88)
  Pallas kernels: 180 us -> 160 us
  waiting for transfers between devices: 38.1 us -> 29.1 us
  starting transfers between devices: 47.7 us -> 42.1 us
  local copies, waits for them, and re-layouts: 15.1 us -> 19.7 us
  other arithmetic: 5.15 us -> 1.23 us
    pallas_call x6 -> x8, Pallas kernels: 14.8 us -> 3.03 us  [the longest x6 1.45 us: step_sum(): pl.pallas_call(step_kernel, in_specs=[IN_VMEM] * len(args), out_specs=[IN...]
    ppermute x34, waiting for transfers between devices: 38.1 us -> 29.1 us  [exchange(): return lax.ppermute(value, axis, [(i, i ^ bit) for i in range(size)])]
    pallas_call x2, Pallas kernels: 13 us -> 6.92 us  [start_sum(): pl.pallas_call(functools.partial(start_kernel, orders, wheres), grid=(wid...]
    ppermute x34, starting transfers between devices: 42.7 us -> 36.9 us  [exchange(): return lax.ppermute(value, axis, [(i, i ^ bit) for i in range(size)])]
    unnamed x67 -> x65, local copies, waits for them, and re-layouts: 9.86 us -> 12.3 us
  transfers between devices with their start and end apart: 37 -> 37, of which waited for: 16 -> 9; matrix products, arithmetic and copies ran while one was open for 3% -> 3% of each run, Pallas kernels for 33% -> 30%
where the time goes in v1:
time: 255 us; the launch traced here: 254 us
  Pallas kernels  160 us (63%)
  starting transfers between devices  42.1 us (17%)
  waiting for transfers between devices  29.1 us (11%)
  local copies, waits for them, and re-layouts  19.7 us (8%)
    pallas_call x1, Pallas kernels, layer(): pl.pallas_call(functools.partial(layer_kernel, (tiles, pairs, chunks)), g...  80.1 us
    pallas_call x2, Pallas kernels, attend_back(): pl.pallas_call(attend_back_kernel, grid=(pairs,), in_specs=[SMEM] + [sour...  38.2 us
    ppermute x34, starting transfers between devices, exchange(): return lax.ppermute(value, axis, [(i, i ^ bit) for i in range(size)])  36.9 us
    ppermute x34, waiting for transfers between devices, exchange(): return lax.ppermute(value, axis, [(i, i ^ bit) for i in range(size)])  29.1 us
    pallas_call x2, Pallas kernels, weigh(): pl.pallas_call(weigh_kernel, grid=(width // PW,), in_specs=[SMEM, pl.Bloc...  12.8 us
    unnamed x65, local copies, waits for them, and re-layouts  12.3 us
    pallas_call x1, Pallas kernels, finish(): pl.pallas_call(functools.partial(finish_kernel, len(dqs)), grid=(seq // R...  9.34 us
    pallas_call x1, Pallas kernels, project(): pl.pallas_call(project_kernel, grid=(seq // R,), in_specs=[SMEM, rows, wh...  9.27 us
  transfers between devices with their start and end apart: 37, of which 9 were waited for; matrix products, arithmetic and copies ran while one was open for 3% of the time, Pallas kernels for 30%

profile of v1, /device:TPU:0, one launch (start us, length us, event | category | flops | bytes accessed | tf_op | source)
XLA Modules:
  0.0 254.1 jit_solution(15325562289188621254)
XLA Ops:
  0.6 2.5 collective-permute-start
  5.6 9.3 %project.1 = (bf16[1024,768]{1,0:T(8,128)(2,1)}, bf16[1024,768]{1,0:T(8,128)(2,1)}, bf16[1024,768]{1,0:T(8,128)(2,1)}, bf16[768,1024]{1,0:T(8,128)(2,1)}, f32[8,768]{1,0:T(8,128)}) custom-call(s32[2]{0:T(128)} %pad_add_fusion.info, bf16[1024,768]{1,0:T(8,128)(2,1)} %bitcast.30, f32[1,768]{1,0:T(1,128)} %reshape.60.gain.gain1, bf16[768,2304]{1,0:T(8,128)(2,1)} %wqkv.1, ...), custom_call_target="tpu_custom_call" | custom-call | flops 34359738368 | bytes 67108864 | tf_op jit(solution)/shard_map/project/pallas_call | solution.py:119
  17.9 80.1 %layer.1 = (bf16[1024,768]{1,0:T(8,128)(2,1)}, bf16[1024,768]{1,0:T(8,128)(2,1)}, bf16[1024,768]{1,0:T(8,128)(2,1)}, f32[6,8,256]{2,1,0:T(8,128)}, bf16[1024,768...) custom-call(s32[2]{0:T(128)} %pad_add_fusion.info, ...), custom_call_target="tpu_custom_call" | custom-call | flops 34359738368 | bytes 67108864 | tf_op jit(solution)/shard_map/layer/pallas_call | solution.py:431
  99.5 19.3 %attend_back.2 = (bf16[1024,384]{1,0:T(8,128)(2,1)S(1)}, bf16[2,1024,384]{2,1,0:T(8,128)(2,1)S(1)}, bf16[2,1024,384]{2,1,0:T(8,128)(2,1)S(1)}) custom-call(s32[2]{0:T(128)S(1)} %copy-done.18, bf16[1024,768]{1,0:T(8,128)(2,1)} %get-tuple-element.116.q, bf16[1024,768]{1,0:T(8,128)(2,1)} %get-tuple-element.117.ko, bf16[1024,768]{1,0:T(8,128)(2,1)} %get-tuple-element.118.vo, ...), custom_call_target="tpu_custom_call" | custom-call | flops 34359738368 | bytes 67108864 | tf_op jit(solution)/shard_map/attend_back/pallas_call | solution.py:258
  122.3 3.9 %start_sum.2 = (bf16[8,72,768]{2,1,0:T(8,128)(2,1)S(1)}, bf16[8,72,768]{2,1,0:T(8,128)(2,1)S(1)}, bf16[8,72,768]{2,1,0:T(8,128)(2,1)S(1)}, bf16[8,72,768]{2,1,0:...) custom-call(s32[1]{0:T(128)} %bitcast.4.me, bf16[48,32,768]{2,1,0:T(8,128)(2,1)S(1)} %bitcast.19, ...), custom_call_target="tpu_custom_call" | custom-call | flops 1048576 | bytes 65536 | tf_op jit(solution)/shard_map/start_sum/pallas_call | solution.py:578
  126.2 2.4 collective-permute-start.4
  128.6 1.5 collective-permute-start.5
  130.1 1.6 collective-permute-start.6
  131.7 18.9 %attend_back.3 = (bf16[1024,384]{1,0:T(8,128)(2,1)S(1)}, bf16[2,1024,384]{2,1,0:T(8,128)(2,1)S(1)}, bf16[2,1024,384]{2,1,0:T(8,128)(2,1)S(1)}) custom-call(s32[2]{0:T(128)S(1)} %copy-done.18, bf16[1024,768]{1,0:T(8,128)(2,1)} %get-tuple-element.116.q, bf16[1024,768]{1,0:T(8,128)(2,1)} %get-tuple-element.117.ko, bf16[1024,768]{1,0:T(8,128)(2,1)} %get-tuple-element.118.vo, ...), custom_call_target="tpu_custom_call" | custom-call | flops 34359738368 | bytes 67108864 | tf_op jit(solution)/shard_map/attend_back/pallas_call | solution.py:258
  152.7 1.5 collective-permute-start.8
  156.0 1.5 collective-permute-start.11
  157.5 6.4 %weigh.2 = (bf16[2,1024,384]{2,1,0:T(8,128)(2,1)S(1)}, bf16[3,384,384]{2,1,0:T(8,128)(2,1)}, bf16[3,384,384]{2,1,0:T(8,128)(2,1)S(1)}) custom-call(s32[2]{0:T(128)S(1)} %copy-done.18, bf16[1024,384]{1,0:T(8,128)(2,1)} %copy-done.23, bf16[2,1024,384]{2,1,0:T(8,128)(2,1)} %copy-done.21, bf16[2,1024,384]{2,1,0:T(8,128)(2,1)S(1)} %collective-permute-done.7.got, ...), custom_call_target="tpu_custom_call" | custom-call | flops 34359738368 | bytes 67108864 | tf_op jit(solution)/shard_map/weigh/pallas_call | solution.py:484
  165.4 6.4 %weigh.3 = (bf16[2,1024,384]{2,1,0:T(8,128)(2,1)S(1)}, bf16[3,384,384]{2,1,0:T(8,128)(2,1)}, bf16[3,384,384]{2,1,0:T(8,128)(2,1)S(1)}) custom-call(s32[2]{0:T(128)S(1)} %copy-done.18, bf16[1024,384]{1,0:T(8,128)(2,1)} %copy-done.24, bf16[2,1024,384]{2,1,0:T(8,128)(2,1)} %copy-done.22, bf16[2,1024,384]{2,1,0:T(8,128)(2,1)S(1)} %collective-permute-done.8.got, ...), custom_call_target="tpu_custom_call" | custom-call | flops 34359738368 | bytes 67108864 | tf_op jit(solution)/shard_map/weigh/pallas_call | solution.py:484
  171.8 6.1 %collective-permute-done.11.refs_5_ = bf16[4,72,768]{2,1,0:T(8,128)(2,1)S(1)} collective-permute-done((bf16[4,72,768]{2,1,0:T(8,128)(2,1)S(1)}, bf16[4,72,768]{2,1,0:T(8,128)(2,1)S(1)}, u32[]{:S(2)}, u32[]{:S(2)}) %collective-permute-start.11) | collective-permute-done | bytes 442400 | tf_op jit(solution)/shard_map/ppermute | solution.py:538
  182.5 9.3 %finish.1 = (bf16[1024,768]{1,0:T(8,128)(2,1)}, f32[8,768]{1,0:T(8,128)S(1)}) custom-call(bf16[1024,768]{1,0:T(8,128)(2,1)} %bitcast.32, f32[1024,768]{1,0:T(8,128)} %get-tuple-element.166.dx2, bf16[768,2304]{1,0:T(8,128)(2,1)} %wqkv.1, f32[1,768]{1,0:T(1,128)S(1)} %copy-done.9, bf16[1024,384]{1,0:T(8,128)(2,1)} %copy-done.23, bf16[1024,384]{1,0:T(8,128)(2,1)} %copy-done.24, ...), custom_call_target="tpu_custom_call" | custom-call | flops 34359738368 | bytes 67108864 | tf_op jit(solution)/shard_map/finish/pallas_call | solution.py:514
  195.0 3.0 %start_sum.3 = (bf16[8,48,384]{2,1,0:T(8,128)(2,1)S(1)}, bf16[8,48,384]{2,1,0:T(8,128)(2,1)S(1)}, bf16[8,48,384]{2,1,0:T(8,128)(2,1)S(1)}, bf16[8,48,384]{2,1,0:...) custom-call(s32[1]{0:T(128)} %bitcast.4.me, bf16[48,24,384]{2,1,0:T(8,128)(2,1)S(1)} %bitcast.22, ...), custom_call_target="tpu_custom_call" | custom-call | flops 1048576 | bytes 65536 | tf_op jit(solution)/shard_map/start_sum/pallas_call | solution.py:578
  198.0 1.6 collective-permute-start.15
  201.7 1.5 collective-permute-start.18
  203.3 6.1 %collective-permute-done.18.refs_7_ = f32[8,768]{1,0:T(8,128)S(1)} collective-permute-done((f32[8,768]{1,0:T(8,128)S(1)}, f32[8,768]{1,0:T(8,128)S(1)}, u32[]{:S(2)}, u32[]{:S(2)}) %collective-permute-start.18) | collective-permute-done | bytes 24608 | tf_op jit(solution)/shard_map/ppermute | solution.py:538
  210.1 1.6 collective-permute-start.32
  211.8 2.6 %collective-permute-start.33 = (bf16[2,72,768]{2,1,0:T(8,128)(2,1)S(1)}, bf16[2,72,768]{2,1,0:T(8,128)(2,1)S(1)}, u32[]{:S(2)}, u32[]{:S(2)}) collective-permute-start(bf16[2,72,768]{2,1,0:T(8,128)(2,1)S(1)} %copy-done.13), channel_id=1, source_target_pairs={{0,8},{1,9},{2,10},{3,11},{4,12},{5,13},{6,14},{7,15},{8,0},{9,1},... | collective-permute-start | bytes 663560 | tf_op jit(solution)/shard_map/ppermute | solution.py:538
  214.8 1.6 collective-permute-start.22
  216.3 2.3 collective-permute-done.22.refs_7_
  220.6 3.1 %collective-permute-done.20.refs_4_ = bf16[4,48,384]{2,1,0:T(8,128)(2,1)S(1)} collective-permute-done((bf16[4,48,384]{2,1,0:T(8,128)(2,1)S(1)}, bf16[4,48,384]{2,1,0:T(8,128)(2,1)S(1)}, u32[]{:S(2)}, u32[]{:S(2)}) %collective-permute-start.20) | collective-permute-done | bytes 147488 | tf_op jit(solution)/shard_map/ppermute | solution.py:538
  223.7 1.6 collective-permute-done.21.refs_5_
  225.4 1.7 collective-permute-start.23
  227.3 2.0 collective-permute-start.34
  229.3 1.6 collective-permute-start.26
  233.4 2.3 collective-permute-start.25
  237.2 4.8 %collective-permute-done.25.refs_5_ = bf16[2,48,384]{2,1,0:T(8,128)(2,1)S(1)} collective-permute-done((bf16[2,48,384]{2,1,0:T(8,128)(2,1)S(1)}, bf16[2,48,384]{2,1,0:T(8,128)(2,1)S(1)}, u32[]{:S(2)}, u32[]{:S(2)}) %collective-permute-start.25) | collective-permute-done | bytes 73760 | tf_op jit(solution)/shard_map/ppermute | solution.py:538
  242.1 2.9 %collective-permute-start.28 = (bf16[1,48,384]{2,1,0:T(8,128)(2,1)S(1)}, bf16[1,48,384]{2,1,0:T(8,128)(2,1)S(1)}, u32[]{:S(2)}, u32[]{:S(2)}) collective-permute-start(bf16[1,48,384]{2,1,0:T(8,128)(2,1)S(1)} %get-tuple-element.201), channel_id=1, source_target_pairs={{0,8},{1,9},{2,10},{3,11},{4,12},{5,13},{6,14},{7,15},{8,0},{9,1},... | collective-permute-start | bytes 110600 | tf_op jit(solution)/shard_map/ppermute | solution.py:538
  248.1 2.9 %collective-permute-done.30.refs_7_ = f32[8,768]{1,0:T(8,128)S(1)} collective-permute-done((f32[8,768]{1,0:T(8,128)S(1)}, f32[8,768]{1,0:T(8,128)S(1)}, u32[]{:S(2)}, u32[]{:S(2)}) %collective-permute-start.30) | collective-permute-done | bytes 24608 | tf_op jit(solution)/shard_map/ppermute | solution.py:538
  (138 shorter events, 38.1 us)
Async XLA Ops:
  0.6 16.1 %collective-permute-start = (bf16[1024,768]{1,0:T(8,128)(2,1)}, bf16[1024,768]{1,0:T(8,128)(2,1)S(1)}, u32[]{:S(2)}, u32[]{:S(2)}) collective-permute-start(bf16[1024,768]{1,0:T(8,128)(2,1)} %bitcast.29), channel_id=1, source_target_pairs={{0,16},{1,17},{2,18},{3,19},{4,20},{5,21},{6,22},{7,23},{8,24},{9,... | collective-permute-start | bytes 4718600 | tf_op jit(solution)/shard_map/ppermute | solution.py:708
  98.1 24.1 %collective-permute-start.3 = (bf16[384,768]{1,0:T(8,128)(2,1)}, bf16[384,768]{1,0:T(8,128)(2,1)S(1)}, u32[]{:S(2)}, u32[]{:S(2)}) collective-permute-start(bf16[384,768]{1,0:T(8,128)(2,1)} %get-tuple-element.134), channel_id=1, source_target_pairs={{0,16},{16,0},{1,17},{17,1},{2,18},{18,2},{3,19},{19,3},{4,20},{20... | collective-permute-start | bytes 1769480 | tf_op jit(solution)/shard_map/ppermute | solution.py:538
  98.2 24.0 %collective-permute-start.1 = (bf16[1536,768]{1,0:T(8,128)(2,1)}, bf16[1536,768]{1,0:T(8,128)(2,1)S(1)}, u32[]{:S(2)}, u32[]{:S(2)}) collective-permute-start(bf16[1536,768]{1,0:T(8,128)(2,1)} %get-tuple-element.128), channel_id=1, source_target_pairs={{0,16},{16,0},{1,17},{17,1},{2,18},{18,2},{3,19},{19,3},{4,20},{20... | collective-permute-start | bytes 7077896 | tf_op jit(solution)/shard_map/ppermute | solution.py:538
  98.7 23.6 %collective-permute-start.2 = (bf16[1536,768]{1,0:T(8,128)(2,1)}, bf16[1536,768]{1,0:T(8,128)(2,1)S(1)}, u32[]{:S(2)}, u32[]{:S(2)}) collective-permute-start(bf16[1536,768]{1,0:T(8,128)(2,1)} %get-tuple-element.131), channel_id=1, source_target_pairs={{0,16},{16,0},{1,17},{17,1},{2,18},{18,2},{3,19},{19,3},{4,20},{20... | collective-permute-start | bytes 7077896 | tf_op jit(solution)/shard_map/ppermute | solution.py:538
  120.9 36.6 %collective-permute-start.7 = (bf16[2,1024,384]{2,1,0:T(8,128)(2,1)S(1)}, bf16[2,1024,384]{2,1,0:T(8,128)(2,1)S(1)}, u32[]{:S(2)}, u32[]{:S(2)}) collective-permute-start(bf16[2,1024,384]{2,1,0:T(8,128)(2,1)S(1)} %get-tuple-element.153), channel_id=1, source_target_pairs={{16,0},{17,1},{18,2},{19,3},{20,4},{21,5},{22,6},{23,7},{24,8},{25... | collective-permute-start | bytes 4718600 | tf_op jit(solution)/shard_map/ppermute | solution.py:724
  126.2 28.0 %collective-permute-start.4 = (bf16[8,72,768]{2,1,0:T(8,128)(2,1)S(1)}, bf16[8,72,768]{2,1,0:T(8,128)(2,1)S(1)}, u32[]{:S(2)}, u32[]{:S(2)}) collective-permute-start(bf16[8,72,768]{2,1,0:T(8,128)(2,1)S(1)} %get-tuple-element.138), channel_id=1, source_target_pairs={{0,1},{1,0},{2,3},{3,2},{4,5},{5,4},{6,7},{7,6},{8,9},{9,8},{10,11... | collective-permute-start | bytes 2654216 | tf_op jit(solution)/shard_map/ppermute | solution.py:538
  128.6 25.6 %collective-permute-start.5 = (bf16[8,72,768]{2,1,0:T(8,128)(2,1)S(1)}, bf16[8,72,768]{2,1,0:T(8,128)(2,1)S(1)}, u32[]{:S(2)}, u32[]{:S(2)}) collective-permute-start(bf16[8,72,768]{2,1,0:T(8,128)(2,1)S(1)} %get-tuple-element.144), channel_id=1, source_target_pairs={{0,2},{1,3},{2,0},{3,1},{4,6},{5,7},{6,4},{7,5},{8,10},{9,11},{10,... | collective-permute-start | bytes 2654216 | tf_op jit(solution)/shard_map/ppermute | solution.py:538
  130.1 24.1 %collective-permute-start.6 = (bf16[8,72,768]{2,1,0:T(8,128)(2,1)S(1)}, bf16[8,72,768]{2,1,0:T(8,128)(2,1)S(1)}, u32[]{:S(2)}, u32[]{:S(2)}) collective-permute-start(bf16[8,72,768]{2,1,0:T(8,128)(2,1)S(1)} %get-tuple-element.145), channel_id=1, source_target_pairs={{0,4},{1,5},{2,6},{3,7},{4,0},{5,1},{6,2},{7,3},{8,12},{9,13},{10,... | collective-permute-start | bytes 2654216 | tf_op jit(solution)/shard_map/ppermute | solution.py:538
  152.7 12.7 %collective-permute-start.8 = (bf16[2,1024,384]{2,1,0:T(8,128)(2,1)S(1)}, bf16[2,1024,384]{2,1,0:T(8,128)(2,1)S(1)}, u32[]{:S(2)}, u32[]{:S(2)}) collective-permute-start(bf16[2,1024,384]{2,1,0:T(8,128)(2,1)S(1)} %get-tuple-element.157), channel_id=1, source_target_pairs={{16,0},{17,1},{18,2},{19,3},{20,4},{21,5},{22,6},{23,7},{24,8},{25... | collective-permute-start | bytes 4718600 | tf_op jit(solution)/shard_map/ppermute | solution.py:734
  154.9 23.1 %collective-permute-start.9 = (bf16[4,72,768]{2,1,0:T(8,128)(2,1)S(1)}, bf16[4,72,768]{2,1,0:T(8,128)(2,1)S(1)}, u32[]{:S(2)}, u32[]{:S(2)}) collective-permute-start(bf16[4,72,768]{2,1,0:T(8,128)(2,1)S(1)} %get-tuple-element.151), channel_id=1, source_target_pairs={{0,2},{1,3},{2,0},{3,1},{4,6},{5,7},{6,4},{7,5},{8,10},{9,11},{10,... | collective-permute-start | bytes 1327112 | tf_op jit(solution)/shard_map/ppermute | solution.py:538
  155.4 16.4 %collective-permute-start.10 = (bf16[4,72,768]{2,1,0:T(8,128)(2,1)S(1)}, bf16[4,72,768]{2,1,0:T(8,128)(2,1)S(1)}, u32[]{:S(2)}, u32[]{:S(2)}) collective-permute-start(bf16[4,72,768]{2,1,0:T(8,128)(2,1)S(1)} %get-tuple-element.162), channel_id=1, source_target_pairs={{0,1},{1,0},{2,3},{3,2},{4,5},{5,4},{6,7},{7,6},{8,9},{9,8},{10,11... | collective-permute-start | bytes 1327112 | tf_op jit(solution)/shard_map/ppermute | solution.py:538
  156.0 22.0 %collective-permute-start.11 = (bf16[4,72,768]{2,1,0:T(8,128)(2,1)S(1)}, bf16[4,72,768]{2,1,0:T(8,128)(2,1)S(1)}, u32[]{:S(2)}, u32[]{:S(2)}) collective-permute-start(bf16[4,72,768]{2,1,0:T(8,128)(2,1)S(1)} %get-tuple-element.163), channel_id=1, source_target_pairs={{0,1},{1,0},{2,3},{3,2},{4,5},{5,4},{6,7},{7,6},{8,9},{9,8},{10,11... | collective-permute-start | bytes 1327112 | tf_op jit(solution)/shard_map/ppermute | solution.py:538
  165.0 29.9 %collective-permute-start.12 = (bf16[3,384,384]{2,1,0:T(8,128)(2,1)}, bf16[3,384,384]{2,1,0:T(8,128)(2,1)S(1)}, u32[]{:S(2)}, u32[]{:S(2)}) collective-permute-start(bf16[3,384,384]{2,1,0:T(8,128)(2,1)} %get-tuple-element.173), channel_id=1, source_target_pairs={{0,16},{16,0},{1,17},{17,1},{2,18},{18,2},{3,19},{19,3},{4,20},{20... | collective-permute-start | bytes 2654216 | tf_op jit(solution)/shard_map/ppermute | solution.py:538
  182.4 12.6 %collective-permute-start.13 = (bf16[3,384,384]{2,1,0:T(8,128)(2,1)}, bf16[3,384,384]{2,1,0:T(8,128)(2,1)S(1)}, u32[]{:S(2)}, u32[]{:S(2)}) collective-permute-start(bf16[3,384,384]{2,1,0:T(8,128)(2,1)} %get-tuple-element.176), channel_id=1, source_target_pairs={{0,16},{16,0},{1,17},{17,1},{2,18},{18,2},{3,19},{19,3},{4,20},{20... | collective-permute-start | bytes 2654216 | tf_op jit(solution)/shard_map/ppermute | solution.py:538
  198.0 11.3 %collective-permute-start.15 = (bf16[8,48,384]{2,1,0:T(8,128)(2,1)S(1)}, bf16[8,48,384]{2,1,0:T(8,128)(2,1)S(1)}, u32[]{:S(2)}, u32[]{:S(2)}) collective-permute-start(bf16[8,48,384]{2,1,0:T(8,128)(2,1)S(1)} %get-tuple-element.181), channel_id=1, source_target_pairs={{0,2},{1,3},{2,0},{3,1},{4,6},{5,7},{6,4},{7,5},{8,10},{9,11},{10,... | collective-permute-start | bytes 884744 | tf_op jit(solution)/shard_map/ppermute | solution.py:538
  199.6 9.8 %collective-permute-start.16 = (bf16[8,48,384]{2,1,0:T(8,128)(2,1)S(1)}, bf16[8,48,384]{2,1,0:T(8,128)(2,1)S(1)}, u32[]{:S(2)}, u32[]{:S(2)}) collective-permute-start(bf16[8,48,384]{2,1,0:T(8,128)(2,1)S(1)} %get-tuple-element.182), channel_id=1, source_target_pairs={{0,4},{1,5},{2,6},{3,7},{4,0},{5,1},{6,2},{7,3},{8,12},{9,13},{10,... | collective-permute-start | bytes 884744 | tf_op jit(solution)/shard_map/ppermute | solution.py:538
  200.1 9.3 %collective-permute-start.14 = (bf16[8,48,384]{2,1,0:T(8,128)(2,1)S(1)}, bf16[8,48,384]{2,1,0:T(8,128)(2,1)S(1)}, u32[]{:S(2)}, u32[]{:S(2)}) collective-permute-start(bf16[8,48,384]{2,1,0:T(8,128)(2,1)S(1)} %get-tuple-element.180), channel_id=1, source_target_pairs={{0,1},{1,0},{2,3},{3,2},{4,5},{5,4},{6,7},{7,6},{8,9},{9,8},{10,11... | collective-permute-start | bytes 884744 | tf_op jit(solution)/shard_map/ppermute | solution.py:538
  201.7 7.6 %collective-permute-start.18 = (f32[8,768]{1,0:T(8,128)S(1)}, f32[8,768]{1,0:T(8,128)S(1)}, u32[]{:S(2)}, u32[]{:S(2)}) collective-permute-start(f32[8,768]{1,0:T(8,128)S(1)} %add.3.refs_6_), channel_id=1, source_target_pairs={{0,1},{1,0},{2,3},{3,2},{4,5},{5,4},{6,7},{7,6},{8,9},{9,8},{10,11... | collective-permute-start | bytes 73736 | tf_op jit(solution)/shard_map/ppermute | solution.py:538
  209.6 9.5 %collective-permute-start.19 = (bf16[4,48,384]{2,1,0:T(8,128)(2,1)S(1)}, bf16[4,48,384]{2,1,0:T(8,128)(2,1)S(1)}, u32[]{:S(2)}, u32[]{:S(2)}) collective-permute-start(bf16[4,48,384]{2,1,0:T(8,128)(2,1)S(1)} %get-tuple-element.186), channel_id=1, source_target_pairs={{0,2},{1,3},{2,0},{3,1},{4,6},{5,7},{6,4},{7,5},{8,10},{9,11},{10,... | collective-permute-start | bytes 442376 | tf_op jit(solution)/shard_map/ppermute | solution.py:538
  210.1 17.0 %collective-permute-start.32 = (bf16[2,72,768]{2,1,0:T(8,128)(2,1)S(1)}, bf16[2,72,768]{2,1,0:T(8,128)(2,1)S(1)}, u32[]{:S(2)}, u32[]{:S(2)}) collective-permute-start(bf16[2,72,768]{2,1,0:T(8,128)(2,1)S(1)} %copy-done.15), channel_id=1, source_target_pairs={{0,4},{1,5},{2,6},{3,7},{4,0},{5,1},{6,2},{7,3},{8,12},{9,13},{10,... | collective-permute-start | bytes 663560 | tf_op jit(solution)/shard_map/ppermute | solution.py:538
  211.8 15.3 %collective-permute-start.33 = (bf16[2,72,768]{2,1,0:T(8,128)(2,1)S(1)}, bf16[2,72,768]{2,1,0:T(8,128)(2,1)S(1)}, u32[]{:S(2)}, u32[]{:S(2)}) collective-permute-start(bf16[2,72,768]{2,1,0:T(8,128)(2,1)S(1)} %copy-done.13), channel_id=1, source_target_pairs={{0,8},{1,9},{2,10},{3,11},{4,12},{5,13},{6,14},{7,15},{8,0},{9,1},... | collective-permute-start | bytes 663560 | tf_op jit(solution)/shard_map/ppermute | solution.py:538
  214.3 12.8 %collective-permute-start.31 = (bf16[2,72,768]{2,1,0:T(8,128)(2,1)S(1)}, bf16[2,72,768]{2,1,0:T(8,128)(2,1)S(1)}, u32[]{:S(2)}, u32[]{:S(2)}) collective-permute-start(bf16[2,72,768]{2,1,0:T(8,128)(2,1)S(1)} %copy-done.11), channel_id=1, source_target_pairs={{0,4},{1,5},{2,6},{3,7},{4,0},{5,1},{6,2},{7,3},{8,12},{9,13},{10,... | collective-permute-start | bytes 663560 | tf_op jit(solution)/shard_map/ppermute | solution.py:538
  219.1 6.2 %collective-permute-start.21 = (bf16[4,48,384]{2,1,0:T(8,128)(2,1)S(1)}, bf16[4,48,384]{2,1,0:T(8,128)(2,1)S(1)}, u32[]{:S(2)}, u32[]{:S(2)}) collective-permute-start(bf16[4,48,384]{2,1,0:T(8,128)(2,1)S(1)} %get-tuple-element.188), channel_id=1, source_target_pairs={{0,1},{1,0},{2,3},{3,2},{4,5},{5,4},{6,7},{7,6},{8,9},{9,8},{10,11... | collective-permute-start | bytes 442376 | tf_op jit(solution)/shard_map/ppermute | solution.py:538
  225.4 10.3 %collective-permute-start.23 = (bf16[2,48,384]{2,1,0:T(8,128)(2,1)S(1)}, bf16[2,48,384]{2,1,0:T(8,128)(2,1)S(1)}, u32[]{:S(2)}, u32[]{:S(2)}) collective-permute-start(bf16[2,48,384]{2,1,0:T(8,128)(2,1)S(1)} %get-tuple-element.193), channel_id=1, source_target_pairs={{0,4},{1,5},{2,6},{3,7},{4,0},{5,1},{6,2},{7,3},{8,12},{9,13},{10,... | collective-permute-start | bytes 221192 | tf_op jit(solution)/shard_map/ppermute | solution.py:538
  227.3 17.7 %collective-permute-start.34 = (bf16[1,72,768]{2,1,0:T(8,128)(2,1)S(1)}, bf16[1,72,768]{2,1,0:T(8,128)(2,1)S(1)}, u32[]{:S(2)}, u32[]{:S(2)}) collective-permute-start(bf16[1,72,768]{2,1,0:T(8,128)(2,1)S(1)} %get-tuple-element.216), channel_id=1, source_target_pairs={{0,8},{1,9},{2,10},{3,11},{4,12},{5,13},{6,14},{7,15},{8,0},{9,1},... | collective-permute-start | bytes 331784 | tf_op jit(solution)/shard_map/ppermute | solution.py:538
  230.9 15.4 %collective-permute-start.35 = (bf16[1,72,768]{2,1,0:T(8,128)(2,1)S(1)}, bf16[1,72,768]{2,1,0:T(8,128)(2,1)S(1)}, u32[]{:S(2)}, u32[]{:S(2)}) collective-permute-start(bf16[1,72,768]{2,1,0:T(8,128)(2,1)S(1)} %get-tuple-element.217), channel_id=1, source_target_pairs={{0,8},{1,9},{2,10},{3,11},{4,12},{5,13},{6,14},{7,15},{8,0},{9,1},... | collective-permute-start | bytes 331784 | tf_op jit(solution)/shard_map/ppermute | solution.py:538
  231.3 5.9 %collective-permute-start.24 = (bf16[2,48,384]{2,1,0:T(8,128)(2,1)S(1)}, bf16[2,48,384]{2,1,0:T(8,128)(2,1)S(1)}, u32[]{:S(2)}, u32[]{:S(2)}) collective-permute-start(bf16[2,48,384]{2,1,0:T(8,128)(2,1)S(1)} %get-tuple-element.194), channel_id=1, source_target_pairs={{0,4},{1,5},{2,6},{3,7},{4,0},{5,1},{6,2},{7,3},{8,12},{9,13},{10,... | collective-permute-start | bytes 221192 | tf_op jit(solution)/shard_map/ppermute | solution.py:538
  233.4 8.6 %collective-permute-start.25 = (bf16[2,48,384]{2,1,0:T(8,128)(2,1)S(1)}, bf16[2,48,384]{2,1,0:T(8,128)(2,1)S(1)}, u32[]{:S(2)}, u32[]{:S(2)}) collective-permute-start(bf16[2,48,384]{2,1,0:T(8,128)(2,1)S(1)} %get-tuple-element.195), channel_id=1, source_target_pairs={{0,8},{1,9},{2,10},{3,11},{4,12},{5,13},{6,14},{7,15},{8,0},{9,1},... | collective-permute-start | bytes 221192 | tf_op jit(solution)/shard_map/ppermute | solution.py:538
  235.7 10.7 %collective-permute-start.36 = (bf16[1,72,768]{2,1,0:T(8,128)(2,1)S(1)}, bf16[1,72,768]{2,1,0:T(8,128)(2,1)S(1)}, u32[]{:S(2)}, u32[]{:S(2)}) collective-permute-start(bf16[1,72,768]{2,1,0:T(8,128)(2,1)S(1)} %get-tuple-element.218), channel_id=1, source_target_pairs={{0,2},{1,3},{2,0},{3,1},{4,6},{5,7},{6,4},{7,5},{8,10},{9,11},{10,... | collective-permute-start | bytes 331784 | tf_op jit(solution)/shard_map/ppermute | solution.py:538
  242.0 9.0 %collective-permute-start.27 = (bf16[1,48,384]{2,1,0:T(8,128)(2,1)S(1)}, bf16[1,48,384]{2,1,0:T(8,128)(2,1)S(1)}, u32[]{:S(2)}, u32[]{:S(2)}) collective-permute-start(bf16[1,48,384]{2,1,0:T(8,128)(2,1)S(1)} %get-tuple-element.200), channel_id=1, source_target_pairs={{0,8},{1,9},{2,10},{3,11},{4,12},{5,13},{6,14},{7,15},{8,0},{9,1},... | collective-permute-start | bytes 110600 | tf_op jit(solution)/shard_map/ppermute | solution.py:538
  242.1 8.9 %collective-permute-start.28 = (bf16[1,48,384]{2,1,0:T(8,128)(2,1)S(1)}, bf16[1,48,384]{2,1,0:T(8,128)(2,1)S(1)}, u32[]{:S(2)}, u32[]{:S(2)}) collective-permute-start(bf16[1,48,384]{2,1,0:T(8,128)(2,1)S(1)} %get-tuple-element.201), channel_id=1, source_target_pairs={{0,8},{1,9},{2,10},{3,11},{4,12},{5,13},{6,14},{7,15},{8,0},{9,1},... | collective-permute-start | bytes 110600 | tf_op jit(solution)/shard_map/ppermute | solution.py:538
  245.0 6.0 %collective-permute-start.29 = (bf16[1,48,384]{2,1,0:T(8,128)(2,1)S(1)}, bf16[1,48,384]{2,1,0:T(8,128)(2,1)S(1)}, u32[]{:S(2)}, u32[]{:S(2)}) collective-permute-start(bf16[1,48,384]{2,1,0:T(8,128)(2,1)S(1)} %get-tuple-element.202), channel_id=1, source_target_pairs={{0,2},{1,3},{2,0},{3,1},{4,6},{5,7},{6,4},{7,5},{8,10},{9,11},{10,... | collective-permute-start | bytes 110600 | tf_op jit(solution)/shard_map/ppermute | solution.py:538
  (37 other events, 548.5 us)

commit v2 on v1

--- a/solution.py
+++ b/solution.py
@@ -18,6 +18,7 @@
 PW = 2 * HD
 T = 128
 R = 256
+AHEAD = 2
 FC = 512
 SCALE = HD**-0.5
 BIG = 60
@@ -27,6 +28,7 @@
 LONG = pl.CostEstimate(flops=1 << 35, bytes_accessed=1 << 26, transcendentals=0)
 
 SMEM = pl.BlockSpec(memory_space=pltpu.SMEM)
+IN_VMEM = pl.BlockSpec(memory_space=pltpu.VMEM)
 
 
 def params(mib):
@@ -94,6 +96,11 @@
     return jnp.sum(v, axis=0, keepdims=True)
 
 
+def by_pairs(ref, rows, value):
+    for p in range(ref.shape[0]):
+        ref[p, rows, :] = value[:, p * PW : (p + 1) * PW].astype(ref.dtype)
+
+
 def project_kernel(info, x, gain, wq, wk, wv, cosine, signed, q, k, v, h1t, sums):
     at = pl.program_id(0)
 
@@ -103,9 +110,9 @@
 
     value = x[...].astype(f32)
     h1 = (value * inv_rms(value) * gain[...]).astype(bf16)
-    q[...] = rotated(nn(h1, wq[...]), cosine[...], signed[...], 1.0).astype(bf16)
-    k[...] = rotated(nn(h1, wk[...]), cosine[...], signed[...], 1.0).astype(bf16)
-    v[...] = nn(h1, wv[...]).astype(bf16)
+    by_pairs(q, slice(None), rotated(nn(h1, wq[...]), cosine[...], signed[...], 1.0))
+    by_pairs(k, slice(None), rotated(nn(h1, wk[...]), cosine[...], signed[...], 1.0))
+    by_pairs(v, slice(None), nn(h1, wv[...]))
     h1t[...] = h1.T
     weight = token_weight(at * R, info[1], R)
     sums[0:1, :] += row_sum(jnp.where(weight, value * value, 0.0))
@@ -115,13 +122,14 @@
     seq, width = x.shape
     rows = pl.BlockSpec((R, width), lambda i: (i, 0))
     table = pl.BlockSpec((R, PW), lambda i: (i, 0))
+    heads = pl.BlockSpec((width // PW, R, PW), lambda i: (0, i, 0))
     third = lambda c: pl.BlockSpec((width, width), lambda i: (0, c), pipeline_mode=pl.Buffered(1))
     return pl.pallas_call(
         project_kernel,
         grid=(seq // R,),
         in_specs=[SMEM, rows, whole((1, width)), third(0), third(1), third(2), table, table],
-        out_specs=[rows, rows, rows, pl.BlockSpec((width, R), lambda i: (0, i)), whole((8, width))],
-        out_shape=[shape((seq, width), bf16)] * 3 + [shape((width, seq), bf16), shape((8, width), f32)],
+        out_specs=[heads, heads, heads, pl.BlockSpec((width, R), lambda i: (0, i)), whole((8, width))],
+        out_shape=[shape((width // PW, seq, PW), bf16)] * 3 + [shape((width, seq), bf16), shape((8, width), f32)],
         compiler_params=params(BIG),
         cost_estimate=LONG,
         name="project",
@@ -147,12 +155,13 @@
     return out
 
 
-def edge_masks(noisy):
+def edge_bias(ref, noisy):
     row = lax.broadcasted_iota(jnp.int32, (T, 2 * T), 0) // BLK
     col = (lax.broadcasted_iota(jnp.int32, (T, 2 * T), 1) % T) // BLK
     own = jnp.logical_or(row == col, jnp.logical_and(row < col, noisy == 0))
     other = jnp.logical_and(row < col, noisy == 1)
-    return own, other
+    ref[:T, :] = jnp.where(own, 0.0, NEG)
+    ref[T:, :] = jnp.where(other, 0.0, NEG)
 
 
 def masked(s, start, length):
@@ -164,19 +173,19 @@
     return op(v.reshape(v.shape[0] // 8, 8, v.shape[1]), axis=0)
 
 
-def attend_pair(noisy, length, q, ko, vo, kc, vc, store, lse, vo_t, vc_t, scores):
+def attend_pair(length, q, ko, vo, kc, vc, store, lse, vo_t, vc_t, scores, bias):
     seq = q.shape[0]
     low = lax.broadcasted_iota(jnp.int32, (1, PW), 1) < HD
-    own_mask, other_mask = edge_masks(noisy)
     vo_t[...] = vo[...].T
     vc_t[...] = vc[...].T
-    for i in range(seq // T):
+
+    def score(i):
         at = pl.ds(i * T, T)
         q2 = stacked(q[at, :] * bf16(SCALE), low)
-        buf = scores.at[i % 2]
-        edge = nt(jnp.concatenate([ko[at, :], kc[at, :]], 0), q2)
-        own = masked(jnp.where(own_mask, edge[:T], NEG), i * T, length)
-        other = masked(jnp.where(other_mask, edge[T:], NEG), i * T, length)
+        buf = scores.at[i % AHEAD]
+        edge = nt(jnp.concatenate([ko[at, :], kc[at, :]], 0), q2) + bias[...]
+        own = masked(edge[:T], i * T, length)
+        other = masked(edge[T:], i * T, length)
         buf[pl.ds(0, T), :] = own
         buf[pl.ds(T, T), :] = other
         top = over_rows(jnp.max, jnp.maximum(own, other))
@@ -184,7 +193,11 @@
             s = masked(nt(kc[pl.ds(start, size), :], q2), start, length)
             buf[pl.ds(2 * T + start, size), :] = s
             top = jnp.maximum(top, over_rows(jnp.max, s))
-        top = jnp.max(top, axis=0, keepdims=True)
+        return jnp.max(top, axis=0, keepdims=True)
+
+    def mix(i, top):
+        at = pl.ds(i * T, T)
+        buf = scores.at[i % AHEAD]
         p = jnp.exp(buf[pl.ds(0, 2 * T), :] - top)
         total = over_rows(jnp.sum, p)
         acc = nn(jnp.concatenate([vo_t[:, at], vc_t[:, at]], 1), p.astype(bf16))
@@ -194,7 +207,14 @@
             acc = acc + nn(vc_t[:, pl.ds(start, size)], p.astype(bf16))
         total = row_sum(total)
         lse[0, pl.ds(i, 1), :] = top + jnp.log(total)
-        store(at, unstacked(acc / total))
+        store(at, unstacked(acc * (1.0 / total)))
+
+    tops = {}
+    for i in range(seq // T + AHEAD - 1):
+        if i < seq // T:
+            tops[i] = score(i)
+        if i >= AHEAD - 1:
+            mix(i - AHEAD + 1, tops.pop(i - AHEAD + 1))
 
 
 def turned_back(v, cosine, sine):
@@ -206,42 +226,70 @@
 
 
 def attend_back_kernel(
-    info, q, ko, vo, kc, vc, o, do, lse, cosine, sine, dq, keep, send, ko_t, kc_t, dko, dvo, dkc, dvc
+    info, q, ko, vo, kc, vc, o, do, lse, cosine, sine, dq, keep, send, ko_t, kc_t, dko, dvo, dkc, dvc, bias
 ):
     noisy, length = info[0], info[1]
+    q, ko, vo, kc, vc = (ref.at[0] for ref in (q, ko, vo, kc, vc))
     seq = q.shape[0]
     low = lax.broadcasted_iota(jnp.int32, (1, PW), 1) < HD
-    own_mask, other_mask = edge_masks(noisy)
+
+    @pl.when(pl.program_id(0) == 0)
+    def _():
+        edge_bias(bias, noisy)
+
     ko_t[...] = ko[...].T
     kc_t[...] = kc[...].T
-    for i in range(seq // T):
+
+    def tile(i):
         at = pl.ds(i * T, T)
-        q2 = stacked(q[at, :] * bf16(SCALE), low)
-        do2 = stacked(do[at, :], low)
         prod = (do[at, :].astype(f32) * o[at, :].astype(f32)).T
         delta = jnp.concatenate([row_sum(prod[:HD]), row_sum(prod[HD:])], 1)
-        norm = lse[0, pl.ds(i, 1), :]
-        s = nt(jnp.concatenate([ko[at, :], kc[at, :]], 0), q2)
-        own = masked(jnp.where(own_mask, s[:T], NEG), i * T, length)
-        other = masked(jnp.where(other_mask, s[T:], NEG), i * T, length)
-        p = jnp.exp(jnp.concatenate([own, other], 0) - norm)
-        dp = nt(jnp.concatenate([vo[at, :], vc[at, :]], 0), do2)
-        ds = (p * (dp - delta)).astype(bf16)
-        dv = nn(p.astype(bf16), do2)
-        dk = nn(ds, q2)
-        dvo[at, :] = dv[:T]
-        dko[at, :] = dk[:T]
-        dvc[at, :] = dv[T:]
-        dkc[at, :] = dk[T:]
-        dq_t = nn(jnp.concatenate([ko_t[:, at], kc_t[:, at]], 1), ds)
-        for start, size in chunks_of(i):
-            rows = pl.ds(start, size)
-            p = jnp.exp(masked(nt(kc[rows, :], q2), start, length) - norm)
-            ds = (p * (nt(vc[rows, :], do2) - delta)).astype(bf16)
-            dvc[rows, :] += nn(p.astype(bf16), do2)
-            dkc[rows, :] += nn(ds, q2)
-            dq_t = dq_t + nn(kc_t[:, rows], ds)
-        dq[at, :] = (turned_back(unstacked(dq_t), cosine[:, at], sine[:, at]) * SCALE).T.astype(bf16)
+        q2 = stacked(q[at, :] * bf16(SCALE), low)
+        return q2, stacked(do[at, :], low), lse[0, pl.ds(i, 1), :], delta
+
+    def products(i, start, size, q2, do2):
+        if start is None:
+            at = pl.ds(i * T, T)
+            s = nt(jnp.concatenate([ko[at, :], kc[at, :]], 0), q2) + bias[...]
+            s = jnp.concatenate([masked(s[:T], i * T, length), masked(s[T:], i * T, length)], 0)
+            return s, nt(jnp.concatenate([vo[at, :], vc[at, :]], 0), do2)
+        rows = pl.ds(start, size)
+        return masked(nt(kc[rows, :], q2), start, length), nt(vc[rows, :], do2)
+
+    def gather(i, start, size, q2, do2, p, ds, dq_t):
+        at = pl.ds(i * T, T)
+        dv, dk = nn(p, do2), nn(ds, q2)
+        if start is None:
+            dvo[at, :] = dv[:T]
+            dko[at, :] = dk[:T]
+            dvc[at, :] = dv[T:]
+            dkc[at, :] = dk[T:]
+            return nn(jnp.concatenate([ko_t[:, at], kc_t[:, at]], 1), ds)
+        rows = pl.ds(start, size)
+        dvc[rows, :] += dv
+        dkc[rows, :] += dk
+        return dq_t + nn(kc_t[:, rows], ds)
+
+    work = [(i, *c) for i in range(seq // T) for c in [(None, None)] + chunks_of(i)]
+    tiles, made, weighed, dq_t = {}, {}, {}, None
+    for n in range(len(work) + 2):
+        if n < len(work):
+            i = work[n][0]
+            if i not in tiles:
+                tiles[i] = tile(i)
+            made[n] = products(*work[n], *tiles[i][:2])
+        if 0 <= n - 1 < len(work):
+            _, _, norm, delta = tiles[work[n - 1][0]]
+            s, dp = made.pop(n - 1)
+            p = jnp.exp(s - norm)
+            weighed[n - 1] = p.astype(bf16), (p * (dp - delta)).astype(bf16)
+        if n >= 2:
+            i, start, size = work[n - 2]
+            dq_t = gather(i, start, size, *tiles[i][:2], *weighed.pop(n - 2), dq_t)
+            if n == len(work) + 1 or work[n - 1][0] != i:
+                at = pl.ds(i * T, T)
+                out = turned_back(unstacked(dq_t), cosine[:, at], sine[:, at]) * SCALE
+                dq[at, :] = out.T.astype(bf16)
     clean = (1 - noisy).astype(f32)
     for at, own, other in ((0, dko, dkc), (1, dvo, dvc)):
         keep[at] = (own[...] + clean * other[...]).astype(bf16)
@@ -249,8 +297,9 @@
 
 
 def attend_back(info, first, pairs, q, ko, vo, kc, vc, o, do, lse, cosine, sine):
-    seq = q.shape[0]
+    seq = q.shape[1]
     width = pairs * PW
+    heads = pl.BlockSpec((1, seq, PW), lambda h: (first + h, 0, 0))
     source = pl.BlockSpec((seq, PW), lambda h: (0, first + h))
     both = pl.BlockSpec((2, seq, PW), lambda h: (0, 0, h))
     lines = pl.BlockSpec((1, seq // T, 2 * T), lambda h: (first + h, 0, 0))
@@ -258,10 +307,12 @@
     return pl.pallas_call(
         attend_back_kernel,
         grid=(pairs,),
-        in_specs=[SMEM] + [source] * 7 + [lines, table, table],
+        in_specs=[SMEM] + [heads] * 5 + [source] * 2 + [lines, table, table],
         out_specs=[pl.BlockSpec((seq, PW), lambda h: (0, h)), both, both],
         out_shape=[shape((seq, width), bf16)] + [shape((2, seq, width), bf16)] * 2,
-        scratch_shapes=[pltpu.VMEM((PW, seq), bf16)] * 2 + [pltpu.VMEM((seq, PW), f32)] * 4,
+        scratch_shapes=[pltpu.VMEM((PW, seq), bf16)] * 2
+        + [pltpu.VMEM((seq, PW), f32)] * 4
+        + [pltpu.VMEM((2 * T, 2 * T), f32)],
         compiler_params=params(24),
         cost_estimate=LONG,
         name="attend_back",
@@ -273,89 +324,116 @@
 
 
 def layer_kernel(
-    plan, info, x, received, gain1, gain2, wk, wv, cosine, signed, q, ko, vo, wo_any, dy_any, w1_any, w2_any,
-    kc_out, vc_out, o_out, lse, out, dx2, do, up_send, up_keep, down_send, down_keep, g_send, g_keep, sums,
-    kc, vc, vo_t, vc_t, scores, o, o_t, x2, h2, m, dh, act, du, acc, wo, dy, w1, w2, sem_a, sem_1, sem_2,
+    info, gain1, gain2, x_any, received_any, wqkv_any, cosine_any, signed_any, q_any, ko_any, vo_any, wo_any,
+    dy_any, w1_any, w2_any,
+    kc_out, vc_out, o_out, lse_out, out_any, dx2_any, do_any,
+    up_send, up_keep, down_send, down_keep, g_send, g_keep, sums,
+    x, received, wkv, cosine, signed, q, ko, vo, wo, dy, w1, w2,
+    kc, vc, vo_t, vc_t, scores, bias, o, o_t, lse, x2, h2, m, dh, act, du, up_grad, down_grad, half_grads,
+    sem_in, sem_1, sem_2, sem_out, sem_up, sem_down, sem_tile,
 ):
-    step = pl.program_id(0)
     noisy, length = info[0], info[1]
-    tiles, pairs, chunks = plan
-    at_attend, at_join = tiles, tiles + pairs
-    at_feed, at_middle = at_join + tiles, at_join + tiles + chunks
-    seq = q.shape[0]
-
-    def fetch(c):
+    seq, width = x.shape
+    chunks, pairs, tiles = w1.shape[0], kc.shape[0], seq // R
+    copy = pltpu.make_async_copy
+
+    def weights(c):
         place = lax.rem(c + (chunks // 2) * (1 - noisy), chunks) * FC
         place = pl.multiple_of(place, FC)
         return (
-            pltpu.make_async_copy(w1_any.at[:, pl.ds(place, FC)], w1.at[c], sem_1.at[c]),
-            pltpu.make_async_copy(w2_any.at[pl.ds(place, FC), :], w2.at[c], sem_2.at[c]),
+            copy(w1_any.at[:, pl.ds(place, FC)], w1.at[c], sem_1.at[c]),
+            copy(w2_any.at[pl.ds(place, FC), :], w2.at[c], sem_2.at[c]),
         )
 
-    copies = (
-        pltpu.make_async_copy(wo_any, wo, sem_a.at[0]),
-        pltpu.make_async_copy(dy_any, dy, sem_a.at[1]),
-    )
-
-    @pl.when(step == 0)
-    def _():
-        for copy in copies:
-            copy.start()
-        for c in range(chunks):
-            for copy in fetch(c):
-                copy.start()
-        sums[...] = jnp.zeros_like(sums)
-        acc[...] = jnp.zeros_like(acc)
-
-    @pl.when(step < at_attend)
-    def _():
-        rows = pl.ds(pl.multiple_of(step * R, R), R)
-        value = jnp.where(noisy == 1, received[...].astype(f32), x[...].astype(f32))
+    sources = (
+        (x_any, x),
+        (received_any, received),
+        (wqkv_any.at[:, pl.ds(width, 2 * width)], wkv),
+        (cosine_any, cosine),
+        (signed_any, signed),
+        (q_any, q),
+        (ko_any, ko),
+        (vo_any, vo),
+        (wo_any, wo),
+        (dy_any, dy),
+    )
+    loads = [copy(a, b, sem_in.at[i]) for i, (a, b) in enumerate(sources)]
+    for load in loads[:5]:
+        load.start()
+    sums[...] = jnp.zeros_like(sums)
+
+    for load in loads[:5]:
+        load.wait()
+    for load in loads[5:]:
+        load.start()
+
+    def clean_rows(t, carry):
+        rows = pl.ds(pl.multiple_of(t * R, R), R)
+        value = jnp.where(noisy == 1, received[rows, :].astype(f32), x[rows, :].astype(f32))
         h1 = (value * inv_rms(value) * gain1[...]).astype(bf16)
-        k = rotated(nn(h1, wk[...]), cosine[...], signed[...], 1.0).astype(bf16)
-        v = nn(h1, wv[...]).astype(bf16)
-        kc_out[...] = k
-        vc_out[...] = v
-        for p in range(pairs):
-            kc[p, rows, :] = k[:, p * PW : (p + 1) * PW]
-            vc[p, rows, :] = v[:, p * PW : (p + 1) * PW]
-
-    @pl.when(jnp.logical_and(step >= at_attend, step < at_join))
-    def _():
-        p = step - at_attend
+        kv = nn(h1, wkv[...])
+        by_pairs(kc, rows, rotated(kv[:, :width], cosine[rows, :], signed[rows, :], 1.0))
+        by_pairs(vc, rows, kv[:, width:])
+        return carry
+
+    lax.fori_loop(0, tiles, clean_rows, 0)
+    stores = [copy(kc, kc_out, sem_out.at[0]), copy(vc, vc_out, sem_out.at[1])]
+    for store in stores:
+        store.start()
+
+    edge_bias(bias, noisy)
+    for load in loads[5:8]:
+        load.wait()
+    for c in range(chunks):
+        for load in weights(c):
+            load.start()
+
+    def one_pair(p, carry):
         lanes = pl.ds(pl.multiple_of(p * PW, PW), PW)
 
-        def store(at, tile_t):
+        def keep(at, tile_t):
             o_t[lanes, at] = tile_t.astype(bf16)
-            tile = tile_t.T.astype(bf16)
-            o[at, lanes] = tile
-            o_out[at, :] = tile
-
-        attend_pair(noisy, length, q, ko, vo, kc.at[p], vc.at[p], store, lse, vo_t, vc_t, scores)
-
-    @pl.when(step == at_join)
-    def _():
-        for copy in copies:
-            copy.wait()
-
-    @pl.when(jnp.logical_and(step >= at_join, step < at_feed))
-    def _():
-        start = pl.multiple_of((step - at_join) * R, R)
+            o[at, lanes] = tile_t.T.astype(bf16)
+
+        heads = (ref.at[p] for ref in (q, ko, vo, kc, vc))
+        attend_pair(length, *heads, keep, lse.at[pl.ds(p, 1)], vo_t, vc_t, scores, bias)
+        return carry
+
+    lax.fori_loop(0, pairs, one_pair, 0)
+    more = [copy(o, o_out, sem_out.at[2]), copy(lse, lse_out, sem_out.at[3])]
+    for store in more:
+        store.start()
+    stores += more
+
+    for load in loads[8:]:
+        load.wait()
+
+    def joined_rows(t, carry):
+        start = pl.multiple_of(t * R, R)
         rows = pl.ds(start, R)
         branch = nn(o[rows, :], wo[...])
-        value = x[...].astype(f32) + branch
+        value = x[rows, :].astype(f32) + branch
         x2[rows, :] = value
         h2[rows, :] = (value * inv_rms(value) * gain2[...]).astype(bf16)
         m[rows, :] = jnp.zeros_like(value)
         dh[rows, :] = jnp.zeros_like(value)
         weight = token_weight(start, length, R)
         sums[0:1, :] += row_sum(jnp.where(weight, branch * branch, 0.0))
-
-    @pl.when(jnp.logical_and(step >= at_feed, step < at_middle))
-    def _():
-        c = step - at_feed
-        for copy in fetch(c):
-            copy.wait()
+        return carry
+
+    lax.fori_loop(0, tiles, joined_rows, 0)
+
+    def grad_stores(c, up, down):
+        slot = lax.rem(c, 2)
+        rows = pl.ds(pl.multiple_of(lax.rem(c, chunks // 2) * FC, FC), FC)
+        return (
+            copy(up_grad.at[slot], up.at[rows, :], sem_up.at[slot]),
+            copy(down_grad.at[slot], down.at[rows, :], sem_down.at[slot]),
+        )
+
+    def one_chunk(c, carry):
+        for load in weights(c):
+            load.wait()
         up, down = w1.at[c], w2.at[c]
         for t in range(0, seq, R):
             rows = pl.ds(t, R)
@@ -370,93 +448,115 @@
             du[rows, :] = back
             m[rows, :] += nn(low, down[...])
             dh[rows, :] += nt(back, up[...])
-        down_grad = tn(act[...], dy[...]).astype(bf16)
-        up_grad = tn(du[...], h2[...]).astype(bf16)
+
+        @pl.when(c >= 2)
+        def _():
+            for store in grad_stores(c, up_send, down_send):
+                store.wait()
+
+        slot = lax.rem(c, 2)
+        down_grad[slot] = tn(act[...], dy[...]).astype(bf16)
+        up_grad[slot] = tn(du[...], h2[...]).astype(bf16)
 
         @pl.when(c < chunks // 2)
         def _():
-            down_send[...] = down_grad
-            up_send[...] = up_grad
+            for store in grad_stores(c, up_send, down_send):
+                store.start()
 
         @pl.when(c >= chunks // 2)
         def _():
-            down_keep[...] = down_grad
-            up_keep[...] = up_grad
-
-    @pl.when(step >= at_middle)
-    def _():
-        start = pl.multiple_of((step - at_middle) * R, R)
+            for store in grad_stores(c, up_keep, down_keep):
+                store.start()
+
+        return carry
+
+    lax.fori_loop(0, chunks, one_chunk, 0)
+
+    def tile_stores(t):
+        rows = pl.ds(pl.multiple_of(t * R, R), R)
+        return (
+            copy(h2.at[rows, :], out_any.at[rows, :], sem_tile.at[t, 0]),
+            copy(x2.at[rows, :], dx2_any.at[rows, :], sem_tile.at[t, 1]),
+            copy(received.at[rows, :], do_any.at[rows, :], sem_tile.at[t, 2]),
+        )
+
+    def middle_rows(t, carry):
+        start = pl.multiple_of(t * R, R)
         rows = pl.ds(start, R)
         value = x2[rows, :]
         mixed = m[rows, :]
-        out[...] = (value + mixed).astype(bf16)
         weight = token_weight(start, length, R)
         sums[1:2, :] += row_sum(jnp.where(weight, mixed * mixed, 0.0))
         grad, gain_terms = norm_back(value, gain2[...], dh[rows, :])
         sums[2:3, :] += row_sum(gain_terms)
         grad = grad + dy[rows, :].astype(f32)
-        dx2[...] = grad
         da = grad.astype(bf16)
-        do[...] = nt(da, wo[...]).astype(bf16)
-        acc[...] += nn(o_t[:, rows], da)
-
-    @pl.when(step == at_middle + tiles - 1)
-    def _():
-        half = acc.shape[0] // 2
-        mine = pl.multiple_of(noisy * half, half)
-        g_keep[...] = acc[pl.ds(mine, half), :].astype(bf16)
-        g_send[...] = acc[pl.ds(half - mine, half), :].astype(bf16)
+        h2[rows, :] = (value + mixed).astype(bf16)
+        x2[rows, :] = grad
+        received[rows, :] = nt(da, wo[...]).astype(bf16)
+        x[rows, :] = da
+        for store in tile_stores(t):
+            store.start()
+        return carry
+
+    lax.fori_loop(0, tiles, middle_rows, 0)
+    half = width // 2
+    mine = pl.multiple_of(noisy * half, half)
+    half_grads[0] = nn(o_t[pl.ds(half - mine, half), :], x[...]).astype(bf16)
+    half_grads[1] = nn(o_t[pl.ds(mine, half), :], x[...]).astype(bf16)
+    more = [copy(half_grads.at[0], g_send, sem_out.at[4]), copy(half_grads.at[1], g_keep, sem_out.at[5])]
+    for store in more:
+        store.start()
+    stores += more
+    for c in range(chunks - 2, chunks):
+        stores += grad_stores(c, up_keep, down_keep)
+    for t in range(tiles):
+        stores += tile_stores(t)
+    for store in stores:
+        store.wait()
 
 
 def layer(info, x, received, gain1, gain2, wqkv, tables, q, ko, vo, wo, dy, w1, w2):
     seq, width = x.shape
     hidden = w1.shape[1]
     tiles, pairs, chunks = seq // R, width // PW, hidden // FC
-    at_join = tiles + pairs
-    at_feed, at_middle = at_join + tiles, at_join + tiles + chunks
-    clip = lambda i, count: jnp.clip(i, 0, count - 1)
-    early = lambda i: (clip(i, tiles), 0)
-    late = lambda i: (clip(i - at_middle, tiles), 0)
-    pair = lambda i: (0, clip(i - tiles, pairs))
-    rows = (R, width)
-    third = lambda c: pl.BlockSpec((width, width), lambda i: (0, c), pipeline_mode=pl.Buffered(1))
-    table = pl.BlockSpec((R, PW), early)
     anywhere = pl.BlockSpec(memory_space=pl.ANY)
-    head = pl.BlockSpec((seq, PW), pair)
-    send = pl.BlockSpec((FC, width), lambda i: (clip(i - at_feed, chunks // 2), 0))
-    keep = pl.BlockSpec((FC, width), lambda i: (clip(i - at_feed - chunks // 2, chunks // 2), 0))
-    half = whole((width // 2, width))
-    both = lambda i: (jnp.where(i < tiles, i, clip(i - at_join, tiles)), 0)
     vmem = pltpu.VMEM
-    return pl.pallas_call(
-        functools.partial(layer_kernel, (tiles, pairs, chunks)),
-        grid=(at_middle + tiles,),
-        in_specs=[SMEM, pl.BlockSpec(rows, both), pl.BlockSpec(rows, early), whole((1, width)), whole((1, width))]
-        + [third(1), third(2), table, table, head, head, head]
-        + [anywhere] * 4,
-        out_specs=[pl.BlockSpec(rows, early)] * 2
-        + [head, pl.BlockSpec((1, seq // T, 2 * T), lambda i: (clip(i - tiles, pairs), 0, 0))]
-        + [pl.BlockSpec(rows, late)] * 3
-        + [send, keep, send, keep, half, half, whole((8, width))],
-        out_shape=[shape((seq, width), bf16)] * 3
-        + [shape((pairs, seq // T, 2 * T), f32)]
+    dma = pltpu.SemaphoreType.DMA
+    heads = (pairs, seq, PW)
+    outs = (
+        [shape(heads, bf16)] * 2
+        + [shape((seq, width), bf16), shape((pairs, seq // T, 2 * T), f32)]
         + [shape((seq, width), bf16), shape((seq, width), f32), shape((seq, width), bf16)]
         + [shape((hidden // 2, width), bf16)] * 4
         + [shape((width // 2, width), bf16)] * 2
-        + [shape((8, width), f32)],
-        scratch_shapes=[vmem((pairs, seq, PW), bf16)] * 2
+        + [shape((8, width), f32)]
+    )
+    return pl.pallas_call(
+        layer_kernel,
+        in_specs=[SMEM, IN_VMEM, IN_VMEM] + [anywhere] * 12,
+        out_specs=[anywhere] * 13 + [IN_VMEM],
+        out_shape=outs,
+        scratch_shapes=[vmem((seq, width), bf16)] * 2
+        + [vmem((width, 2 * width), bf16), vmem((seq, PW), f32), vmem((seq, PW), f32)]
+        + [vmem(heads, bf16)] * 3
+        + [vmem((width, width), bf16), vmem((seq, width), bf16)]
+        + [vmem((chunks, width, FC), bf16), vmem((chunks, FC, width), bf16)]
+        + [vmem(heads, bf16)] * 2
         + [vmem((PW, seq), bf16)] * 2
-        + [vmem((2, seq + T, 2 * T), f32), vmem((seq, width), bf16), vmem((width, seq), bf16)]
+        + [vmem((AHEAD, seq + T, 2 * T), f32), vmem((2 * T, 2 * T), f32)]
+        + [vmem((seq, width), bf16), vmem((width, seq), bf16)]
+        + [vmem((pairs, seq // T, 2 * T), f32)]
         + [vmem((seq, width), f32), vmem((seq, width), bf16)]
         + [vmem((seq, width), f32)] * 2
         + [vmem((seq, FC), bf16)] * 2
-        + [vmem((width, width), f32), vmem((width, width), bf16), vmem((seq, width), bf16)]
-        + [vmem((chunks, width, FC), bf16), vmem((chunks, FC, width), bf16)]
-        + [pltpu.SemaphoreType.DMA((n,)) for n in (2, chunks, chunks)],
+        + [vmem((2, FC, width), bf16)] * 2
+        + [vmem((2, width // 2, width), bf16)]
+        + [dma((10,)), dma((chunks,)), dma((chunks,)), dma((6,)), dma((2,)), dma((2,)), dma((tiles, 3))],
         compiler_params=params(BIG),
         cost_estimate=LONG,
         name="layer",
-    )(info, *pinned(x, received), gain1, gain2, *pinned(wqkv, wqkv, *tables, q, ko, vo, wo, dy, w1, w2))
+    )(info, gain1, gain2, *pinned(x, received, wqkv, *tables, q, ko, vo, wo, dy, w1, w2))
 
 
 def weigh_kernel(info, dq, keep, got, cosine, signed, h1t, dkv, g_send, g_keep):
@@ -588,9 +688,6 @@
     return outs[0::2], outs[1::2]
 
 
-IN_VMEM = pl.BlockSpec(memory_space=pltpu.VMEM)
-
-
 def step_kernel(*refs):
     half = refs[0].shape[0] // 2
     kept, got = refs[:GROUPS], refs[GROUPS : 2 * GROUPS]

time: 255 us -> 232 us (0.910)
  Pallas kernels: 160 us -> 136 us
    pallas_call x3, Pallas kernels: 118 us -> 94.3 us  [the longest x1 66.5 us: layer(): pl.pallas_call(layer_kernel, in_specs=[SMEM, IN_VMEM, IN_VMEM] + [anywher...]
  transfers between devices with their start and end apart: 37 -> 37, of which waited for: 9 -> 12; matrix products, arithmetic and copies ran while one was open for 3% -> 3% of each run, Pallas kernels for 30% -> 28%
where the time goes in v2:
time: 232 us; the launch traced here: 231 us
  Pallas kernels  136 us (59%)
  starting transfers between devices  42.1 us (18%)
  waiting for transfers between devices  30.2 us (13%)
  local copies, waits for them, and re-layouts  19.7 us (8%)
    pallas_call x1, Pallas kernels, layer(): pl.pallas_call(layer_kernel, in_specs=[SMEM, IN_VMEM, IN_VMEM] + [anywher...  66.5 us
    ppermute x34, starting transfers between devices, exchange(): return lax.ppermute(value, axis, [(i, i ^ bit) for i in range(size)])  36.8 us
    ppermute x34, waiting for transfers between devices, exchange(): return lax.ppermute(value, axis, [(i, i ^ bit) for i in range(size)])  30.2 us
    pallas_call x2, Pallas kernels, attend_back(): pl.pallas_call(attend_back_kernel, grid=(pairs,), in_specs=[SMEM] + [head...  27.9 us
    pallas_call x2, Pallas kernels, weigh(): pl.pallas_call(weigh_kernel, grid=(width // PW,), in_specs=[SMEM, pl.Bloc...  12.8 us
    unnamed x65, local copies, waits for them, and re-layouts  12.3 us
    pallas_call x1, Pallas kernels, project(): pl.pallas_call(project_kernel, grid=(seq // R,), in_specs=[SMEM, rows, wh...  9.54 us
    pallas_call x1, Pallas kernels, finish(): pl.pallas_call(functools.partial(finish_kernel, len(dqs)), grid=(seq // R...  9.35 us
  transfers between devices with their start and end apart: 37, of which 12 were waited for; matrix products, arithmetic and copies ran while one was open for 3% of the time, Pallas kernels for 28%

profile of v2, /device:TPU:0, one launch (start us, length us, event | category | flops | bytes accessed | tf_op | source)
XLA Modules:
  0.0 231.4 jit_solution(3996544803363597398)
XLA Ops:
  0.6 2.5 %collective-permute-start = (bf16[1024,768]{1,0:T(8,128)(2,1)}, bf16[1024,768]{1,0:T(8,128)(2,1)S(1)}, u32[]{:S(2)}, u32[]{:S(2)}) collective-permute-start(bf16[1024,768]{1,0:T(8,128)(2,1)} %bitcast.29), channel_id=1, source_target_pairs={{0,16},{1,17},{2,18},{3,19},{4,20},{5,21},{6,22},{7,23},{8,24},{9,... | collective-permute-start | bytes 4718600 | tf_op jit(solution)/shard_map/ppermute | solution.py:805
  5.6 9.5 %project.1 = (bf16[6,1024,128]{2,1,0:T(8,128)(2,1)}, bf16[6,1024,128]{2,1,0:T(8,128)(2,1)}, bf16[6,1024,128]{2,1,0:T(8,128)(2,1)}, bf16[768,1024]{1,0:T(8,128)(2,1)}, f32[8,768]{1,0:T(8,128)}) custom-call(s32[2]{0:T(128)} %pad_add_fusion.info, bf16[1024,768]{1,0:T(8,128)(2,1)} %bitcast.30, f32[1,768]{1,0:T(1,128)} %reshape.60.gain.gain1, ...), custom_call_target="tpu_custom_call" | custom-call | flops 34359738368 | bytes 67108864 | tf_op jit(solution)/shard_map/project/pallas_call | solution.py:127
  18.2 66.5 %layer.1 = (bf16[6,1024,128]{2,1,0:T(8,128)(2,1)}, bf16[6,1024,128]{2,1,0:T(8,128)(2,1)}, bf16[1024,768]{1,0:T(8,128)(2,1)}, f32[6,8,256]{2,1,0:T(8,128)}, bf16[...) custom-call(s32[2]{0:T(128)} %pad_add_fusion.info, ...), custom_call_target="tpu_custom_call" | custom-call | flops 34359738368 | bytes 67108864 | tf_op jit(solution)/shard_map/layer/pallas_call | solution.py:535
  86.2 14.0 %attend_back.2 = (bf16[1024,384]{1,0:T(8,128)(2,1)S(1)}, bf16[2,1024,384]{2,1,0:T(8,128)(2,1)S(1)}, bf16[2,1024,384]{2,1,0:T(8,128)(2,1)S(1)}) custom-call(s32[2]{0:T(128)S(1)} %copy-done.18, bf16[6,1024,128]{2,1,0:T(8,128)(2,1)} %get-tuple-element.116.q_any.q, bf16[6,1024,128]{2,1,0:T(8,128)(2,1)} %get-tuple-element.117.ko_any.ko, ...), custom_call_target="tpu_custom_call" | custom-call | flops 34359738368 | bytes 67108864 | tf_op jit(solution)/shard_map/attend_back/pallas_call | solution.py:307
  103.6 3.9 %start_sum.2 = (bf16[8,72,768]{2,1,0:T(8,128)(2,1)S(1)}, bf16[8,72,768]{2,1,0:T(8,128)(2,1)S(1)}, bf16[8,72,768]{2,1,0:T(8,128)(2,1)S(1)}, bf16[8,72,768]{2,1,0:...) custom-call(s32[1]{0:T(128)} %bitcast.4.me, bf16[48,32,768]{2,1,0:T(8,128)(2,1)S(1)} %bitcast.19, ...), custom_call_target="tpu_custom_call" | custom-call | flops 1048576 | bytes 65536 | tf_op jit(solution)/shard_map/start_sum/pallas_call | solution.py:678
  107.5 2.4 %collective-permute-start.4 = (bf16[8,72,768]{2,1,0:T(8,128)(2,1)S(1)}, bf16[8,72,768]{2,1,0:T(8,128)(2,1)S(1)}, u32[]{:S(2)}, u32[]{:S(2)}) collective-permute-start(bf16[8,72,768]{2,1,0:T(8,128)(2,1)S(1)} %get-tuple-element.138), channel_id=1, source_target_pairs={{0,1},{1,0},{2,3},{3,2},{4,5},{5,4},{6,7},{7,6},{8,9},{9,8},{10,11... | collective-permute-start | bytes 2654216 | tf_op jit(solution)/shard_map/ppermute | solution.py:638
  109.9 1.5 collective-permute-start.5
  111.4 1.6 collective-permute-start.6
  113.0 13.9 %attend_back.3 = (bf16[1024,384]{1,0:T(8,128)(2,1)S(1)}, bf16[2,1024,384]{2,1,0:T(8,128)(2,1)S(1)}, bf16[2,1024,384]{2,1,0:T(8,128)(2,1)S(1)}) custom-call(s32[2]{0:T(128)S(1)} %copy-done.18, bf16[6,1024,128]{2,1,0:T(8,128)(2,1)} %get-tuple-element.116.q_any.q, bf16[6,1024,128]{2,1,0:T(8,128)(2,1)} %get-tuple-element.117.ko_any.ko, ...), custom_call_target="tpu_custom_call" | custom-call | flops 34359738368 | bytes 67108864 | tf_op jit(solution)/shard_map/attend_back/pallas_call | solution.py:307
  129.0 1.5 collective-permute-start.8
  130.5 2.0 collective-permute-done.5.refs_4_
  135.2 1.7 collective-permute-start.11
  136.9 6.4 %weigh.2 = (bf16[2,1024,384]{2,1,0:T(8,128)(2,1)S(1)}, bf16[3,384,384]{2,1,0:T(8,128)(2,1)}, bf16[3,384,384]{2,1,0:T(8,128)(2,1)S(1)}) custom-call(s32[2]{0:T(128)S(1)} %copy-done.18, bf16[1024,384]{1,0:T(8,128)(2,1)} %copy-done.23, bf16[2,1024,384]{2,1,0:T(8,128)(2,1)} %copy-done.21, bf16[2,1024,384]{2,1,0:T(8,128)(2,1)S(1)} %collective-permute-done.7.got, ...), custom_call_target="tpu_custom_call" | custom-call | flops 34359738368 | bytes 67108864 | tf_op jit(solution)/shard_map/weigh/pallas_call | solution.py:584
  144.4 6.4 %weigh.3 = (bf16[2,1024,384]{2,1,0:T(8,128)(2,1)S(1)}, bf16[3,384,384]{2,1,0:T(8,128)(2,1)}, bf16[3,384,384]{2,1,0:T(8,128)(2,1)S(1)}) custom-call(s32[2]{0:T(128)S(1)} %copy-done.18, bf16[1024,384]{1,0:T(8,128)(2,1)} %copy-done.24, bf16[2,1024,384]{2,1,0:T(8,128)(2,1)} %copy-done.22, bf16[2,1024,384]{2,1,0:T(8,128)(2,1)S(1)} %collective-permute-done.8.got, ...), custom_call_target="tpu_custom_call" | custom-call | flops 34359738368 | bytes 67108864 | tf_op jit(solution)/shard_map/weigh/pallas_call | solution.py:584
  150.9 5.1 %collective-permute-done.11.refs_5_ = bf16[4,72,768]{2,1,0:T(8,128)(2,1)S(1)} collective-permute-done((bf16[4,72,768]{2,1,0:T(8,128)(2,1)S(1)}, bf16[4,72,768]{2,1,0:T(8,128)(2,1)S(1)}, u32[]{:S(2)}, u32[]{:S(2)}) %collective-permute-start.11) | collective-permute-done | bytes 442400 | tf_op jit(solution)/shard_map/ppermute | solution.py:638
  160.4 9.4 %finish.1 = (bf16[1024,768]{1,0:T(8,128)(2,1)}, f32[8,768]{1,0:T(8,128)S(1)}) custom-call(bf16[1024,768]{1,0:T(8,128)(2,1)} %bitcast.32, f32[1024,768]{1,0:T(8,128)} %get-tuple-element.166.dx2, bf16[768,2304]{1,0:T(8,128)(2,1)} %wqkv.1, f32[1,768]{1,0:T(1,128)S(1)} %copy-done.9, bf16[1024,384]{1,0:T(8,128)(2,1)} %copy-done.23, bf16[1024,384]{1,0:T(8,128)(2,1)} %copy-done.24, ...), custom_call_target="tpu_custom_call" | custom-call | flops 34359738368 | bytes 67108864 | tf_op jit(solution)/shard_map/finish/pallas_call | solution.py:614
  172.9 3.0 %start_sum.3 = (bf16[8,48,384]{2,1,0:T(8,128)(2,1)S(1)}, bf16[8,48,384]{2,1,0:T(8,128)(2,1)S(1)}, bf16[8,48,384]{2,1,0:T(8,128)(2,1)S(1)}, bf16[8,48,384]{2,1,0:...) custom-call(s32[1]{0:T(128)} %bitcast.4.me, bf16[48,24,384]{2,1,0:T(8,128)(2,1)S(1)} %bitcast.22, ...), custom_call_target="tpu_custom_call" | custom-call | flops 1048576 | bytes 65536 | tf_op jit(solution)/shard_map/start_sum/pallas_call | solution.py:678
  176.0 1.5 collective-permute-start.15
  177.5 1.6 collective-permute-start.16
  180.8 1.5 collective-permute-start.18
  182.3 6.1 %collective-permute-done.18.refs_7_ = f32[8,768]{1,0:T(8,128)S(1)} collective-permute-done((f32[8,768]{1,0:T(8,128)S(1)}, f32[8,768]{1,0:T(8,128)S(1)}, u32[]{:S(2)}, u32[]{:S(2)}) %collective-permute-start.18) | collective-permute-done | bytes 24608 | tf_op jit(solution)/shard_map/ppermute | solution.py:638
  189.8 2.6 %collective-permute-start.33 = (bf16[2,72,768]{2,1,0:T(8,128)(2,1)S(1)}, bf16[2,72,768]{2,1,0:T(8,128)(2,1)S(1)}, u32[]{:S(2)}, u32[]{:S(2)}) collective-permute-start(bf16[2,72,768]{2,1,0:T(8,128)(2,1)S(1)} %copy-done.13), channel_id=1, source_target_pairs={{0,8},{1,9},{2,10},{3,11},{4,12},{5,13},{6,14},{7,15},{8,0},{9,1},... | collective-permute-start | bytes 663560 | tf_op jit(solution)/shard_map/ppermute | solution.py:638
  192.4 1.6 collective-permute-start.31
  195.4 2.4 %collective-permute-done.22.refs_7_ = f32[8,768]{1,0:T(8,128)S(1)} collective-permute-done((f32[8,768]{1,0:T(8,128)S(1)}, f32[8,768]{1,0:T(8,128)S(1)}, u32[]{:S(2)}, u32[]{:S(2)}) %collective-permute-start.22) | collective-permute-done | bytes 24608 | tf_op jit(solution)/shard_map/ppermute | solution.py:638
  199.8 3.1 %collective-permute-done.20.refs_4_ = bf16[4,48,384]{2,1,0:T(8,128)(2,1)S(1)} collective-permute-done((bf16[4,48,384]{2,1,0:T(8,128)(2,1)S(1)}, bf16[4,48,384]{2,1,0:T(8,128)(2,1)S(1)}, u32[]{:S(2)}, u32[]{:S(2)}) %collective-permute-start.20) | collective-permute-done | bytes 147488 | tf_op jit(solution)/shard_map/ppermute | solution.py:638
  202.9 1.6 collective-permute-done.21.refs_5_
  205.9 3.8 %collective-permute-start.34 = (bf16[1,72,768]{2,1,0:T(8,128)(2,1)S(1)}, bf16[1,72,768]{2,1,0:T(8,128)(2,1)S(1)}, u32[]{:S(2)}, u32[]{:S(2)}) collective-permute-start(bf16[1,72,768]{2,1,0:T(8,128)(2,1)S(1)} %get-tuple-element.216), channel_id=1, source_target_pairs={{0,8},{1,9},{2,10},{3,11},{4,12},{5,13},{6,14},{7,15},{8,0},{9,1},... | collective-permute-start | bytes 331784 | tf_op jit(solution)/shard_map/ppermute | solution.py:638
  209.9 1.9 collective-permute-start.24
  211.8 1.9 collective-permute-done.26.refs_7_
  216.1 2.9 %collective-permute-done.25.refs_5_ = bf16[2,48,384]{2,1,0:T(8,128)(2,1)S(1)} collective-permute-done((bf16[2,48,384]{2,1,0:T(8,128)(2,1)S(1)}, bf16[2,48,384]{2,1,0:T(8,128)(2,1)S(1)}, u32[]{:S(2)}, u32[]{:S(2)}) %collective-permute-start.25) | collective-permute-done | bytes 73760 | tf_op jit(solution)/shard_map/ppermute | solution.py:638
  220.1 1.9 collective-permute-start.28
  226.2 2.0 collective-permute-done.30.refs_7_
  (138 shorter events, 41.6 us)
Async XLA Ops:
  0.6 16.4 %collective-permute-start = (bf16[1024,768]{1,0:T(8,128)(2,1)}, bf16[1024,768]{1,0:T(8,128)(2,1)S(1)}, u32[]{:S(2)}, u32[]{:S(2)}) collective-permute-start(bf16[1024,768]{1,0:T(8,128)(2,1)} %bitcast.29), channel_id=1, source_target_pairs={{0,16},{1,17},{2,18},{3,19},{4,20},{5,21},{6,22},{7,23},{8,24},{9,... | collective-permute-start | bytes 4718600 | tf_op jit(solution)/shard_map/ppermute | solution.py:805
  84.7 18.8 %collective-permute-start.3 = (bf16[384,768]{1,0:T(8,128)(2,1)}, bf16[384,768]{1,0:T(8,128)(2,1)S(1)}, u32[]{:S(2)}, u32[]{:S(2)}) collective-permute-start(bf16[384,768]{1,0:T(8,128)(2,1)} %get-tuple-element.134), channel_id=1, source_target_pairs={{0,16},{16,0},{1,17},{17,1},{2,18},{18,2},{3,19},{19,3},{4,20},{20... | collective-permute-start | bytes 1769480 | tf_op jit(solution)/shard_map/ppermute | solution.py:638
  84.8 18.8 %collective-permute-start.1 = (bf16[1536,768]{1,0:T(8,128)(2,1)}, bf16[1536,768]{1,0:T(8,128)(2,1)S(1)}, u32[]{:S(2)}, u32[]{:S(2)}) collective-permute-start(bf16[1536,768]{1,0:T(8,128)(2,1)} %get-tuple-element.128), channel_id=1, source_target_pairs={{0,16},{16,0},{1,17},{17,1},{2,18},{18,2},{3,19},{19,3},{4,20},{20... | collective-permute-start | bytes 7077896 | tf_op jit(solution)/shard_map/ppermute | solution.py:638
  85.3 18.3 %collective-permute-start.2 = (bf16[1536,768]{1,0:T(8,128)(2,1)}, bf16[1536,768]{1,0:T(8,128)(2,1)S(1)}, u32[]{:S(2)}, u32[]{:S(2)}) collective-permute-start(bf16[1536,768]{1,0:T(8,128)(2,1)} %get-tuple-element.131), channel_id=1, source_target_pairs={{0,16},{16,0},{1,17},{17,1},{2,18},{18,2},{3,19},{19,3},{4,20},{20... | collective-permute-start | bytes 7077896 | tf_op jit(solution)/shard_map/ppermute | solution.py:638
  102.2 34.6 %collective-permute-start.7 = (bf16[2,1024,384]{2,1,0:T(8,128)(2,1)S(1)}, bf16[2,1024,384]{2,1,0:T(8,128)(2,1)S(1)}, u32[]{:S(2)}, u32[]{:S(2)}) collective-permute-start(bf16[2,1024,384]{2,1,0:T(8,128)(2,1)S(1)} %get-tuple-element.153), channel_id=1, source_target_pairs={{16,0},{17,1},{18,2},{19,3},{20,4},{21,5},{22,6},{23,7},{24,8},{25... | collective-permute-start | bytes 4718600 | tf_op jit(solution)/shard_map/ppermute | solution.py:821
  107.5 26.1 %collective-permute-start.4 = (bf16[8,72,768]{2,1,0:T(8,128)(2,1)S(1)}, bf16[8,72,768]{2,1,0:T(8,128)(2,1)S(1)}, u32[]{:S(2)}, u32[]{:S(2)}) collective-permute-start(bf16[8,72,768]{2,1,0:T(8,128)(2,1)S(1)} %get-tuple-element.138), channel_id=1, source_target_pairs={{0,1},{1,0},{2,3},{3,2},{4,5},{5,4},{6,7},{7,6},{8,9},{9,8},{10,11... | collective-permute-start | bytes 2654216 | tf_op jit(solution)/shard_map/ppermute | solution.py:638
  109.9 22.5 %collective-permute-start.5 = (bf16[8,72,768]{2,1,0:T(8,128)(2,1)S(1)}, bf16[8,72,768]{2,1,0:T(8,128)(2,1)S(1)}, u32[]{:S(2)}, u32[]{:S(2)}) collective-permute-start(bf16[8,72,768]{2,1,0:T(8,128)(2,1)S(1)} %get-tuple-element.144), channel_id=1, source_target_pairs={{0,2},{1,3},{2,0},{3,1},{4,6},{5,7},{6,4},{7,5},{8,10},{9,11},{10,... | collective-permute-start | bytes 2654216 | tf_op jit(solution)/shard_map/ppermute | solution.py:638
  111.4 22.2 %collective-permute-start.6 = (bf16[8,72,768]{2,1,0:T(8,128)(2,1)S(1)}, bf16[8,72,768]{2,1,0:T(8,128)(2,1)S(1)}, u32[]{:S(2)}, u32[]{:S(2)}) collective-permute-start(bf16[8,72,768]{2,1,0:T(8,128)(2,1)S(1)} %get-tuple-element.145), channel_id=1, source_target_pairs={{0,4},{1,5},{2,6},{3,7},{4,0},{5,1},{6,2},{7,3},{8,12},{9,13},{10,... | collective-permute-start | bytes 2654216 | tf_op jit(solution)/shard_map/ppermute | solution.py:638
  129.0 15.5 %collective-permute-start.8 = (bf16[2,1024,384]{2,1,0:T(8,128)(2,1)S(1)}, bf16[2,1024,384]{2,1,0:T(8,128)(2,1)S(1)}, u32[]{:S(2)}, u32[]{:S(2)}) collective-permute-start(bf16[2,1024,384]{2,1,0:T(8,128)(2,1)S(1)} %get-tuple-element.157), channel_id=1, source_target_pairs={{16,0},{17,1},{18,2},{19,3},{20,4},{21,5},{22,6},{23,7},{24,8},{25... | collective-permute-start | bytes 4718600 | tf_op jit(solution)/shard_map/ppermute | solution.py:831
  134.3 21.7 %collective-permute-start.9 = (bf16[4,72,768]{2,1,0:T(8,128)(2,1)S(1)}, bf16[4,72,768]{2,1,0:T(8,128)(2,1)S(1)}, u32[]{:S(2)}, u32[]{:S(2)}) collective-permute-start(bf16[4,72,768]{2,1,0:T(8,128)(2,1)S(1)} %get-tuple-element.151), channel_id=1, source_target_pairs={{0,2},{1,3},{2,0},{3,1},{4,6},{5,7},{6,4},{7,5},{8,10},{9,11},{10,... | collective-permute-start | bytes 1327112 | tf_op jit(solution)/shard_map/ppermute | solution.py:638
  134.8 16.0 %collective-permute-start.10 = (bf16[4,72,768]{2,1,0:T(8,128)(2,1)S(1)}, bf16[4,72,768]{2,1,0:T(8,128)(2,1)S(1)}, u32[]{:S(2)}, u32[]{:S(2)}) collective-permute-start(bf16[4,72,768]{2,1,0:T(8,128)(2,1)S(1)} %get-tuple-element.162), channel_id=1, source_target_pairs={{0,1},{1,0},{2,3},{3,2},{4,5},{5,4},{6,7},{7,6},{8,9},{9,8},{10,11... | collective-permute-start | bytes 1327112 | tf_op jit(solution)/shard_map/ppermute | solution.py:638
  135.2 20.8 %collective-permute-start.11 = (bf16[4,72,768]{2,1,0:T(8,128)(2,1)S(1)}, bf16[4,72,768]{2,1,0:T(8,128)(2,1)S(1)}, u32[]{:S(2)}, u32[]{:S(2)}) collective-permute-start(bf16[4,72,768]{2,1,0:T(8,128)(2,1)S(1)} %get-tuple-element.163), channel_id=1, source_target_pairs={{0,1},{1,0},{2,3},{3,2},{4,5},{5,4},{6,7},{7,6},{8,9},{9,8},{10,11... | collective-permute-start | bytes 1327112 | tf_op jit(solution)/shard_map/ppermute | solution.py:638
  144.4 28.5 %collective-permute-start.12 = (bf16[3,384,384]{2,1,0:T(8,128)(2,1)}, bf16[3,384,384]{2,1,0:T(8,128)(2,1)S(1)}, u32[]{:S(2)}, u32[]{:S(2)}) collective-permute-start(bf16[3,384,384]{2,1,0:T(8,128)(2,1)} %get-tuple-element.173), channel_id=1, source_target_pairs={{0,16},{16,0},{1,17},{17,1},{2,18},{18,2},{3,19},{19,3},{4,20},{20... | collective-permute-start | bytes 2654216 | tf_op jit(solution)/shard_map/ppermute | solution.py:638
  160.4 12.5 %collective-permute-start.13 = (bf16[3,384,384]{2,1,0:T(8,128)(2,1)}, bf16[3,384,384]{2,1,0:T(8,128)(2,1)S(1)}, u32[]{:S(2)}, u32[]{:S(2)}) collective-permute-start(bf16[3,384,384]{2,1,0:T(8,128)(2,1)} %get-tuple-element.176), channel_id=1, source_target_pairs={{0,16},{16,0},{1,17},{17,1},{2,18},{18,2},{3,19},{19,3},{4,20},{20... | collective-permute-start | bytes 2654216 | tf_op jit(solution)/shard_map/ppermute | solution.py:638
  176.0 12.5 %collective-permute-start.15 = (bf16[8,48,384]{2,1,0:T(8,128)(2,1)S(1)}, bf16[8,48,384]{2,1,0:T(8,128)(2,1)S(1)}, u32[]{:S(2)}, u32[]{:S(2)}) collective-permute-start(bf16[8,48,384]{2,1,0:T(8,128)(2,1)S(1)} %get-tuple-element.181), channel_id=1, source_target_pairs={{0,2},{1,3},{2,0},{3,1},{4,6},{5,7},{6,4},{7,5},{8,10},{9,11},{10,... | collective-permute-start | bytes 884744 | tf_op jit(solution)/shard_map/ppermute | solution.py:638
  177.5 11.0 %collective-permute-start.16 = (bf16[8,48,384]{2,1,0:T(8,128)(2,1)S(1)}, bf16[8,48,384]{2,1,0:T(8,128)(2,1)S(1)}, u32[]{:S(2)}, u32[]{:S(2)}) collective-permute-start(bf16[8,48,384]{2,1,0:T(8,128)(2,1)S(1)} %get-tuple-element.182), channel_id=1, source_target_pairs={{0,4},{1,5},{2,6},{3,7},{4,0},{5,1},{6,2},{7,3},{8,12},{9,13},{10,... | collective-permute-start | bytes 884744 | tf_op jit(solution)/shard_map/ppermute | solution.py:638
  179.1 9.4 %collective-permute-start.14 = (bf16[8,48,384]{2,1,0:T(8,128)(2,1)S(1)}, bf16[8,48,384]{2,1,0:T(8,128)(2,1)S(1)}, u32[]{:S(2)}, u32[]{:S(2)}) collective-permute-start(bf16[8,48,384]{2,1,0:T(8,128)(2,1)S(1)} %get-tuple-element.180), channel_id=1, source_target_pairs={{0,1},{1,0},{2,3},{3,2},{4,5},{5,4},{6,7},{7,6},{8,9},{9,8},{10,11... | collective-permute-start | bytes 884744 | tf_op jit(solution)/shard_map/ppermute | solution.py:638
  180.8 7.6 %collective-permute-start.18 = (f32[8,768]{1,0:T(8,128)S(1)}, f32[8,768]{1,0:T(8,128)S(1)}, u32[]{:S(2)}, u32[]{:S(2)}) collective-permute-start(f32[8,768]{1,0:T(8,128)S(1)} %add.3.refs_6_), channel_id=1, source_target_pairs={{0,1},{1,0},{2,3},{3,2},{4,5},{5,4},{6,7},{7,6},{8,9},{9,8},{10,11... | collective-permute-start | bytes 73736 | tf_op jit(solution)/shard_map/ppermute | solution.py:638
  188.7 9.6 %collective-permute-start.19 = (bf16[4,48,384]{2,1,0:T(8,128)(2,1)S(1)}, bf16[4,48,384]{2,1,0:T(8,128)(2,1)S(1)}, u32[]{:S(2)}, u32[]{:S(2)}) collective-permute-start(bf16[4,48,384]{2,1,0:T(8,128)(2,1)S(1)} %get-tuple-element.186), channel_id=1, source_target_pairs={{0,2},{1,3},{2,0},{3,1},{4,6},{5,7},{6,4},{7,5},{8,10},{9,11},{10,... | collective-permute-start | bytes 442376 | tf_op jit(solution)/shard_map/ppermute | solution.py:638
  189.3 15.8 %collective-permute-start.32 = (bf16[2,72,768]{2,1,0:T(8,128)(2,1)S(1)}, bf16[2,72,768]{2,1,0:T(8,128)(2,1)S(1)}, u32[]{:S(2)}, u32[]{:S(2)}) collective-permute-start(bf16[2,72,768]{2,1,0:T(8,128)(2,1)S(1)} %copy-done.15), channel_id=1, source_target_pairs={{0,4},{1,5},{2,6},{3,7},{4,0},{5,1},{6,2},{7,3},{8,12},{9,13},{10,... | collective-permute-start | bytes 663560 | tf_op jit(solution)/shard_map/ppermute | solution.py:638
  189.8 15.4 %collective-permute-start.33 = (bf16[2,72,768]{2,1,0:T(8,128)(2,1)S(1)}, bf16[2,72,768]{2,1,0:T(8,128)(2,1)S(1)}, u32[]{:S(2)}, u32[]{:S(2)}) collective-permute-start(bf16[2,72,768]{2,1,0:T(8,128)(2,1)S(1)} %copy-done.13), channel_id=1, source_target_pairs={{0,8},{1,9},{2,10},{3,11},{4,12},{5,13},{6,14},{7,15},{8,0},{9,1},... | collective-permute-start | bytes 663560 | tf_op jit(solution)/shard_map/ppermute | solution.py:638
  192.4 13.3 %collective-permute-start.31 = (bf16[2,72,768]{2,1,0:T(8,128)(2,1)S(1)}, bf16[2,72,768]{2,1,0:T(8,128)(2,1)S(1)}, u32[]{:S(2)}, u32[]{:S(2)}) collective-permute-start(bf16[2,72,768]{2,1,0:T(8,128)(2,1)S(1)} %copy-done.11), channel_id=1, source_target_pairs={{0,4},{1,5},{2,6},{3,7},{4,0},{5,1},{6,2},{7,3},{8,12},{9,13},{10,... | collective-permute-start | bytes 663560 | tf_op jit(solution)/shard_map/ppermute | solution.py:638
  198.3 6.2 %collective-permute-start.21 = (bf16[4,48,384]{2,1,0:T(8,128)(2,1)S(1)}, bf16[4,48,384]{2,1,0:T(8,128)(2,1)S(1)}, u32[]{:S(2)}, u32[]{:S(2)}) collective-permute-start(bf16[4,48,384]{2,1,0:T(8,128)(2,1)S(1)} %get-tuple-element.188), channel_id=1, source_target_pairs={{0,1},{1,0},{2,3},{3,2},{4,5},{5,4},{6,7},{7,6},{8,9},{9,8},{10,11... | collective-permute-start | bytes 442376 | tf_op jit(solution)/shard_map/ppermute | solution.py:638
  204.6 10.0 %collective-permute-start.23 = (bf16[2,48,384]{2,1,0:T(8,128)(2,1)S(1)}, bf16[2,48,384]{2,1,0:T(8,128)(2,1)S(1)}, u32[]{:S(2)}, u32[]{:S(2)}) collective-permute-start(bf16[2,48,384]{2,1,0:T(8,128)(2,1)S(1)} %get-tuple-element.193), channel_id=1, source_target_pairs={{0,4},{1,5},{2,6},{3,7},{4,0},{5,1},{6,2},{7,3},{8,12},{9,13},{10,... | collective-permute-start | bytes 221192 | tf_op jit(solution)/shard_map/ppermute | solution.py:638
  205.9 16.2 %collective-permute-start.34 = (bf16[1,72,768]{2,1,0:T(8,128)(2,1)S(1)}, bf16[1,72,768]{2,1,0:T(8,128)(2,1)S(1)}, u32[]{:S(2)}, u32[]{:S(2)}) collective-permute-start(bf16[1,72,768]{2,1,0:T(8,128)(2,1)S(1)} %get-tuple-element.216), channel_id=1, source_target_pairs={{0,8},{1,9},{2,10},{3,11},{4,12},{5,13},{6,14},{7,15},{8,0},{9,1},... | collective-permute-start | bytes 331784 | tf_op jit(solution)/shard_map/ppermute | solution.py:638
  209.7 13.8 %collective-permute-start.35 = (bf16[1,72,768]{2,1,0:T(8,128)(2,1)S(1)}, bf16[1,72,768]{2,1,0:T(8,128)(2,1)S(1)}, u32[]{:S(2)}, u32[]{:S(2)}) collective-permute-start(bf16[1,72,768]{2,1,0:T(8,128)(2,1)S(1)} %get-tuple-element.217), channel_id=1, source_target_pairs={{0,8},{1,9},{2,10},{3,11},{4,12},{5,13},{6,14},{7,15},{8,0},{9,1},... | collective-permute-start | bytes 331784 | tf_op jit(solution)/shard_map/ppermute | solution.py:638
  209.9 6.2 %collective-permute-start.24 = (bf16[2,48,384]{2,1,0:T(8,128)(2,1)S(1)}, bf16[2,48,384]{2,1,0:T(8,128)(2,1)S(1)}, u32[]{:S(2)}, u32[]{:S(2)}) collective-permute-start(bf16[2,48,384]{2,1,0:T(8,128)(2,1)S(1)} %get-tuple-element.194), channel_id=1, source_target_pairs={{0,4},{1,5},{2,6},{3,7},{4,0},{5,1},{6,2},{7,3},{8,12},{9,13},{10,... | collective-permute-start | bytes 221192 | tf_op jit(solution)/shard_map/ppermute | solution.py:638
  213.7 5.3 %collective-permute-start.25 = (bf16[2,48,384]{2,1,0:T(8,128)(2,1)S(1)}, bf16[2,48,384]{2,1,0:T(8,128)(2,1)S(1)}, u32[]{:S(2)}, u32[]{:S(2)}) collective-permute-start(bf16[2,48,384]{2,1,0:T(8,128)(2,1)S(1)} %get-tuple-element.195), channel_id=1, source_target_pairs={{0,8},{1,9},{2,10},{3,11},{4,12},{5,13},{6,14},{7,15},{8,0},{9,1},... | collective-permute-start | bytes 221192 | tf_op jit(solution)/shard_map/ppermute | solution.py:638
  214.6 9.9 %collective-permute-start.36 = (bf16[1,72,768]{2,1,0:T(8,128)(2,1)S(1)}, bf16[1,72,768]{2,1,0:T(8,128)(2,1)S(1)}, u32[]{:S(2)}, u32[]{:S(2)}) collective-permute-start(bf16[1,72,768]{2,1,0:T(8,128)(2,1)S(1)} %get-tuple-element.218), channel_id=1, source_target_pairs={{0,2},{1,3},{2,0},{3,1},{4,6},{5,7},{6,4},{7,5},{8,10},{9,11},{10,... | collective-permute-start | bytes 331784 | tf_op jit(solution)/shard_map/ppermute | solution.py:638
  219.1 9.2 %collective-permute-start.27 = (bf16[1,48,384]{2,1,0:T(8,128)(2,1)S(1)}, bf16[1,48,384]{2,1,0:T(8,128)(2,1)S(1)}, u32[]{:S(2)}, u32[]{:S(2)}) collective-permute-start(bf16[1,48,384]{2,1,0:T(8,128)(2,1)S(1)} %get-tuple-element.200), channel_id=1, source_target_pairs={{0,8},{1,9},{2,10},{3,11},{4,12},{5,13},{6,14},{7,15},{8,0},{9,1},... | collective-permute-start | bytes 110600 | tf_op jit(solution)/shard_map/ppermute | solution.py:638
  220.1 8.1 %collective-permute-start.28 = (bf16[1,48,384]{2,1,0:T(8,128)(2,1)S(1)}, bf16[1,48,384]{2,1,0:T(8,128)(2,1)S(1)}, u32[]{:S(2)}, u32[]{:S(2)}) collective-permute-start(bf16[1,48,384]{2,1,0:T(8,128)(2,1)S(1)} %get-tuple-element.201), channel_id=1, source_target_pairs={{0,8},{1,9},{2,10},{3,11},{4,12},{5,13},{6,14},{7,15},{8,0},{9,1},... | collective-permute-start | bytes 110600 | tf_op jit(solution)/shard_map/ppermute | solution.py:638
  222.0 6.2 %collective-permute-start.29 = (bf16[1,48,384]{2,1,0:T(8,128)(2,1)S(1)}, bf16[1,48,384]{2,1,0:T(8,128)(2,1)S(1)}, u32[]{:S(2)}, u32[]{:S(2)}) collective-permute-start(bf16[1,48,384]{2,1,0:T(8,128)(2,1)S(1)} %get-tuple-element.202), channel_id=1, source_target_pairs={{0,2},{1,3},{2,0},{3,1},{4,6},{5,7},{6,4},{7,5},{8,10},{9,11},{10,... | collective-permute-start | bytes 110600 | tf_op jit(solution)/shard_map/ppermute | solution.py:638
  (37 other events, 489.0 us)

commit v3 on v2

--- a/solution.py
+++ b/solution.py
@@ -99,41 +99,6 @@
 def by_pairs(ref, rows, value):
     for p in range(ref.shape[0]):
         ref[p, rows, :] = value[:, p * PW : (p + 1) * PW].astype(ref.dtype)
-
-
-def project_kernel(info, x, gain, wq, wk, wv, cosine, signed, q, k, v, h1t, sums):
-    at = pl.program_id(0)
-
-    @pl.when(at == 0)
-    def _():
-        sums[...] = jnp.zeros_like(sums)
-
-    value = x[...].astype(f32)
-    h1 = (value * inv_rms(value) * gain[...]).astype(bf16)
-    by_pairs(q, slice(None), rotated(nn(h1, wq[...]), cosine[...], signed[...], 1.0))
-    by_pairs(k, slice(None), rotated(nn(h1, wk[...]), cosine[...], signed[...], 1.0))
-    by_pairs(v, slice(None), nn(h1, wv[...]))
-    h1t[...] = h1.T
-    weight = token_weight(at * R, info[1], R)
-    sums[0:1, :] += row_sum(jnp.where(weight, value * value, 0.0))
-
-
-def project(info, x, gain, weight, tables):
-    seq, width = x.shape
-    rows = pl.BlockSpec((R, width), lambda i: (i, 0))
-    table = pl.BlockSpec((R, PW), lambda i: (i, 0))
-    heads = pl.BlockSpec((width // PW, R, PW), lambda i: (0, i, 0))
-    third = lambda c: pl.BlockSpec((width, width), lambda i: (0, c), pipeline_mode=pl.Buffered(1))
-    return pl.pallas_call(
-        project_kernel,
-        grid=(seq // R,),
-        in_specs=[SMEM, rows, whole((1, width)), third(0), third(1), third(2), table, table],
-        out_specs=[heads, heads, heads, pl.BlockSpec((width, R), lambda i: (0, i)), whole((8, width))],
-        out_shape=[shape((width // PW, seq, PW), bf16)] * 3 + [shape((width, seq), bf16), shape((8, width), f32)],
-        compiler_params=params(BIG),
-        cost_estimate=LONG,
-        name="project",
-    )(info, *pinned(x), gain, *pinned(weight, weight, weight, *tables))
 
 
 def stacked(tile, low):
@@ -324,11 +289,11 @@
 
 
 def layer_kernel(
-    info, gain1, gain2, x_any, received_any, wqkv_any, cosine_any, signed_any, q_any, ko_any, vo_any, wo_any,
-    dy_any, w1_any, w2_any,
-    kc_out, vc_out, o_out, lse_out, out_any, dx2_any, do_any,
+    info, gain1_line, gain2_line, received_any, x_any, wqkv_any, cosine_any, signed_any, wo_any, dy_any,
+    w1_any, w2_any,
+    q_out, ko_out, vo_out, kc_out, vc_out, h1t_out, o_out, lse_out, out_any, dx2_any, do_any,
     up_send, up_keep, down_send, down_keep, g_send, g_keep, sums,
-    x, received, wkv, cosine, signed, q, ko, vo, wo, dy, w1, w2,
+    x, received, wqkv, cosine, signed, q, ko, vo, h1t, wo, dy, w1, w2,
     kc, vc, vo_t, vc_t, scores, bias, o, o_t, lse, x2, h2, m, dh, act, du, up_grad, down_grad, half_grads,
     sem_in, sem_1, sem_2, sem_out, sem_up, sem_down, sem_tile,
 ):
@@ -336,6 +301,7 @@
     seq, width = x.shape
     chunks, pairs, tiles = w1.shape[0], kc.shape[0], seq // R
     copy = pltpu.make_async_copy
+    gain1, gain2 = gain1_line[...].reshape(1, width), gain2_line[...].reshape(1, width)
 
     def weights(c):
         place = lax.rem(c + (chunks // 2) * (1 - noisy), chunks) * FC
@@ -347,13 +313,10 @@
 
     sources = (
         (x_any, x),
-        (received_any, received),
-        (wqkv_any.at[:, pl.ds(width, 2 * width)], wkv),
+        (wqkv_any, wqkv),
         (cosine_any, cosine),
         (signed_any, signed),
-        (q_any, q),
-        (ko_any, ko),
-        (vo_any, vo),
+        (received_any, received),
         (wo_any, wo),
         (dy_any, dy),
     )
@@ -361,29 +324,47 @@
     for load in loads[:5]:
         load.start()
     sums[...] = jnp.zeros_like(sums)
-
-    for load in loads[:5]:
+    edge_bias(bias, noisy)
+
+    for load in loads[:4]:
         load.wait()
-    for load in loads[5:]:
-        load.start()
+
+    def own_rows(t, carry):
+        start = pl.multiple_of(t * R, R)
+        rows = pl.ds(start, R)
+        value = x[rows, :].astype(f32)
+        h1 = (value * inv_rms(value) * gain1).astype(bf16)
+        h1t[:, rows] = h1.T
+        tables = (cosine[rows, :], signed[rows, :], 1.0)
+        by_pairs(q, rows, rotated(nn(h1, wqkv[:, :width]), *tables))
+        by_pairs(ko, rows, rotated(nn(h1, wqkv[:, width : 2 * width]), *tables))
+        by_pairs(vo, rows, nn(h1, wqkv[:, 2 * width :]))
+        weight = token_weight(start, length, R)
+        sums[0:1, :] += row_sum(jnp.where(weight, value * value, 0.0))
+        return carry
+
+    lax.fori_loop(0, tiles, own_rows, 0)
+    stores = [copy(a, b, sem_out.at[6 + i]) for i, (a, b) in enumerate(((q, q_out), (ko, ko_out), (vo, vo_out), (h1t, h1t_out)))]
+    for store in stores:
+        store.start()
+    loads[4].wait()
 
     def clean_rows(t, carry):
         rows = pl.ds(pl.multiple_of(t * R, R), R)
         value = jnp.where(noisy == 1, received[rows, :].astype(f32), x[rows, :].astype(f32))
-        h1 = (value * inv_rms(value) * gain1[...]).astype(bf16)
-        kv = nn(h1, wkv[...])
-        by_pairs(kc, rows, rotated(kv[:, :width], cosine[rows, :], signed[rows, :], 1.0))
-        by_pairs(vc, rows, kv[:, width:])
+        h1 = (value * inv_rms(value) * gain1).astype(bf16)
+        by_pairs(kc, rows, rotated(nn(h1, wqkv[:, width : 2 * width]), cosine[rows, :], signed[rows, :], 1.0))
+        by_pairs(vc, rows, nn(h1, wqkv[:, 2 * width :]))
         return carry
 
     lax.fori_loop(0, tiles, clean_rows, 0)
-    stores = [copy(kc, kc_out, sem_out.at[0]), copy(vc, vc_out, sem_out.at[1])]
-    for store in stores:
+    for load in loads[5:]:
+        load.start()
+    more = [copy(kc, kc_out, sem_out.at[0]), copy(vc, vc_out, sem_out.at[1])]
+    for store in more:
         store.start()
-
-    edge_bias(bias, noisy)
-    for load in loads[5:8]:
-        load.wait()
+    stores += more
+
     for c in range(chunks):
         for load in weights(c):
             load.start()
@@ -405,7 +386,7 @@
         store.start()
     stores += more
 
-    for load in loads[8:]:
+    for load in loads[5:]:
         load.wait()
 
     def joined_rows(t, carry):
@@ -414,11 +395,11 @@
         branch = nn(o[rows, :], wo[...])
         value = x[rows, :].astype(f32) + branch
         x2[rows, :] = value
-        h2[rows, :] = (value * inv_rms(value) * gain2[...]).astype(bf16)
+        h2[rows, :] = (value * inv_rms(value) * gain2).astype(bf16)
         m[rows, :] = jnp.zeros_like(value)
         dh[rows, :] = jnp.zeros_like(value)
         weight = token_weight(start, length, R)
-        sums[0:1, :] += row_sum(jnp.where(weight, branch * branch, 0.0))
+        sums[1:2, :] += row_sum(jnp.where(weight, branch * branch, 0.0))
         return carry
 
     lax.fori_loop(0, tiles, joined_rows, 0)
@@ -486,9 +467,9 @@
         value = x2[rows, :]
         mixed = m[rows, :]
         weight = token_weight(start, length, R)
-        sums[1:2, :] += row_sum(jnp.where(weight, mixed * mixed, 0.0))
-        grad, gain_terms = norm_back(value, gain2[...], dh[rows, :])
-        sums[2:3, :] += row_sum(gain_terms)
+        sums[2:3, :] += row_sum(jnp.where(weight, mixed * mixed, 0.0))
+        grad, gain_terms = norm_back(value, gain2, dh[rows, :])
+        sums[3:4, :] += row_sum(gain_terms)
         grad = grad + dy[rows, :].astype(f32)
         da = grad.astype(bf16)
         h2[rows, :] = (value + mixed).astype(bf16)
@@ -516,7 +497,7 @@
         store.wait()
 
 
-def layer(info, x, received, gain1, gain2, wqkv, tables, q, ko, vo, wo, dy, w1, w2):
+def layer(info, gain1, gain2, received, x, wqkv, tables, wo, dy, w1, w2):
     seq, width = x.shape
     hidden = w1.shape[1]
     tiles, pairs, chunks = seq // R, width // PW, hidden // FC
@@ -524,112 +505,124 @@
     vmem = pltpu.VMEM
     dma = pltpu.SemaphoreType.DMA
     heads = (pairs, seq, PW)
+    flat = (seq, width)
     outs = (
-        [shape(heads, bf16)] * 2
-        + [shape((seq, width), bf16), shape((pairs, seq // T, 2 * T), f32)]
-        + [shape((seq, width), bf16), shape((seq, width), f32), shape((seq, width), bf16)]
+        [shape(heads, bf16)] * 5
+        + [shape((width, seq), bf16), shape(flat, bf16), shape((pairs, seq // T, 2 * T), f32)]
+        + [shape(flat, bf16), shape(flat, f32), shape(flat, bf16)]
         + [shape((hidden // 2, width), bf16)] * 4
         + [shape((width // 2, width), bf16)] * 2
         + [shape((8, width), f32)]
     )
     return pl.pallas_call(
         layer_kernel,
-        in_specs=[SMEM, IN_VMEM, IN_VMEM] + [anywhere] * 12,
-        out_specs=[anywhere] * 13 + [IN_VMEM],
+        in_specs=[SMEM, IN_VMEM, IN_VMEM] + [anywhere] * 9,
+        out_specs=[anywhere] * 17 + [IN_VMEM],
         out_shape=outs,
-        scratch_shapes=[vmem((seq, width), bf16)] * 2
-        + [vmem((width, 2 * width), bf16), vmem((seq, PW), f32), vmem((seq, PW), f32)]
+        scratch_shapes=[vmem(flat, bf16)] * 2
+        + [vmem(wqkv.shape, bf16), vmem((seq, PW), f32), vmem((seq, PW), f32)]
         + [vmem(heads, bf16)] * 3
-        + [vmem((width, width), bf16), vmem((seq, width), bf16)]
+        + [vmem((width, seq), bf16), vmem((width, width), bf16), vmem(flat, bf16)]
         + [vmem((chunks, width, FC), bf16), vmem((chunks, FC, width), bf16)]
         + [vmem(heads, bf16)] * 2
         + [vmem((PW, seq), bf16)] * 2
         + [vmem((AHEAD, seq + T, 2 * T), f32), vmem((2 * T, 2 * T), f32)]
-        + [vmem((seq, width), bf16), vmem((width, seq), bf16)]
+        + [vmem(flat, bf16), vmem((width, seq), bf16)]
         + [vmem((pairs, seq // T, 2 * T), f32)]
-        + [vmem((seq, width), f32), vmem((seq, width), bf16)]
-        + [vmem((seq, width), f32)] * 2
+        + [vmem(flat, f32), vmem(flat, bf16)]
+        + [vmem(flat, f32)] * 2
         + [vmem((seq, FC), bf16)] * 2
         + [vmem((2, FC, width), bf16)] * 2
         + [vmem((2, width // 2, width), bf16)]
-        + [dma((10,)), dma((chunks,)), dma((chunks,)), dma((6,)), dma((2,)), dma((2,)), dma((tiles, 3))],
+        + [dma((7,)), dma((chunks,)), dma((chunks,)), dma((10,)), dma((2,)), dma((2,)), dma((tiles, 3))],
         compiler_params=params(BIG),
         cost_estimate=LONG,
         name="layer",
-    )(info, gain1, gain2, *pinned(x, received, wqkv, *tables, q, ko, vo, wo, dy, w1, w2))
-
-
-def weigh_kernel(info, dq, keep, got, cosine, signed, h1t, dkv, g_send, g_keep):
-    half = h1t.shape[0] // 2
+    )(info, gain1, gain2, received, *pinned(x, wqkv, *tables, wo, dy, w1, w2))
+
+
+def weigh_kernel(first, info, dq, keep, got, cosine, signed, h1t, wqkv, sums, dkv, g_send, g_keep, small):
+    width, half = wqkv.shape[0], wqkv.shape[0] // 2
     mine = pl.multiple_of(info[0] * half, half)
     dk = keep[0].astype(f32) + got[0].astype(f32)
-    dk = rotated(dk, cosine[...], signed[...], -1.0).astype(bf16)
-    dv = (keep[1].astype(f32) + got[1].astype(f32)).astype(bf16)
-    dkv[0] = dk
-    dkv[1] = dv
-    grads = jnp.concatenate([dq[...], dk, dv], axis=1)
+    dkv[0] = rotated(dk, cosine[...], signed[...], -1.0).astype(bf16)
+    dkv[1] = (keep[1].astype(f32) + got[1].astype(f32)).astype(bf16)
+    small[...] = sums[...]
     for out, start in ((g_send, half - mine), (g_keep, mine)):
-        total = nn(h1t[pl.ds(start, half), :], grads).astype(bf16)
-        for i in range(3):
-            out[i] = total[:, i * PW : (i + 1) * PW]
-
-
-def weigh(info, piece, got, tables, h1t):
-    dq, keep = piece
+        rows = pl.ds(start, half)
+        terms = 0.0
+        for i, part in enumerate((dq, dkv.at[0], dkv.at[1])):
+            total = nn(h1t[rows, :], part[...])
+            out[i] = total.astype(bf16)
+            at = i * width + first * PW
+            weighted = total * wqkv[rows, at : at + total.shape[1]].astype(f32)
+            for c in range(0, total.shape[1], PW):
+                terms = terms + weighted[:, c : c + PW]
+        line = jnp.sum(terms.T, axis=0, keepdims=True)
+        lanes = lax.broadcasted_iota(jnp.int32, (1, width), 1)
+        inside = jnp.logical_and(lanes >= start, lanes < start + half)
+        small[4:5, :] += jnp.where(inside, jnp.concatenate([line, line], axis=1), 0.0)
+    small[5:6, :] = jnp.full((1, width), info[1].astype(f32))
+
+
+def weigh(info, first, dq, keep, got, tables, h1t, wqkv, sums):
     seq, width = dq.shape
     tall = h1t.shape[0]
-    both = pl.BlockSpec((2, seq, PW), lambda h: (0, 0, h))
-    table = whole((seq, PW))
-    half = pl.BlockSpec((3, tall // 2, PW), lambda h: (0, 0, h))
     return pl.pallas_call(
-        weigh_kernel,
-        grid=(width // PW,),
-        in_specs=[SMEM, pl.BlockSpec((seq, PW), lambda h: (0, h)), both, both, table, table, whole((tall, seq))],
-        out_specs=[both, half, half],
-        out_shape=[shape((2, seq, width), bf16)] + [shape((3, tall // 2, width), bf16)] * 2,
+        functools.partial(weigh_kernel, first),
+        in_specs=[SMEM] + [IN_VMEM] * 8,
+        out_specs=[IN_VMEM] * 4,
+        out_shape=[shape((2, seq, width), bf16)]
+        + [shape((3, tall // 2, width), bf16)] * 2
+        + [shape(sums.shape, f32)],
         compiler_params=params(24),
         cost_estimate=LONG,
         name="weigh",
-    )(info, *pinned(dq, keep), got, *pinned(*tables, h1t))
-
-
-def finish_kernel(parts, x, dx2, wqkv, gain, *refs):
-    dx, sums = refs[-2:]
-
-    @pl.when(pl.program_id(0) == 0)
-    def _():
-        sums[...] = jnp.zeros_like(sums)
-
+    )(info, dq, keep, got, *tables, h1t, wqkv, sums)
+
+
+def finish_kernel(parts, x, dx2, wqkv, gain_line, *refs):
+    dx_any, dx, sem = refs[-3:]
     dqs, dkvs = refs[:parts], refs[parts : 2 * parts]
-    grads = [r[...] for r in dqs] + [r[0] for r in dkvs] + [r[1] for r in dkvs]
-    dh = nt(jnp.concatenate(grads, axis=1), wqkv[...])
-    grad, gain_terms = norm_back(x[...].astype(f32), gain[...], dh)
-    sums[0:1, :] += row_sum(gain_terms)
-    dx[...] = (dx2[...] + grad).astype(bf16)
+    tiles = sem.shape[0]
+    gain = gain_line[...].reshape(1, x.shape[1])
+
+    def store(t):
+        rows = pl.ds(pl.multiple_of(t * R, R), R)
+        return pltpu.make_async_copy(dx.at[rows, :], dx_any.at[rows, :], sem.at[t])
+
+    def some_rows(t, carry):
+        rows = pl.ds(pl.multiple_of(t * R, R), R)
+        grads = [r[rows, :] for r in dqs] + [r[0, rows, :] for r in dkvs] + [r[1, rows, :] for r in dkvs]
+        dh = nt(jnp.concatenate(grads, axis=1), wqkv[...])
+        grad, _ = norm_back(x[rows, :].astype(f32), gain, dh)
+        dx[rows, :] = (dx2[rows, :] + grad).astype(bf16)
+        store(t).start()
+        return carry
+
+    lax.fori_loop(0, tiles, some_rows, 0)
+    for t in range(tiles):
+        store(t).wait()
 
 
 def finish(x, dx2, dqs, dkvs, weight, gain):
-    seq, width = x.shape
-    rows = pl.BlockSpec((R, width), lambda i: (i, 0))
     return pl.pallas_call(
         functools.partial(finish_kernel, len(dqs)),
-        grid=(seq // R,),
-        in_specs=[rows, rows, whole(weight.shape), whole((1, width))]
-        + [pl.BlockSpec((R, a.shape[1]), lambda i: (i, 0)) for a in dqs]
-        + [pl.BlockSpec((2, R, a.shape[2]), lambda i: (0, i, 0)) for a in dkvs],
-        out_specs=[rows, whole((8, width))],
-        out_shape=[shape((seq, width), bf16), shape((8, width), f32)],
+        in_specs=[IN_VMEM] * (4 + len(dqs) + len(dkvs)),
+        out_specs=pl.BlockSpec(memory_space=pl.ANY),
+        out_shape=shape(x.shape, bf16),
+        scratch_shapes=[pltpu.VMEM(x.shape, bf16), pltpu.SemaphoreType.DMA((x.shape[0] // R,))],
         compiler_params=params(24),
         cost_estimate=LONG,
         name="finish",
-    )(*pinned(x, dx2, weight), gain, *pinned(*dqs, *dkvs))
+    )(x, dx2, weight, gain, *dqs, *dkvs)
 
 
 def bit_orders(count):
     bits = [1 << i for i in range(count.bit_length() - 1)]
     if len(bits) == 4:
         x, y, z, far = bits
-        return [(x, y, z, far), (y, x, z, far), (z, x, far, y)]
+        return [(x, y, z, far), (y, z, x, far), (z, x, y, far)]
     return [tuple(bits[g:] + bits[:g]) for g in range(GROUPS)]
 
 
@@ -647,8 +640,11 @@
 
 def start_kernel(orders, wheres, me, *refs):
     arrays = len(wheres)
-    ins, outs = refs[: 2 * arrays], refs[2 * arrays :]
+    ins, outs = refs[: 2 * arrays], refs[-2 * GROUPS :]
     half = outs[0].shape[0]
+    if len(refs) > 2 * arrays + 2 * GROUPS:
+        here, there, total = refs[2 * arrays : -2 * GROUPS]
+        total[...] = here[...] + there[...]
     for g, order in enumerate(orders):
         for side in range(2):
 
@@ -666,26 +662,37 @@
             lax.fori_loop(0, half, one, 0)
 
 
-def start_sum(me, kept, got, wheres, orders):
+def start_sum(me, kept, got, wheres, orders, small):
     count = 1 << len(orders[0])
     half = count // 2
     rows = sum(a.shape[1] for a in kept)
     width = kept[0].shape[2]
     cols = width // 3
-    block = lambda a: pl.BlockSpec((a.shape[0], a.shape[1], cols), lambda c: (0, 0, c))
-    out = pl.BlockSpec((half, rows, cols), lambda c: (0, 0, c))
     args = [a for pair in zip(kept, got, strict=True) for a in pair]
+    sums = [shape((half, rows, width), bf16)] * (2 * GROUPS)
+    if small:
+        specs = dict(
+            in_specs=[SMEM] + [IN_VMEM] * (len(args) + 2),
+            out_specs=[IN_VMEM] * (1 + 2 * GROUPS),
+            out_shape=[shape(small[0].shape, f32)] + sums,
+        )
+    else:
+        block = lambda a: pl.BlockSpec((a.shape[0], a.shape[1], cols), lambda c: (0, 0, c))
+        specs = dict(
+            grid=(width // cols,),
+            in_specs=[SMEM] + [block(a) for a in args],
+            out_specs=[pl.BlockSpec((half, rows, cols), lambda c: (0, 0, c))] * (2 * GROUPS),
+            out_shape=sums,
+        )
     outs = pl.pallas_call(
         functools.partial(start_kernel, orders, wheres),
-        grid=(width // cols,),
-        in_specs=[SMEM] + [block(a) for a in args],
-        out_specs=[out] * (2 * GROUPS),
-        out_shape=[shape((half, rows, width), bf16)] * (2 * GROUPS),
         compiler_params=params(30),
         cost_estimate=COST,
         name="start_sum",
-    )(me, *args)
-    return outs[0::2], outs[1::2]
+        **specs,
+    )(me, *args, *small)
+    small, outs = list(outs[: len(outs) - 2 * GROUPS]), outs[-2 * GROUPS :]
+    return outs[0::2], outs[1::2], small
 
 
 def step_kernel(*refs):
@@ -741,28 +748,34 @@
     )(*kept, *got)
 
 
-def qkv_end_kernel(*refs):
-    ins, small, (out, sums) = refs[: 2 * GROUPS], refs[2 * GROUPS : 2 * GROUPS + 2], refs[2 * GROUPS + 2 :]
+def qkv_end_kernel(gain_line, *refs):
+    ins, small, outs = refs[: 2 * GROUPS], refs[2 * GROUPS : 2 * GROUPS + 2], refs[2 * GROUPS + 2 :]
+    out, gain1, gain2, rms = outs
     tall = out.shape[0]
+    width = gain1.shape[0]
     cols = ins[0].shape[2]
     for g in range(GROUPS):
         total = ins[g][0].astype(f32) + ins[GROUPS + g][0].astype(f32)
         for part in range(total.shape[0] // tall):
             at = (2 * g + part) * cols
             out[:, at : at + cols] = total[part * tall : (part + 1) * tall]
-    sums[...] = small[0][...] + small[1][...]
-
-
-def qkv_end(kept, got, small, tall, wide):
+    sums = small[0][...] + small[1][...]
+    gain2[...] = sums[3:4, :].reshape(width)
+    gain1[...] = (sums[4:5, :] / gain_line[...].reshape(1, width)).reshape(width)
+    count = jnp.max(sums[5:6, :], axis=1, keepdims=True) * width
+    rms[...] = jnp.broadcast_to(jnp.sqrt(jnp.sum(sums, axis=1, keepdims=True) / count), rms.shape)
+
+
+def qkv_end(gain, kept, got, small, tall, wide):
     return pl.pallas_call(
         qkv_end_kernel,
-        in_specs=[IN_VMEM] * (2 * GROUPS + 2),
-        out_specs=[IN_VMEM] * 2,
-        out_shape=[shape((tall, wide), f32), shape(small[0].shape, f32)],
+        in_specs=[IN_VMEM] * (2 * GROUPS + 3),
+        out_specs=[IN_VMEM] * 4,
+        out_shape=[shape((tall, wide), f32), shape(gain.shape, f32), shape(gain.shape, f32), shape((8, 128), f32)],
         compiler_params=params(16),
         cost_estimate=COST,
         name="qkv_end",
-    )(*kept, *got, *small)
+    )(gain, *kept, *got, *small)
 
 
 def after(value, *earlier):
@@ -771,7 +784,7 @@
 
 def sum_parts(me, kept, got, wheres, small):
     orders = bit_orders(lax.axis_size("batch"))
-    keep, send = start_sum(me, kept, got, wheres, orders)
+    keep, send, small = start_sum(me, kept, got, wheres, orders, small)
     for i in range(len(orders[0])):
         got = [exchange(s, "batch", order[i]) for s, order in zip(send, orders, strict=True)]
         small = [small[0], exchange(small[0], "batch", orders[0][i])] if small else []
@@ -794,7 +807,6 @@
     stream = lax.axis_index("stream").astype(jnp.int32)
     me = lax.axis_index("batch").astype(jnp.int32).reshape(1)
     info = jnp.stack([stream, lengths[0]])
-    gain1, gain2 = attn_gain.reshape(1, width), mlp_gain.reshape(1, width)
     cosine, sine = rotary_tables(seq)
     tables = (
         jnp.asarray(np.concatenate([cosine] * 4, axis=1)),
@@ -803,21 +815,20 @@
     tables_t = (jnp.asarray(cosine.T), jnp.asarray(sine.T))
 
     received = lax.ppermute(x, "stream", [(0, 1)])
-    q, ko, vo, h1t, sums_x = project(info, x, gain1, qkv_weight, tables)
     (
-        kc, vc, o, lse, outputs, dx2, do,
-        up_send, up_keep, down_send, down_keep, out_send, out_keep, sums_m,
+        q, ko, vo, kc, vc, h1t, o, lse, outputs, dx2, do,
+        up_send, up_keep, down_send, down_keep, out_send, out_keep, sums,
     ) = layer(
-        info, x, received, gain1, gain2, qkv_weight, tables, q, ko, vo, out_weight, dy, up_weight, down_weight
+        info, attn_gain, mlp_gain, received, x, qkv_weight, tables, out_weight, dy, up_weight, down_weight
     )
     down_got, up_got, out_got = (exchange(a, "stream", 1) for a in (down_send, up_send, out_send))
 
     def by_rows(array):
         return array.reshape(count * GROUPS, array.shape[0] // (count * GROUPS), width)
 
-    heads = (q, ko, vo, kc, vc, o, do, lse, *tables_t)
+    heads = (q, ko, vo, kc, vc, o)
     pairs = width // PW // 2
-    dq1, keep1, send1 = attend_back(info, 0, pairs, *heads)
+    dq1, keep1, send1 = attend_back(info, 0, pairs, *heads, do, lse, *tables_t)
     got1 = lax.ppermute(send1, "stream", [(1, 0)])
     early = sum_parts(
         me,
@@ -827,51 +838,36 @@
         [],
     )
     token = next(early)
-    dq2, keep2, send2 = attend_back(info, pairs, pairs, q, ko, vo, kc, vc, o, after(do, token), lse, *tables_t)
+    dq2, keep2, send2 = attend_back(info, pairs, pairs, *heads, after(do, token), lse, *tables_t)
     got2 = lax.ppermute(send2, "stream", [(1, 0)])
     token = early.send(dq2)
-    dkv1, qkv_send1, qkv_keep1 = weigh(info, (dq1, after(keep1, token)), got1, tables, h1t)
+    dkv1, qkv_send1, qkv_keep1, small = weigh(info, 0, dq1, after(keep1, token), got1, tables, h1t, qkv_weight, sums)
     qkv_got1 = exchange(qkv_send1, "stream", 1)
-    dkv2, qkv_send2, qkv_keep2 = weigh(info, (dq2, after(keep2, dkv1)), got2, tables, h1t)
+    dkv2, qkv_send2, qkv_keep2, small = weigh(info, pairs, dq2, keep2, got2, tables, h1t, qkv_weight, small)
     qkv_got2 = exchange(qkv_send2, "stream", 1)
+    small_got = exchange(small, "stream", 1)
     token = early.send(dkv2)
-    dx, sums_h = finish(after(x, token), dx2, [dq1, dq2], [dkv1, dkv2], qkv_weight, gain1)
-
-    small = jnp.concatenate(
-        [
-            sums_x[:1],
-            sums_m[:3],
-            sums_h[:1],
-            jnp.full((1, width), lengths[0].astype(f32)),
-            jnp.zeros((2, width), f32),
-        ]
-    )
-    small_got = exchange(small, "stream", 1)
+
     tall = width // (2 * count)
     split = lambda a: a.reshape(GROUPS * count, tall, a.shape[2])
     late = sum_parts(
         me,
-        [split(after(a, small)) for a in (qkv_keep1, qkv_keep2)],
+        [split(after(a, token)) for a in (qkv_keep1, qkv_keep2)],
         [split(a) for a in (qkv_got1, qkv_got2)],
         [lambda part, g: g * count + part] * 2,
-        [small + small_got],
+        [small, small_got],
     )
     token = next(late)
-    token = early.send(token)
-    out = late.send(token if isinstance(token, jax.Array) else None)
-    ends = token
-    while not isinstance(ends, tuple):
-        ends = early.send(out)
-        if not isinstance(out, tuple):
-            out = late.send(None if isinstance(ends, tuple) else ends)
-    while not isinstance(out, tuple):
-        out = late.send(None)
+    dx = finish(after(x, token), dx2, [dq1, dq2], [dkv1, dkv2], qkv_weight, attn_gain)
+    late_out = late.send(dx)
+    early_out = early.send(late_out)
+    while not isinstance(late_out, tuple):
+        late_out = late.send(None)
+    while not isinstance(early_out, tuple):
+        early_out = early.send(None)
     up_cols = down_keep.shape[0] // count
-    down_grad, up_grad, out_grad = feed_end(ends[0], ends[1], up_cols, tall)
-    qkv_grad, small = qkv_end(*out, tall, 3 * width)
-
-    squares = jnp.sum(small[:3], axis=1)
-    rms = jnp.sqrt(squares / (small[5, 0] * width))
+    down_grad, up_grad, out_grad = feed_end(*early_out[:2], up_cols, tall)
+    qkv_grad, gain1_grad, gain2_grad, rms = qkv_end(attn_gain, *late_out, tall, 3 * width)
     return (
         outputs[None, None],
         dx[None, None],
@@ -879,9 +875,9 @@
         out_grad,
         up_grad,
         down_grad,
-        small[4],
-        small[3],
-        rms,
+        gain1_grad,
+        gain2_grad,
+        rms[:3, 0],
     )
 
 

time: 232 us -> 199 us (0.86)
  local copies, waits for them, and re-layouts: 19.7 us -> 3.5 us
  Pallas kernels: 136 us -> 121 us
    pallas_call x7 -> x6, Pallas kernels: 39.3 us -> 19.2 us  [the longest x2 7.31 us: weigh(): pl.pallas_call(functools.partial(weigh_kernel, first), in_specs=[SMEM] +...]
    unnamed x65 -> x33, local copies, waits for them, and re-layouts: 12.3 us -> 2.88 us
    pallas_call x1, Pallas kernels: 66.5 us -> 71.5 us  [layer(): pl.pallas_call(layer_kernel, in_specs=[SMEM, IN_VMEM, IN_VMEM] + [anywher...]
    slice x5 -> x1, local copies, waits for them, and re-layouts: 3.02 us -> 0.63 us  [on_device(): rms[:3, 0]]
  transfers between devices with their start and end apart: 37 -> 37, of which waited for: 12 -> 15; matrix products, arithmetic and copies ran while one was open for 3% -> 1% of each run, Pallas kernels for 28% -> 24%
where the time goes in v3:
time: 199 us
  Pallas kernels  121 us (61%)
  starting transfers between devices  41.8 us (21%)
  waiting for transfers between devices  30.2 us (15%)
  local copies, waits for them, and re-layouts  3.5 us (2%)
    pallas_call x1, Pallas kernels, layer(): pl.pallas_call(layer_kernel, in_specs=[SMEM, IN_VMEM, IN_VMEM] + [anywher...  71.5 us
    ppermute x34, starting transfers between devices, exchange(): return lax.ppermute(value, axis, [(i, i ^ bit) for i in range(size)])  36.3 us
    ppermute x34, waiting for transfers between devices, exchange(): return lax.ppermute(value, axis, [(i, i ^ bit) for i in range(size)])  28.3 us
    pallas_call x2, Pallas kernels, attend_back(): pl.pallas_call(attend_back_kernel, grid=(pairs,), in_specs=[SMEM] + [head...  27.9 us
    pallas_call x2, Pallas kernels, weigh(): pl.pallas_call(functools.partial(weigh_kernel, first), in_specs=[SMEM] +...  7.31 us
    pallas_call x1, Pallas kernels, finish(): pl.pallas_call(functools.partial(finish_kernel, len(dqs)), in_specs=[IN_V...  6.3 us
    pallas_call x2, Pallas kernels, start_sum(): pl.pallas_call(functools.partial(start_kernel, orders, wheres), compiler_...  4.82 us
  transfers between devices with their start and end apart: 37, of which 15 were waited for; matrix products, arithmetic and copies ran while one was open for 1% of the time, Pallas kernels for 24%

profile of v3, /device:TPU:0, one launch (start us, length us, event | category | flops | bytes accessed | tf_op | source)
XLA Modules:
  0.0 198.7 jit_solution(1834813835877257513)
XLA Ops:
  0.6 2.5 %collective-permute-start = (bf16[1024,768]{1,0:T(8,128)(2,1)}, bf16[1024,768]{1,0:T(8,128)(2,1)S(1)}, u32[]{:S(2)}, u32[]{:S(2)}) collective-permute-start(bf16[1024,768]{1,0:T(8,128)(2,1)} %bitcast.26), channel_id=1, source_target_pairs={{0,16},{1,17},{2,18},{3,19},{4,20},{5,21},{6,22},{7,23},{8,24},{9,... | collective-permute-start | bytes 4718600 | tf_op jit(solution)/shard_map/ppermute | solution.py:817
  4.3 1.9 collective-permute-done.received_any
  7.4 71.5 %layer.1 = (bf16[6,1024,128]{2,1,0:T(8,128)(2,1)}, bf16[6,1024,128]{2,1,0:T(8,128)(2,1)}, bf16[6,1024,128]{2,1,0:T(8,128)(2,1)}, bf16[6,1024,128]{2,1,0:T(8,128)...) custom-call(s32[2]{0:T(128)} %pad_add_fusion.info, ...), custom_call_target="tpu_custom_call" | custom-call | flops 34359738368 | bytes 67108864 | tf_op jit(solution)/shard_map/layer/pallas_call | solution.py:517
  80.6 14.0 %attend_back.2 = (bf16[1024,384]{1,0:T(8,128)(2,1)S(1)}, bf16[2,1024,384]{2,1,0:T(8,128)(2,1)S(1)}, bf16[2,1024,384]{2,1,0:T(8,128)(2,1)S(1)}) custom-call(s32[2]{0:T(128)S(1)} %copy-done.10, bf16[6,1024,128]{2,1,0:T(8,128)(2,1)} %get-tuple-element.121.q, bf16[6,1024,128]{2,1,0:T(8,128)(2,1)} %get-tuple-element.122.ko, ...), custom_call_target="tpu_custom_call" | custom-call | flops 34359738368 | bytes 67108864 | tf_op jit(solution)/shard_map/attend_back/pallas_call | solution.py:272
  94.6 1.3 collective-permute-start.7
  96.0 3.9 %start_sum.2 = (bf16[8,72,768]{2,1,0:T(8,128)(2,1)S(1)}, bf16[8,72,768]{2,1,0:T(8,128)(2,1)S(1)}, bf16[8,72,768]{2,1,0:T(8,128)(2,1)S(1)}, bf16[8,72,768]{2,1,0:...) custom-call(s32[1]{0:T(128)} %bitcast.4.me, bf16[48,32,768]{2,1,0:T(8,128)(2,1)S(1)} %bitcast.17, ...), custom_call_target="tpu_custom_call" | custom-call | flops 1048576 | bytes 65536 | tf_op jit(solution)/shard_map/start_sum/pallas_call | solution.py:687
  99.9 2.4 %collective-permute-start.4 = (bf16[8,72,768]{2,1,0:T(8,128)(2,1)S(1)}, bf16[8,72,768]{2,1,0:T(8,128)(2,1)S(1)}, u32[]{:S(2)}, u32[]{:S(2)}) collective-permute-start(bf16[8,72,768]{2,1,0:T(8,128)(2,1)S(1)} %get-tuple-element.143), channel_id=1, source_target_pairs={{0,1},{1,0},{2,3},{3,2},{4,5},{5,4},{6,7},{7,6},{8,9},{9,8},{10,11... | collective-permute-start | bytes 2654216 | tf_op jit(solution)/shard_map/ppermute | solution.py:631
  102.3 1.5 collective-permute-start.5
  103.8 1.6 collective-permute-start.6
  105.4 14.0 %attend_back.3 = (bf16[1024,384]{1,0:T(8,128)(2,1)S(1)}, bf16[2,1024,384]{2,1,0:T(8,128)(2,1)S(1)}, bf16[2,1024,384]{2,1,0:T(8,128)(2,1)S(1)}) custom-call(s32[2]{0:T(128)S(1)} %copy-done.10, bf16[6,1024,128]{2,1,0:T(8,128)(2,1)} %get-tuple-element.121.q, bf16[6,1024,128]{2,1,0:T(8,128)(2,1)} %get-tuple-element.122.ko, ...), custom_call_target="tpu_custom_call" | custom-call | flops 34359738368 | bytes 67108864 | tf_op jit(solution)/shard_map/attend_back/pallas_call | solution.py:272
  119.5 1.8 collective-permute-start.8
  121.2 3.6 %collective-permute-done.5.refs_4_ = bf16[8,72,768]{2,1,0:T(8,128)(2,1)S(1)} collective-permute-done((bf16[8,72,768]{2,1,0:T(8,128)(2,1)S(1)}, bf16[8,72,768]{2,1,0:T(8,128)(2,1)S(1)}, u32[]{:S(2)}, u32[]{:S(2)}) %collective-permute-start.5) | collective-permute-done | bytes 884768 | tf_op jit(solution)/shard_map/ppermute | solution.py:631
  126.7 3.6 %weigh.2 = (bf16[2,1024,384]{2,1,0:T(8,128)(2,1)S(1)}, bf16[3,384,384]{2,1,0:T(8,128)(2,1)S(1)}, bf16[3,384,384]{2,1,0:T(8,128)(2,1)S(1)}, f32[8,768]{1,0:T(8,128)S(1)}) custom-call(s32[2]{0:T(128)S(1)} %copy-done.10, bf16[1024,384]{1,0:T(8,128)(2,1)S(1)} %get-tuple-element.129.dq.refs_0_, bf16[2,1024,384]{2,1,0:T(8,128)(2,1)S(1)} %get-tuple-element.152.keep, ...), custom_call_target="tpu_custom_call" | custom-call | flops 34359738368 | bytes 67108864 | tf_op jit(solution)/shard_map/weigh/pallas_call | solution.py:571
  130.4 3.7 %weigh.3 = (bf16[2,1024,384]{2,1,0:T(8,128)(2,1)S(1)}, bf16[3,384,384]{2,1,0:T(8,128)(2,1)S(1)}, bf16[3,384,384]{2,1,0:T(8,128)(2,1)S(1)}, f32[8,768]{1,0:T(8,128)S(1)}) custom-call(s32[2]{0:T(128)S(1)} %copy-done.10, bf16[1024,384]{1,0:T(8,128)(2,1)S(1)} %get-tuple-element.145.dq.refs_1_, bf16[2,1024,384]{2,1,0:T(8,128)(2,1)S(1)} %get-tuple-element.160.keep, ...), custom_call_target="tpu_custom_call" | custom-call | flops 34359738368 | bytes 67108864 | tf_op jit(solution)/shard_map/weigh/pallas_call | solution.py:571
  134.7 1.6 collective-permute-start.10
  137.3 9.5 %collective-permute-done.10.refs_4_ = bf16[4,72,768]{2,1,0:T(8,128)(2,1)S(1)} collective-permute-done((bf16[4,72,768]{2,1,0:T(8,128)(2,1)S(1)}, bf16[4,72,768]{2,1,0:T(8,128)(2,1)S(1)}, u32[]{:S(2)}, u32[]{:S(2)}) %collective-permute-start.10) | collective-permute-done | bytes 442400 | tf_op jit(solution)/shard_map/ppermute | solution.py:631
  146.8 1.3 collective-permute-done.11.refs_5_
  149.6 1.6 collective-permute-start.15
  153.1 6.3 %finish.1 = bf16[1024,768]{1,0:T(8,128)(2,1)} custom-call(bf16[1024,768]{1,0:T(8,128)(2,1)S(1)} %bitcast.28, f32[1024,768]{1,0:T(8,128)S(1)} %copy-done.11, bf16[768,2304]{1,0:T(8,128)(2,1)S(1)} %copy-done.4, f32[768]{0:T(1024)S(1)} %copy-done.3, bf16[1024,384]{1,0:T(8,128)(2,1)S(1)} %get-tuple-element.129.dq.refs_0_, ...), custom_call_target="tpu_custom_call" | custom-call | flops 34359738368 | bytes 67108864 | tf_op jit(solution)/shard_map/finish/pallas_call | solution.py:609
  160.0 1.7 collective-permute-start.20
  162.4 1.5 collective-permute-start.33
  164.9 3.7 %collective-permute-done.22.refs_7_ = f32[8,768]{1,0:T(8,128)S(1)} collective-permute-done((f32[8,768]{1,0:T(8,128)S(1)}, f32[8,768]{1,0:T(8,128)S(1)}, u32[]{:S(2)}, u32[]{:S(2)}) %collective-permute-start.22) | collective-permute-done | bytes 24608 | tf_op jit(solution)/shard_map/ppermute | solution.py:631
  168.6 1.6 collective-permute-start.21
  170.2 1.6 collective-permute-start.19
  171.8 2.0 collective-permute-done.21.refs_5_
  173.8 1.6 collective-permute-done.19.refs_3_
  176.8 2.6 %collective-permute-start.34 = (bf16[1,72,768]{2,1,0:T(8,128)(2,1)S(1)}, bf16[1,72,768]{2,1,0:T(8,128)(2,1)S(1)}, u32[]{:S(2)}, u32[]{:S(2)}) collective-permute-start(bf16[1,72,768]{2,1,0:T(8,128)(2,1)S(1)} %get-tuple-element.222), channel_id=1, source_target_pairs={{0,8},{1,9},{2,10},{3,11},{4,12},{5,13},{6,14},{7,15},{8,0},{9,1},... | collective-permute-start | bytes 331784 | tf_op jit(solution)/shard_map/ppermute | solution.py:631
  181.2 2.1 %collective-permute-done.26.refs_7_ = f32[8,768]{1,0:T(8,128)S(1)} collective-permute-done((f32[8,768]{1,0:T(8,128)S(1)}, f32[8,768]{1,0:T(8,128)S(1)}, u32[]{:S(2)}, u32[]{:S(2)}) %collective-permute-start.26) | collective-permute-done | bytes 24608 | tf_op jit(solution)/shard_map/ppermute | solution.py:631
  184.1 2.8 %collective-permute-start.36 = (bf16[1,72,768]{2,1,0:T(8,128)(2,1)S(1)}, bf16[1,72,768]{2,1,0:T(8,128)(2,1)S(1)}, u32[]{:S(2)}, u32[]{:S(2)}) collective-permute-start(bf16[1,72,768]{2,1,0:T(8,128)(2,1)S(1)} %get-tuple-element.224), channel_id=1, source_target_pairs={{0,8},{1,9},{2,10},{3,11},{4,12},{5,13},{6,14},{7,15},{8,0},{9,1},... | collective-permute-start | bytes 331784 | tf_op jit(solution)/shard_map/ppermute | solution.py:631
  187.7 1.7 collective-permute-start.27
  190.7 1.7 collective-permute-start.29
  192.4 1.2 collective-permute-start.30
  (93 shorter events, 23.6 us)
Async XLA Ops:
  0.6 5.6 %collective-permute-start = (bf16[1024,768]{1,0:T(8,128)(2,1)}, bf16[1024,768]{1,0:T(8,128)(2,1)S(1)}, u32[]{:S(2)}, u32[]{:S(2)}) collective-permute-start(bf16[1024,768]{1,0:T(8,128)(2,1)} %bitcast.26), channel_id=1, source_target_pairs={{0,16},{1,17},{2,18},{3,19},{4,20},{5,21},{6,22},{7,23},{8,24},{9,... | collective-permute-start | bytes 4718600 | tf_op jit(solution)/shard_map/ppermute | solution.py:817
  78.9 17.1 %collective-permute-start.3 = (bf16[384,768]{1,0:T(8,128)(2,1)}, bf16[384,768]{1,0:T(8,128)(2,1)S(1)}, u32[]{:S(2)}, u32[]{:S(2)}) collective-permute-start(bf16[384,768]{1,0:T(8,128)(2,1)} %get-tuple-element.139), channel_id=1, source_target_pairs={{0,16},{16,0},{1,17},{17,1},{2,18},{18,2},{3,19},{19,3},{4,20},{20... | collective-permute-start | bytes 1769480 | tf_op jit(solution)/shard_map/ppermute | solution.py:631
  79.3 16.6 %collective-permute-start.1 = (bf16[1536,768]{1,0:T(8,128)(2,1)}, bf16[1536,768]{1,0:T(8,128)(2,1)S(1)}, u32[]{:S(2)}, u32[]{:S(2)}) collective-permute-start(bf16[1536,768]{1,0:T(8,128)(2,1)} %get-tuple-element.133), channel_id=1, source_target_pairs={{0,16},{16,0},{1,17},{17,1},{2,18},{18,2},{3,19},{19,3},{4,20},{20... | collective-permute-start | bytes 7077896 | tf_op jit(solution)/shard_map/ppermute | solution.py:631
  79.4 16.5 %collective-permute-start.2 = (bf16[1536,768]{1,0:T(8,128)(2,1)}, bf16[1536,768]{1,0:T(8,128)(2,1)S(1)}, u32[]{:S(2)}, u32[]{:S(2)}) collective-permute-start(bf16[1536,768]{1,0:T(8,128)(2,1)} %get-tuple-element.136), channel_id=1, source_target_pairs={{0,16},{16,0},{1,17},{17,1},{2,18},{18,2},{3,19},{19,3},{4,20},{20... | collective-permute-start | bytes 7077896 | tf_op jit(solution)/shard_map/ppermute | solution.py:631
  94.6 32.0 %collective-permute-start.7 = (bf16[2,1024,384]{2,1,0:T(8,128)(2,1)S(1)}, bf16[2,1024,384]{2,1,0:T(8,128)(2,1)S(1)}, u32[]{:S(2)}, u32[]{:S(2)}) collective-permute-start(bf16[2,1024,384]{2,1,0:T(8,128)(2,1)S(1)} %get-tuple-element.153), channel_id=1, source_target_pairs={{16,0},{17,1},{18,2},{19,3},{20,4},{21,5},{22,6},{23,7},{24,8},{25... | collective-permute-start | bytes 4718600 | tf_op jit(solution)/shard_map/ppermute | solution.py:832
  99.9 26.1 %collective-permute-start.4 = (bf16[8,72,768]{2,1,0:T(8,128)(2,1)S(1)}, bf16[8,72,768]{2,1,0:T(8,128)(2,1)S(1)}, u32[]{:S(2)}, u32[]{:S(2)}) collective-permute-start(bf16[8,72,768]{2,1,0:T(8,128)(2,1)S(1)} %get-tuple-element.143), channel_id=1, source_target_pairs={{0,1},{1,0},{2,3},{3,2},{4,5},{5,4},{6,7},{7,6},{8,9},{9,8},{10,11... | collective-permute-start | bytes 2654216 | tf_op jit(solution)/shard_map/ppermute | solution.py:631
  102.3 22.5 %collective-permute-start.5 = (bf16[8,72,768]{2,1,0:T(8,128)(2,1)S(1)}, bf16[8,72,768]{2,1,0:T(8,128)(2,1)S(1)}, u32[]{:S(2)}, u32[]{:S(2)}) collective-permute-start(bf16[8,72,768]{2,1,0:T(8,128)(2,1)S(1)} %get-tuple-element.149), channel_id=1, source_target_pairs={{0,2},{1,3},{2,0},{3,1},{4,6},{5,7},{6,4},{7,5},{8,10},{9,11},{10,... | collective-permute-start | bytes 2654216 | tf_op jit(solution)/shard_map/ppermute | solution.py:631
  103.8 22.2 %collective-permute-start.6 = (bf16[8,72,768]{2,1,0:T(8,128)(2,1)S(1)}, bf16[8,72,768]{2,1,0:T(8,128)(2,1)S(1)}, u32[]{:S(2)}, u32[]{:S(2)}) collective-permute-start(bf16[8,72,768]{2,1,0:T(8,128)(2,1)S(1)} %get-tuple-element.150), channel_id=1, source_target_pairs={{0,4},{1,5},{2,6},{3,7},{4,0},{5,1},{6,2},{7,3},{8,12},{9,13},{10,... | collective-permute-start | bytes 2654216 | tf_op jit(solution)/shard_map/ppermute | solution.py:631
  119.5 11.0 %collective-permute-start.8 = (bf16[2,1024,384]{2,1,0:T(8,128)(2,1)S(1)}, bf16[2,1024,384]{2,1,0:T(8,128)(2,1)S(1)}, u32[]{:S(2)}, u32[]{:S(2)}) collective-permute-start(bf16[2,1024,384]{2,1,0:T(8,128)(2,1)S(1)} %get-tuple-element.161), channel_id=1, source_target_pairs={{16,0},{17,1},{18,2},{19,3},{20,4},{21,5},{22,6},{23,7},{24,8},{25... | collective-permute-start | bytes 4718600 | tf_op jit(solution)/shard_map/ppermute | solution.py:842
  130.3 18.3 %collective-permute-start.12 = (bf16[3,384,384]{2,1,0:T(8,128)(2,1)S(1)}, bf16[3,384,384]{2,1,0:T(8,128)(2,1)S(1)}, u32[]{:S(2)}, u32[]{:S(2)}) collective-permute-start(bf16[3,384,384]{2,1,0:T(8,128)(2,1)S(1)} %get-tuple-element.171), channel_id=1, source_target_pairs={{0,16},{16,0},{1,17},{17,1},{2,18},{18,2},{3,19},{19,3},{4,20},{20... | collective-permute-start | bytes 2654216 | tf_op jit(solution)/shard_map/ppermute | solution.py:631
  134.1 14.6 %collective-permute-start.13 = (bf16[3,384,384]{2,1,0:T(8,128)(2,1)S(1)}, bf16[3,384,384]{2,1,0:T(8,128)(2,1)S(1)}, u32[]{:S(2)}, u32[]{:S(2)}) collective-permute-start(bf16[3,384,384]{2,1,0:T(8,128)(2,1)S(1)} %get-tuple-element.174), channel_id=1, source_target_pairs={{0,16},{16,0},{1,17},{17,1},{2,18},{18,2},{3,19},{19,3},{4,20},{20... | collective-permute-start | bytes 2654216 | tf_op jit(solution)/shard_map/ppermute | solution.py:631
  134.7 12.2 %collective-permute-start.10 = (bf16[4,72,768]{2,1,0:T(8,128)(2,1)S(1)}, bf16[4,72,768]{2,1,0:T(8,128)(2,1)S(1)}, u32[]{:S(2)}, u32[]{:S(2)}) collective-permute-start(bf16[4,72,768]{2,1,0:T(8,128)(2,1)S(1)} %get-tuple-element.167), channel_id=1, source_target_pairs={{0,4},{1,5},{2,6},{3,7},{4,0},{5,1},{6,2},{7,3},{8,12},{9,13},{10,... | collective-permute-start | bytes 1327112 | tf_op jit(solution)/shard_map/ppermute | solution.py:631
  136.3 11.9 %collective-permute-start.11 = (bf16[4,72,768]{2,1,0:T(8,128)(2,1)S(1)}, bf16[4,72,768]{2,1,0:T(8,128)(2,1)S(1)}, u32[]{:S(2)}, u32[]{:S(2)}) collective-permute-start(bf16[4,72,768]{2,1,0:T(8,128)(2,1)S(1)} %get-tuple-element.168), channel_id=1, source_target_pairs={{0,1},{1,0},{2,3},{3,2},{4,5},{5,4},{6,7},{7,6},{8,9},{9,8},{10,11... | collective-permute-start | bytes 1327112 | tf_op jit(solution)/shard_map/ppermute | solution.py:631
  136.8 11.6 %collective-permute-start.9 = (bf16[4,72,768]{2,1,0:T(8,128)(2,1)S(1)}, bf16[4,72,768]{2,1,0:T(8,128)(2,1)S(1)}, u32[]{:S(2)}, u32[]{:S(2)}) collective-permute-start(bf16[4,72,768]{2,1,0:T(8,128)(2,1)S(1)} %get-tuple-element.151), channel_id=1, source_target_pairs={{0,2},{1,3},{2,0},{3,1},{4,6},{5,7},{6,4},{7,5},{8,10},{9,11},{10,... | collective-permute-start | bytes 1327112 | tf_op jit(solution)/shard_map/ppermute | solution.py:631
  149.6 10.2 %collective-permute-start.15 = (bf16[8,48,384]{2,1,0:T(8,128)(2,1)S(1)}, bf16[8,48,384]{2,1,0:T(8,128)(2,1)S(1)}, u32[]{:S(2)}, u32[]{:S(2)}) collective-permute-start(bf16[8,48,384]{2,1,0:T(8,128)(2,1)S(1)} %get-tuple-element.176), channel_id=1, source_target_pairs={{0,1},{1,0},{2,3},{3,2},{4,5},{5,4},{6,7},{7,6},{8,9},{9,8},{10,11... | collective-permute-start | bytes 884744 | tf_op jit(solution)/shard_map/ppermute | solution.py:631
  151.2 8.2 %collective-permute-start.18 = (f32[8,768]{1,0:T(8,128)S(1)}, f32[8,768]{1,0:T(8,128)S(1)}, u32[]{:S(2)}, u32[]{:S(2)}) collective-permute-start(f32[8,768]{1,0:T(8,128)S(1)} %get-tuple-element.188.refs_6_), channel_id=1, source_target_pairs={{0,1},{1,0},{2,3},{3,2},{4,5},{5,4},{6,7},{7,6},{8,9},{9,8},{10,11... | collective-permute-start | bytes 73736 | tf_op jit(solution)/shard_map/ppermute | solution.py:631
  151.7 7.8 %collective-permute-start.16 = (bf16[8,48,384]{2,1,0:T(8,128)(2,1)S(1)}, bf16[8,48,384]{2,1,0:T(8,128)(2,1)S(1)}, u32[]{:S(2)}, u32[]{:S(2)}) collective-permute-start(bf16[8,48,384]{2,1,0:T(8,128)(2,1)S(1)} %get-tuple-element.186), channel_id=1, source_target_pairs={{0,2},{1,3},{2,0},{3,1},{4,6},{5,7},{6,4},{7,5},{8,10},{9,11},{10,... | collective-permute-start | bytes 884744 | tf_op jit(solution)/shard_map/ppermute | solution.py:631
  152.2 7.5 %collective-permute-start.17 = (bf16[8,48,384]{2,1,0:T(8,128)(2,1)S(1)}, bf16[8,48,384]{2,1,0:T(8,128)(2,1)S(1)}, u32[]{:S(2)}, u32[]{:S(2)}) collective-permute-start(bf16[8,48,384]{2,1,0:T(8,128)(2,1)S(1)} %get-tuple-element.187), channel_id=1, source_target_pairs={{0,4},{1,5},{2,6},{3,7},{4,0},{5,1},{6,2},{7,3},{8,12},{9,13},{10,... | collective-permute-start | bytes 884744 | tf_op jit(solution)/shard_map/ppermute | solution.py:631
  160.0 10.2 %collective-permute-start.20 = (bf16[4,48,384]{2,1,0:T(8,128)(2,1)S(1)}, bf16[4,48,384]{2,1,0:T(8,128)(2,1)S(1)}, u32[]{:S(2)}, u32[]{:S(2)}) collective-permute-start(bf16[4,48,384]{2,1,0:T(8,128)(2,1)S(1)} %get-tuple-element.193), channel_id=1, source_target_pairs={{0,4},{1,5},{2,6},{3,7},{4,0},{5,1},{6,2},{7,3},{8,12},{9,13},{10,... | collective-permute-start | bytes 442376 | tf_op jit(solution)/shard_map/ppermute | solution.py:631
  161.7 15.0 %collective-permute-start.32 = (bf16[2,72,768]{2,1,0:T(8,128)(2,1)S(1)}, bf16[2,72,768]{2,1,0:T(8,128)(2,1)S(1)}, u32[]{:S(2)}, u32[]{:S(2)}) collective-permute-start(bf16[2,72,768]{2,1,0:T(8,128)(2,1)S(1)} %get-tuple-element.217), channel_id=1, source_target_pairs={{0,1},{1,0},{2,3},{3,2},{4,5},{5,4},{6,7},{7,6},{8,9},{9,8},{10,11... | collective-permute-start | bytes 663560 | tf_op jit(solution)/shard_map/ppermute | solution.py:631
  162.4 14.2 %collective-permute-start.33 = (bf16[2,72,768]{2,1,0:T(8,128)(2,1)S(1)}, bf16[2,72,768]{2,1,0:T(8,128)(2,1)S(1)}, u32[]{:S(2)}, u32[]{:S(2)}) collective-permute-start(bf16[2,72,768]{2,1,0:T(8,128)(2,1)S(1)} %get-tuple-element.218), channel_id=1, source_target_pairs={{0,2},{1,3},{2,0},{3,1},{4,6},{5,7},{6,4},{7,5},{8,10},{9,11},{10,... | collective-permute-start | bytes 663560 | tf_op jit(solution)/shard_map/ppermute | solution.py:631
  164.0 12.7 %collective-permute-start.31 = (bf16[2,72,768]{2,1,0:T(8,128)(2,1)S(1)}, bf16[2,72,768]{2,1,0:T(8,128)(2,1)S(1)}, u32[]{:S(2)}, u32[]{:S(2)}) collective-permute-start(bf16[2,72,768]{2,1,0:T(8,128)(2,1)S(1)} %get-tuple-element.169), channel_id=1, source_target_pairs={{0,4},{1,5},{2,6},{3,7},{4,0},{5,1},{6,2},{7,3},{8,12},{9,13},{10,... | collective-permute-start | bytes 663560 | tf_op jit(solution)/shard_map/ppermute | solution.py:631
  168.6 5.1 %collective-permute-start.21 = (bf16[4,48,384]{2,1,0:T(8,128)(2,1)S(1)}, bf16[4,48,384]{2,1,0:T(8,128)(2,1)S(1)}, u32[]{:S(2)}, u32[]{:S(2)}) collective-permute-start(bf16[4,48,384]{2,1,0:T(8,128)(2,1)S(1)} %get-tuple-element.194), channel_id=1, source_target_pairs={{0,1},{1,0},{2,3},{3,2},{4,5},{5,4},{6,7},{7,6},{8,9},{9,8},{10,11... | collective-permute-start | bytes 442376 | tf_op jit(solution)/shard_map/ppermute | solution.py:631
  170.2 5.1 %collective-permute-start.19 = (bf16[4,48,384]{2,1,0:T(8,128)(2,1)S(1)}, bf16[4,48,384]{2,1,0:T(8,128)(2,1)S(1)}, u32[]{:S(2)}, u32[]{:S(2)}) collective-permute-start(bf16[4,48,384]{2,1,0:T(8,128)(2,1)S(1)} %get-tuple-element.192), channel_id=1, source_target_pairs={{0,2},{1,3},{2,0},{3,1},{4,6},{5,7},{6,4},{7,5},{8,10},{9,11},{10,... | collective-permute-start | bytes 442376 | tf_op jit(solution)/shard_map/ppermute | solution.py:631
  175.4 8.7 %collective-permute-start.23 = (bf16[2,48,384]{2,1,0:T(8,128)(2,1)S(1)}, bf16[2,48,384]{2,1,0:T(8,128)(2,1)S(1)}, u32[]{:S(2)}, u32[]{:S(2)}) collective-permute-start(bf16[2,48,384]{2,1,0:T(8,128)(2,1)S(1)} %get-tuple-element.199), channel_id=1, source_target_pairs={{0,4},{1,5},{2,6},{3,7},{4,0},{5,1},{6,2},{7,3},{8,12},{9,13},{10,... | collective-permute-start | bytes 221192 | tf_op jit(solution)/shard_map/ppermute | solution.py:631
  176.8 13.9 %collective-permute-start.34 = (bf16[1,72,768]{2,1,0:T(8,128)(2,1)S(1)}, bf16[1,72,768]{2,1,0:T(8,128)(2,1)S(1)}, u32[]{:S(2)}, u32[]{:S(2)}) collective-permute-start(bf16[1,72,768]{2,1,0:T(8,128)(2,1)S(1)} %get-tuple-element.222), channel_id=1, source_target_pairs={{0,8},{1,9},{2,10},{3,11},{4,12},{5,13},{6,14},{7,15},{8,0},{9,1},... | collective-permute-start | bytes 331784 | tf_op jit(solution)/shard_map/ppermute | solution.py:631
  180.3 12.1 %collective-permute-start.35 = (bf16[1,72,768]{2,1,0:T(8,128)(2,1)S(1)}, bf16[1,72,768]{2,1,0:T(8,128)(2,1)S(1)}, u32[]{:S(2)}, u32[]{:S(2)}) collective-permute-start(bf16[1,72,768]{2,1,0:T(8,128)(2,1)S(1)} %get-tuple-element.223), channel_id=1, source_target_pairs={{0,8},{1,9},{2,10},{3,11},{4,12},{5,13},{6,14},{7,15},{8,0},{9,1},... | collective-permute-start | bytes 331784 | tf_op jit(solution)/shard_map/ppermute | solution.py:631
  180.7 6.2 %collective-permute-start.24 = (bf16[2,48,384]{2,1,0:T(8,128)(2,1)S(1)}, bf16[2,48,384]{2,1,0:T(8,128)(2,1)S(1)}, u32[]{:S(2)}, u32[]{:S(2)}) collective-permute-start(bf16[2,48,384]{2,1,0:T(8,128)(2,1)S(1)} %get-tuple-element.200), channel_id=1, source_target_pairs={{0,1},{1,0},{2,3},{3,2},{4,5},{5,4},{6,7},{7,6},{8,9},{9,8},{10,11... | collective-permute-start | bytes 221192 | tf_op jit(solution)/shard_map/ppermute | solution.py:631
  184.1 10.3 %collective-permute-start.36 = (bf16[1,72,768]{2,1,0:T(8,128)(2,1)S(1)}, bf16[1,72,768]{2,1,0:T(8,128)(2,1)S(1)}, u32[]{:S(2)}, u32[]{:S(2)}) collective-permute-start(bf16[1,72,768]{2,1,0:T(8,128)(2,1)S(1)} %get-tuple-element.224), channel_id=1, source_target_pairs={{0,8},{1,9},{2,10},{3,11},{4,12},{5,13},{6,14},{7,15},{8,0},{9,1},... | collective-permute-start | bytes 331784 | tf_op jit(solution)/shard_map/ppermute | solution.py:631
  187.7 9.6 %collective-permute-start.27 = (bf16[1,48,384]{2,1,0:T(8,128)(2,1)S(1)}, bf16[1,48,384]{2,1,0:T(8,128)(2,1)S(1)}, u32[]{:S(2)}, u32[]{:S(2)}) collective-permute-start(bf16[1,48,384]{2,1,0:T(8,128)(2,1)S(1)} %get-tuple-element.206), channel_id=1, source_target_pairs={{0,8},{1,9},{2,10},{3,11},{4,12},{5,13},{6,14},{7,15},{8,0},{9,1},... | collective-permute-start | bytes 110600 | tf_op jit(solution)/shard_map/ppermute | solution.py:631
  189.5 7.8 %collective-permute-start.28 = (bf16[1,48,384]{2,1,0:T(8,128)(2,1)S(1)}, bf16[1,48,384]{2,1,0:T(8,128)(2,1)S(1)}, u32[]{:S(2)}, u32[]{:S(2)}) collective-permute-start(bf16[1,48,384]{2,1,0:T(8,128)(2,1)S(1)} %get-tuple-element.207), channel_id=1, source_target_pairs={{0,8},{1,9},{2,10},{3,11},{4,12},{5,13},{6,14},{7,15},{8,0},{9,1},... | collective-permute-start | bytes 110600 | tf_op jit(solution)/shard_map/ppermute | solution.py:631
  190.7 6.6 %collective-permute-start.29 = (bf16[1,48,384]{2,1,0:T(8,128)(2,1)S(1)}, bf16[1,48,384]{2,1,0:T(8,128)(2,1)S(1)}, u32[]{:S(2)}, u32[]{:S(2)}) collective-permute-start(bf16[1,48,384]{2,1,0:T(8,128)(2,1)S(1)} %get-tuple-element.208), channel_id=1, source_target_pairs={{0,8},{1,9},{2,10},{3,11},{4,12},{5,13},{6,14},{7,15},{8,0},{9,1},... | collective-permute-start | bytes 110600 | tf_op jit(solution)/shard_map/ppermute | solution.py:631
  (21 other events, 366.4 us)

commit v4 on v3

--- a/solution.py
+++ b/solution.py
@@ -21,7 +21,7 @@
 AHEAD = 2
 FC = 512
 SCALE = HD**-0.5
-BIG = 60
+BIG = 57
 GROUPS = 3
 
 COST = pl.CostEstimate(flops=1 << 20, bytes_accessed=1 << 16, transcendentals=0)
@@ -618,12 +618,11 @@
     )(x, dx2, weight, gain, *dqs, *dkvs)
 
 
-def bit_orders(count):
+def bit_orders(count, groups):
     bits = [1 << i for i in range(count.bit_length() - 1)]
-    if len(bits) == 4:
-        x, y, z, far = bits
-        return [(x, y, z, far), (y, z, x, far), (z, x, y, far)]
-    return [tuple(bits[g:] + bits[:g]) for g in range(GROUPS)]
+    if groups == 2:
+        return [bits, bits[1::-1] + bits[2:]]
+    return [bits[g:-1] + bits[:g] + bits[-1:] for g in range(groups)]
 
 
 def exchange(value, axis, bit):
@@ -638,163 +637,213 @@
     return out
 
 
-def start_kernel(orders, wheres, me, *refs):
-    arrays = len(wheres)
-    ins, outs = refs[: 2 * arrays], refs[-2 * GROUPS :]
+LINES = 16
+
+
+def halves(value):
+    high = value.astype(bf16)
+    return high, (value - high.astype(f32)).astype(bf16)
+
+
+def put_sums(value, kept, block):
+    high, low = halves(value)
+    block[:LINES, :] = high
+    block[LINES : 2 * LINES, :] = low
+    kept[...] = high.astype(f32) + low.astype(f32)
+
+
+def got_sums(block):
+    return block[:LINES, :].astype(f32) + block[LINES : 2 * LINES, :].astype(f32)
+
+
+def start_kernel(orders, sources, small, me, *refs):
+    groups = len(orders)
+    arrays = max(a for source in sources for a, _ in source) + 1
+    ins, outs = refs[: 2 * arrays], refs[len(refs) - 2 * groups :]
     half = outs[0].shape[0]
-    if len(refs) > 2 * arrays + 2 * GROUPS:
-        here, there, total = refs[2 * arrays : -2 * GROUPS]
-        total[...] = here[...] + there[...]
     for g, order in enumerate(orders):
         for side in range(2):
 
             def one(r, carry, g=g, order=order, side=side):
                 part = me[0] ^ distance(order, r + side * half)
                 row = 0
-                for kept, got, where in zip(ins[::2], ins[1::2], wheres, strict=True):
-                    place = where(part, g)
+                for a, where in sources[g]:
+                    kept, got = ins[2 * a : 2 * a + 2]
+                    place = where(part)
                     size = kept.shape[1]
                     total = kept[place].astype(f32) + got[place].astype(f32)
-                    outs[g * 2 + side][r, row : row + size, :] = total.astype(bf16)
+                    outs[2 * g + side][r, row : row + size, :] = total.astype(bf16)
                     row += size
                 return carry
 
             lax.fori_loop(0, half, one, 0)
-
-
-def start_sum(me, kept, got, wheres, orders, small):
+    if small:
+        here, there, kept = refs[2 * arrays : 2 * arrays + 3]
+        total = here[...] + there[...]
+        if small == "rides":
+            wide = total.shape[1] // 2
+            total = jnp.concatenate([total[:, :wide], total[:, wide:]], axis=0)
+            put_sums(total, kept, outs[1].at[half])
+        else:
+            kept[...] = total
+
+
+def start_sum(me, kept, got, sources, orders, small, rides):
     count = 1 << len(orders[0])
     half = count // 2
-    rows = sum(a.shape[1] for a in kept)
+    rows = [sum(kept[a].shape[1] for a, _ in source) for source in sources]
     width = kept[0].shape[2]
     cols = width // 3
     args = [a for pair in zip(kept, got, strict=True) for a in pair]
-    sums = [shape((half, rows, width), bf16)] * (2 * GROUPS)
+    sums = []
+    for g in range(len(orders)):
+        sums += [shape((half, rows[g], width), bf16), shape((half + (rides and g == 0), rows[g], width), bf16)]
+    mode = "rides" if rides else "alone" if small else ""
     if small:
+        lines = (LINES, width) if rides else small[0].shape
         specs = dict(
             in_specs=[SMEM] + [IN_VMEM] * (len(args) + 2),
-            out_specs=[IN_VMEM] * (1 + 2 * GROUPS),
-            out_shape=[shape(small[0].shape, f32)] + sums,
+            out_specs=[IN_VMEM] * (1 + len(sums)),
+            out_shape=[shape(lines, f32)] + sums,
         )
     else:
         block = lambda a: pl.BlockSpec((a.shape[0], a.shape[1], cols), lambda c: (0, 0, c))
         specs = dict(
             grid=(width // cols,),
             in_specs=[SMEM] + [block(a) for a in args],
-            out_specs=[pl.BlockSpec((half, rows, cols), lambda c: (0, 0, c))] * (2 * GROUPS),
+            out_specs=[block(a) for a in sums],
             out_shape=sums,
         )
     outs = pl.pallas_call(
-        functools.partial(start_kernel, orders, wheres),
+        functools.partial(start_kernel, orders, sources, mode),
         compiler_params=params(30),
         cost_estimate=COST,
         name="start_sum",
         **specs,
     )(me, *args, *small)
-    small, outs = list(outs[: len(outs) - 2 * GROUPS]), outs[-2 * GROUPS :]
-    return outs[0::2], outs[1::2], small
-
-
-def step_kernel(*refs):
-    half = refs[0].shape[0] // 2
-    kept, got = refs[:GROUPS], refs[GROUPS : 2 * GROUPS]
-    outs = refs[len(refs) - 2 * GROUPS - len(refs) % 2 :]
-    for g in range(GROUPS):
-        total = (kept[g][...].astype(f32) + got[g][...].astype(f32)).astype(bf16)
-        outs[2 * g][...] = total[:half]
-        outs[2 * g + 1][...] = total[half:]
-    if len(refs) % 2:
-        outs[-1][...] = refs[2 * GROUPS][...] + refs[2 * GROUPS + 1][...]
-
-
-def step_sum(kept, got, small):
-    count, rows, width = kept[0].shape
+    small, outs = list(outs[: len(outs) - len(sums)]), outs[len(outs) - len(sums) :]
+    return list(outs[0::2]), list(outs[1::2]), small
+
+
+def step_kernel(groups, merge, mode, *refs):
+    kept, got = refs[:groups], refs[groups : 2 * groups]
+    outs = refs[2 * groups + (2 if mode == "alone" else 1 if mode else 0) :]
+    count = kept[0].shape[0]
+    half = count // 2
+    row = 0
+    for g in range(groups):
+        total = (kept[g][...].astype(f32) + got[g][:count].astype(f32)).astype(bf16)
+        keep, send = outs[:2] if merge else outs[2 * g : 2 * g + 2]
+        size = total.shape[1]
+        keep[:, row : row + size, :] = total[:half]
+        send[:half, row : row + size, :] = total[half:]
+        row += size if merge else 0
+    if mode == "rides":
+        total = refs[2 * groups][...] + got_sums(got[0].at[count])
+        put_sums(total, outs[-1], outs[1].at[half])
+    elif mode:
+        outs[-1][...] = refs[2 * groups][...] + refs[2 * groups + 1][...]
+
+
+def step_sum(kept, got, small, merge, rides):
+    groups = len(kept)
+    half = kept[0].shape[0] // 2
+    rows = [a.shape[1] for a in kept]
+    width = kept[0].shape[2]
     args = [*kept, *got, *small]
+    sums = []
+    for g, r in enumerate([sum(rows)] if merge else rows):
+        sums += [shape((half, r, width), bf16), shape((half + (rides and g == 0), r, width), bf16)]
     outs = pl.pallas_call(
-        step_kernel,
+        functools.partial(step_kernel, groups, merge, "rides" if rides else "alone" if small else ""),
         in_specs=[IN_VMEM] * len(args),
-        out_specs=[IN_VMEM] * (2 * GROUPS + len(small) // 2),
-        out_shape=[shape((count // 2, rows, width), bf16)] * (2 * GROUPS)
-        + [shape(a.shape, f32) for a in small[:1]],
+        out_specs=[IN_VMEM] * (len(sums) + len(small[:1])),
+        out_shape=sums + [shape(a.shape, f32) for a in small[:1]],
         compiler_params=params(16),
-        cost_estimate=COST,
+        cost_estimate=COST if small else LONG,
         name="step_sum",
     )(*args)
-    return outs[0 : 2 * GROUPS : 2], outs[1 : 2 * GROUPS : 2], list(outs[2 * GROUPS :])
-
-
-def feed_end_kernel(*refs):
-    ins, (down, up, out) = refs[: 2 * GROUPS], refs[2 * GROUPS :]
+    return list(outs[0 : len(sums) : 2]), list(outs[1 : len(sums) : 2]), list(outs[len(sums) :])
+
+
+def feed_end_kernel(kept, got, down, up, out):
+    total = kept[0].astype(f32) + got[0].astype(f32)
     tall, few = down.shape[0] // GROUPS, out.shape[0] // GROUPS
     ups = []
     for g in range(GROUPS):
-        total = ins[g][0].astype(f32) + ins[GROUPS + g][0].astype(f32)
-        down[g * tall : (g + 1) * tall, :] = total[:tall]
-        ups.append(total[tall : 2 * tall])
-        out[g * few : (g + 1) * few, :] = total[2 * tall :]
+        row = g * (2 * tall + few)
+        down[g * tall : (g + 1) * tall, :] = total[row : row + tall]
+        ups.append(total[row + tall : row + 2 * tall])
+        out[g * few : (g + 1) * few, :] = total[row + 2 * tall : row + 2 * tall + few]
     up[...] = jnp.concatenate(ups, axis=0).T
 
 
 def feed_end(kept, got, tall, few):
-    width = kept[0].shape[2]
+    width = kept.shape[2]
     return pl.pallas_call(
         feed_end_kernel,
-        in_specs=[IN_VMEM] * (2 * GROUPS),
+        in_specs=[IN_VMEM] * 2,
         out_specs=[IN_VMEM] * 3,
         out_shape=[shape((tall, width), f32), shape((width, tall), f32), shape((few, width), f32)],
         compiler_params=params(16),
         cost_estimate=COST,
         name="feed_end",
-    )(*kept, *got)
-
-
-def qkv_end_kernel(gain_line, *refs):
-    ins, small, outs = refs[: 2 * GROUPS], refs[2 * GROUPS : 2 * GROUPS + 2], refs[2 * GROUPS + 2 :]
-    out, gain1, gain2, rms = outs
+    )(kept, got)
+
+
+def qkv_end_kernel(rides, gain_line, kept, got, *refs):
+    out, gain1, gain2, rms = refs[-4:]
     tall = out.shape[0]
     width = gain1.shape[0]
-    cols = ins[0].shape[2]
-    for g in range(GROUPS):
-        total = ins[g][0].astype(f32) + ins[GROUPS + g][0].astype(f32)
-        for part in range(total.shape[0] // tall):
-            at = (2 * g + part) * cols
-            out[:, at : at + cols] = total[part * tall : (part + 1) * tall]
-    sums = small[0][...] + small[1][...]
+    cols = kept.shape[2]
+    total = kept[0].astype(f32) + got[0].astype(f32)
+    for i in range(total.shape[0] // tall):
+        part, third = i // 3, i % 3
+        at = third * width + part * cols
+        out[:, at : at + cols] = total[i * tall : (i + 1) * tall]
+    if rides:
+        sums = refs[0][...] + got_sums(got.at[1])
+        sums = jnp.concatenate([sums[: LINES // 2], sums[LINES // 2 :]], axis=1)
+    else:
+        sums = refs[0][...] + refs[1][...]
     gain2[...] = sums[3:4, :].reshape(width)
     gain1[...] = (sums[4:5, :] / gain_line[...].reshape(1, width)).reshape(width)
     count = jnp.max(sums[5:6, :], axis=1, keepdims=True) * width
     rms[...] = jnp.broadcast_to(jnp.sqrt(jnp.sum(sums, axis=1, keepdims=True) / count), rms.shape)
 
 
-def qkv_end(gain, kept, got, small, tall, wide):
+def qkv_end(gain, kept, got, small, tall, wide, rides):
     return pl.pallas_call(
-        qkv_end_kernel,
-        in_specs=[IN_VMEM] * (2 * GROUPS + 3),
+        functools.partial(qkv_end_kernel, rides),
+        in_specs=[IN_VMEM] * (3 + len(small)),
         out_specs=[IN_VMEM] * 4,
         out_shape=[shape((tall, wide), f32), shape(gain.shape, f32), shape(gain.shape, f32), shape((8, 128), f32)],
         compiler_params=params(16),
         cost_estimate=COST,
         name="qkv_end",
-    )(gain, *kept, *got, *small)
+    )(gain, kept, got, *small)
 
 
 def after(value, *earlier):
     return lax.optimization_barrier((value, earlier))[0]
 
 
-def sum_parts(me, kept, got, wheres, small):
-    orders = bit_orders(lax.axis_size("batch"))
-    keep, send, small = start_sum(me, kept, got, wheres, orders, small)
-    for i in range(len(orders[0])):
-        got = [exchange(s, "batch", order[i]) for s, order in zip(send, orders, strict=True)]
-        small = [small[0], exchange(small[0], "batch", orders[0][i])] if small else []
-        if i == len(orders[0]) - 1:
+def sum_parts(me, kept, got, sources, small, rides):
+    orders = bit_orders(lax.axis_size("batch"), len(sources))
+    steps = len(orders[0])
+    common = min(i for i in range(steps + 1) if all(order[i:] == orders[0][i:] for order in orders))
+    keep, send, small = start_sum(me, kept, got, sources, orders, small, rides)
+    for i in range(steps):
+        got = [exchange(s, "batch", order[i]) for s, order in zip(send, orders[: len(send)], strict=True)]
+        if small and not rides:
+            small = [small[0], exchange(small[0], "batch", orders[0][i])]
+        earlier = yield send[0], got
+        if i == steps - 1:
             break
-        earlier = yield send[0]
         if earlier is not None:
-            keep = after(list(keep), earlier)
-        keep, send, small = step_sum(keep, got, small)
-    yield keep, got, small
+            keep = after(keep, earlier)
+        keep, send, small = step_sum(keep, got, small, i + 1 == common, rides)
+    yield keep[0], got[0], small
 
 
 def on_device(
@@ -834,40 +883,44 @@
         me,
         [by_rows(after(a, dq1)) for a in (down_keep, up_keep, out_keep)],
         [by_rows(a) for a in (down_got, up_got, out_got)],
-        [lambda part, g: part * GROUPS + g] * 3,
+        [[(a, lambda part, g=g: part * GROUPS + g) for a in range(3)] for g in range(GROUPS)],
         [],
+        False,
     )
-    token = next(early)
+    token = next(early)[0]
     dq2, keep2, send2 = attend_back(info, pairs, pairs, *heads, after(do, token), lse, *tables_t)
     got2 = lax.ppermute(send2, "stream", [(1, 0)])
-    token = early.send(dq2)
+    token = early.send(dq2)[0]
     dkv1, qkv_send1, qkv_keep1, small = weigh(info, 0, dq1, after(keep1, token), got1, tables, h1t, qkv_weight, sums)
     qkv_got1 = exchange(qkv_send1, "stream", 1)
     dkv2, qkv_send2, qkv_keep2, small = weigh(info, pairs, dq2, keep2, got2, tables, h1t, qkv_weight, small)
     qkv_got2 = exchange(qkv_send2, "stream", 1)
     small_got = exchange(small, "stream", 1)
-    token = early.send(dkv2)
+    token = early.send(dkv2)[0]
 
     tall = width // (2 * count)
-    split = lambda a: a.reshape(GROUPS * count, tall, a.shape[2])
+    split = lambda a: a.reshape(3 * count, tall, a.shape[2])
+    rides = 3 * tall >= 2 * LINES
     late = sum_parts(
         me,
         [split(after(a, token)) for a in (qkv_keep1, qkv_keep2)],
         [split(a) for a in (qkv_got1, qkv_got2)],
-        [lambda part, g: g * count + part] * 2,
+        [[(g, lambda part, i=i: i * count + part) for i in range(3)] for g in range(2)],
         [small, small_got],
+        rides,
     )
-    token = next(late)
+    token, came = next(late)
     dx = finish(after(x, token), dx2, [dq1, dq2], [dkv1, dkv2], qkv_weight, attn_gain)
-    late_out = late.send(dx)
-    early_out = early.send(late_out)
-    while not isinstance(late_out, tuple):
-        late_out = late.send(None)
-    while not isinstance(early_out, tuple):
+    early_out = early.send((dx, came))
+    late_out = late.send(early_out[0])
+    while len(late_out) == 2:
+        last = late_out[0].shape[0] <= 3
+        late_out = late.send(early_out[1] if last and len(early_out) == 2 else None)
+    while len(early_out) == 2:
         early_out = early.send(None)
     up_cols = down_keep.shape[0] // count
     down_grad, up_grad, out_grad = feed_end(*early_out[:2], up_cols, tall)
-    qkv_grad, gain1_grad, gain2_grad, rms = qkv_end(attn_gain, *late_out, tall, 3 * width)
+    qkv_grad, gain1_grad, gain2_grad, rms = qkv_end(attn_gain, *late_out, tall, 3 * width, rides)
     return (
         outputs[None, None],
         dx[None, None],

time: 199 us -> 195 us (0.980)
  starting transfers between devices: 41.8 us -> 24.8 us
  waiting for transfers between devices: 30.2 us -> 43.6 us
    ppermute x34 -> x22, starting transfers between devices: 36.3 us -> 19.3 us  [exchange(): return lax.ppermute(value, axis, [(i, i ^ bit) for i in range(size)])]
    ppermute x34 -> x22, waiting for transfers between devices: 28.3 us -> 41.7 us  [exchange(): return lax.ppermute(value, axis, [(i, i ^ bit) for i in range(size)])]
  transfers between devices with their start and end apart: 37 -> 25, of which waited for: 15 -> 11; matrix products, arithmetic and copies ran while one was open for 1% -> 1% of each run, Pallas kernels for 24% -> 25%
where the time goes in v4:
time: 195 us
  Pallas kernels  121 us (62%)
  waiting for transfers between devices  43.6 us (22%)
  starting transfers between devices  24.8 us (13%)
  local copies, waits for them, and re-layouts  3.51 us (2%)
    pallas_call x1, Pallas kernels, layer(): pl.pallas_call(layer_kernel, in_specs=[SMEM, IN_VMEM, IN_VMEM] + [anywher...  71.5 us
    ppermute x22, waiting for transfers between devices, exchange(): return lax.ppermute(value, axis, [(i, i ^ bit) for i in range(size)])  41.7 us
    pallas_call x2, Pallas kernels, attend_back(): pl.pallas_call(attend_back_kernel, grid=(pairs,), in_specs=[SMEM] + [head...  27.8 us
    ppermute x22, starting transfers between devices, exchange(): return lax.ppermute(value, axis, [(i, i ^ bit) for i in range(size)])  19.3 us
    pallas_call x2, Pallas kernels, weigh(): pl.pallas_call(functools.partial(weigh_kernel, first), in_specs=[SMEM] +...  7.33 us
    pallas_call x1, Pallas kernels, finish(): pl.pallas_call(functools.partial(finish_kernel, len(dqs)), in_specs=[IN_V...  6.34 us
    pallas_call x2, Pallas kernels, start_sum(): pl.pallas_call(functools.partial(start_kernel, orders, sources, mode), co...  4.66 us
  transfers between devices with their start and end apart: 25, of which 11 were waited for; matrix products, arithmetic and copies ran while one was open for 1% of the time, Pallas kernels for 25%

profile of v4, /device:TPU:0, one launch (start us, length us, event | category | flops | bytes accessed | tf_op | source)
XLA Modules:
  0.0 194.8 jit_solution(2375858140263055760)
XLA Ops:
  0.6 2.5 %collective-permute-start = (bf16[1024,768]{1,0:T(8,128)(2,1)}, bf16[1024,768]{1,0:T(8,128)(2,1)S(1)}, u32[]{:S(2)}, u32[]{:S(2)}) collective-permute-start(bf16[1024,768]{1,0:T(8,128)(2,1)} %bitcast.26), channel_id=1, source_target_pairs={{0,16},{1,17},{2,18},{3,19},{4,20},{5,21},{6,22},{7,23},{8,24},{9,... | collective-permute-start | bytes 4718600 | tf_op jit(solution)/shard_map/ppermute | solution.py:866
  4.3 1.9 collective-permute-done.received_any
  6.2 1.1 copy-done.16
  7.4 71.5 %layer.1 = (bf16[6,1024,128]{2,1,0:T(8,128)(2,1)}, bf16[6,1024,128]{2,1,0:T(8,128)(2,1)}, bf16[6,1024,128]{2,1,0:T(8,128)(2,1)}, bf16[6,1024,128]{2,1,0:T(8,128)...) custom-call(s32[2]{0:T(128)} %pad_add_fusion.info, ...), custom_call_target="tpu_custom_call" | custom-call | flops 34359738368 | bytes 67108864 | tf_op jit(solution)/shard_map/layer/pallas_call | solution.py:517
  80.7 14.0 %attend_back.2 = (bf16[1024,384]{1,0:T(8,128)(2,1)S(1)}, bf16[2,1024,384]{2,1,0:T(8,128)(2,1)S(1)}, bf16[2,1024,384]{2,1,0:T(8,128)(2,1)S(1)}) custom-call(s32[2]{0:T(128)S(1)} %copy-done.10, bf16[6,1024,128]{2,1,0:T(8,128)(2,1)} %get-tuple-element.105.q, bf16[6,1024,128]{2,1,0:T(8,128)(2,1)} %get-tuple-element.106.ko, ...), custom_call_target="tpu_custom_call" | custom-call | flops 34359738368 | bytes 67108864 | tf_op jit(solution)/shard_map/attend_back/pallas_call | solution.py:272
  94.6 1.3 collective-permute-start.7
  96.0 3.9 %start_sum.2 = (bf16[8,72,768]{2,1,0:T(8,128)(2,1)S(1)}, bf16[8,72,768]{2,1,0:T(8,128)(2,1)S(1)}, bf16[8,72,768]{2,1,0:T(8,128)(2,1)S(1)}, bf16[8,72,768]{2,1,0:...) custom-call(s32[1]{0:T(128)} %bitcast.4.me, bf16[48,32,768]{2,1,0:T(8,128)(2,1)S(1)} %bitcast.17, ...), custom_call_target="tpu_custom_call" | custom-call | flops 1048576 | bytes 65536 | tf_op jit(solution)/shard_map/start_sum/pallas_call | solution.py:717
  100.0 2.4 %collective-permute-start.4 = (bf16[8,72,768]{2,1,0:T(8,128)(2,1)S(1)}, bf16[8,72,768]{2,1,0:T(8,128)(2,1)S(1)}, u32[]{:S(2)}, u32[]{:S(2)}) collective-permute-start(bf16[8,72,768]{2,1,0:T(8,128)(2,1)S(1)} %get-tuple-element.127), channel_id=1, source_target_pairs={{0,1},{1,0},{2,3},{3,2},{4,5},{5,4},{6,7},{7,6},{8,9},{9,8},{10,11... | collective-permute-start | bytes 2654216 | tf_op jit(solution)/shard_map/ppermute | solution.py:630
  102.4 1.5 collective-permute-start.5
  103.9 1.6 collective-permute-start.6
  105.5 13.8 %attend_back.3 = (bf16[1024,384]{1,0:T(8,128)(2,1)S(1)}, bf16[2,1024,384]{2,1,0:T(8,128)(2,1)S(1)}, bf16[2,1024,384]{2,1,0:T(8,128)(2,1)S(1)}) custom-call(s32[2]{0:T(128)S(1)} %copy-done.10, bf16[6,1024,128]{2,1,0:T(8,128)(2,1)} %get-tuple-element.105.q, bf16[6,1024,128]{2,1,0:T(8,128)(2,1)} %get-tuple-element.106.ko, ...), custom_call_target="tpu_custom_call" | custom-call | flops 34359738368 | bytes 67108864 | tf_op jit(solution)/shard_map/attend_back/pallas_call | solution.py:272
  119.4 1.8 collective-permute-start.8
  121.1 3.7 %collective-permute-done.5.refs_4_ = bf16[8,72,768]{2,1,0:T(8,128)(2,1)S(1)} collective-permute-done((bf16[8,72,768]{2,1,0:T(8,128)(2,1)S(1)}, bf16[8,72,768]{2,1,0:T(8,128)(2,1)S(1)}, u32[]{:S(2)}, u32[]{:S(2)}) %collective-permute-start.5) | collective-permute-done | bytes 884768 | tf_op jit(solution)/shard_map/ppermute | solution.py:630
  124.9 1.2 collective-permute-done.6.refs_5_
  127.3 1.6 collective-permute-start.10
  129.4 3.7 %weigh.2 = (bf16[2,1024,384]{2,1,0:T(8,128)(2,1)S(1)}, bf16[3,384,384]{2,1,0:T(8,128)(2,1)S(1)}, bf16[3,384,384]{2,1,0:T(8,128)(2,1)S(1)}, f32[8,768]{1,0:T(8,128)S(1)}) custom-call(s32[2]{0:T(128)S(1)} %copy-done.10, bf16[1024,384]{1,0:T(8,128)(2,1)S(1)} %get-tuple-element.113.dq.refs_0_, bf16[2,1024,384]{2,1,0:T(8,128)(2,1)S(1)} %get-tuple-element.136.keep, ...), custom_call_target="tpu_custom_call" | custom-call | flops 34359738368 | bytes 67108864 | tf_op jit(solution)/shard_map/weigh/pallas_call | solution.py:571
  133.2 3.7 %weigh.3 = (bf16[2,1024,384]{2,1,0:T(8,128)(2,1)S(1)}, bf16[3,384,384]{2,1,0:T(8,128)(2,1)S(1)}, bf16[3,384,384]{2,1,0:T(8,128)(2,1)S(1)}, f32[8,768]{1,0:T(8,128)S(1)}) custom-call(s32[2]{0:T(128)S(1)} %copy-done.10, bf16[1024,384]{1,0:T(8,128)(2,1)S(1)} %get-tuple-element.129.dq.refs_1_, bf16[2,1024,384]{2,1,0:T(8,128)(2,1)S(1)} %get-tuple-element.144.keep, ...), custom_call_target="tpu_custom_call" | custom-call | flops 34359738368 | bytes 67108864 | tf_op jit(solution)/shard_map/weigh/pallas_call | solution.py:571
  137.4 1.5 collective-permute-done.10.refs_4_
  138.9 1.3 collective-permute-done.11.refs_5_
  141.6 1.4 collective-permute-start.19
  143.8 1.6 collective-permute-start.15
  145.9 6.3 %finish.1 = bf16[1024,768]{1,0:T(8,128)(2,1)} custom-call(bf16[1024,768]{1,0:T(8,128)(2,1)S(1)} %bitcast.28, f32[1024,768]{1,0:T(8,128)S(1)} %copy-done.11, bf16[768,2304]{1,0:T(8,128)(2,1)S(1)} %copy-done.4, f32[768]{0:T(1024)S(1)} %copy-done.3, bf16[1024,384]{1,0:T(8,128)(2,1)S(1)} %get-tuple-element.113.dq.refs_0_, ...), custom_call_target="tpu_custom_call" | custom-call | flops 34359738368 | bytes 67108864 | tf_op jit(solution)/shard_map/finish/pallas_call | solution.py:609
  152.3 5.9 %collective-permute-done.16.refs_3_ = bf16[8,72,384]{2,1,0:T(8,128)(2,1)S(1)} collective-permute-done((bf16[8,72,384]{2,1,0:T(8,128)(2,1)S(1)}, bf16[8,72,384]{2,1,0:T(8,128)(2,1)S(1)}, u32[]{:S(2)}, u32[]{:S(2)}) %collective-permute-start.16) | collective-permute-done | bytes 442400 | tf_op jit(solution)/shard_map/ppermute | solution.py:630
  158.2 0.9 collective-permute-done.15.refs_2_
  159.5 1.5 collective-permute-start.20
  161.6 2.6 %collective-permute-start.22 = (bf16[1,216,768]{2,1,0:T(8,128)(2,1)S(1)}, bf16[1,216,768]{2,1,0:T(8,128)(2,1)S(1)}, u32[]{:S(2)}, u32[]{:S(2)}) collective-permute-start(bf16[1,216,768]{2,1,0:T(8,128)(2,1)S(1)} %get-tuple-element.175), channel_id=1, source_target_pairs={{0,8},{1,9},{2,10},{3,11},{4,12},{5,13},{6,14},{7,15},{8,0},{9,1},... | collective-permute-start | bytes 995336 | tf_op jit(solution)/shard_map/ppermute | solution.py:630
  164.2 3.1 %collective-permute-done.21.refs_3_ = bf16[4,72,384]{2,1,0:T(8,128)(2,1)S(1)} collective-permute-done((bf16[4,72,384]{2,1,0:T(8,128)(2,1)S(1)}, bf16[4,72,384]{2,1,0:T(8,128)(2,1)S(1)}, u32[]{:S(2)}, u32[]{:S(2)}) %collective-permute-start.21) | collective-permute-done | bytes 221216 | tf_op jit(solution)/shard_map/ppermute | solution.py:630
  167.6 9.2 %collective-permute-done.22.got = bf16[1,216,768]{2,1,0:T(8,128)(2,1)S(1)} collective-permute-done((bf16[1,216,768]{2,1,0:T(8,128)(2,1)S(1)}, bf16[1,216,768]{2,1,0:T(8,128)(2,1)S(1)}, u32[]{:S(2)}, u32[]{:S(2)}) %collective-permute-start.22) | collective-permute-done | bytes 331808 | tf_op jit(solution)/shard_map/ppermute | solution.py:630
  176.8 5.8 %collective-permute-done.23.refs_1_ = bf16[3,144,384]{2,1,0:T(8,128)(2,1)S(1)} collective-permute-done((bf16[3,144,384]{2,1,0:T(8,128)(2,1)S(1)}, bf16[3,144,384]{2,1,0:T(8,128)(2,1)S(1)}, u32[]{:S(2)}, u32[]{:S(2)}) %collective-permute-start.23) | collective-permute-done | bytes 331808 | tf_op jit(solution)/shard_map/ppermute | solution.py:630
  182.7 0.9 feed_end.1
  183.6 0.9 copy.23
  184.5 8.9 %collective-permute-done.24.got = bf16[2,144,384]{2,1,0:T(8,128)(2,1)S(1)} collective-permute-done((bf16[2,144,384]{2,1,0:T(8,128)(2,1)S(1)}, bf16[2,144,384]{2,1,0:T(8,128)(2,1)S(1)}, u32[]{:S(2)}, u32[]{:S(2)}) %collective-permute-start.24) | collective-permute-done | bytes 221216 | tf_op jit(solution)/shard_map/ppermute | solution.py:630
  (71 shorter events, 10.2 us)
Async XLA Ops:
  0.6 5.6 %collective-permute-start = (bf16[1024,768]{1,0:T(8,128)(2,1)}, bf16[1024,768]{1,0:T(8,128)(2,1)S(1)}, u32[]{:S(2)}, u32[]{:S(2)}) collective-permute-start(bf16[1024,768]{1,0:T(8,128)(2,1)} %bitcast.26), channel_id=1, source_target_pairs={{0,16},{1,17},{2,18},{3,19},{4,20},{5,21},{6,22},{7,23},{8,24},{9,... | collective-permute-start | bytes 4718600 | tf_op jit(solution)/shard_map/ppermute | solution.py:866
  7.4 72.5 %copy-start.8 = (f32[32,1024]{1,0:T(8,128)S(1)}, f32[32,1024]{1,0:T(8,128)}, u32[]{:S(2)}) copy-start(f32[32,1024]{1,0:T(8,128)} %constant.20.clone.sine) | copy-start | bytes 393220
  7.4 72.5 %copy-start.9 = (f32[32,1024]{1,0:T(8,128)S(1)}, f32[32,1024]{1,0:T(8,128)}, u32[]{:S(2)}) copy-start(f32[32,1024]{1,0:T(8,128)} %constant.19.clone.cosine) | copy-start | bytes 393220
  7.4 72.5 %copy-start.10 = (s32[2]{0:T(128)S(1)}, s32[2]{0:T(128)}, u32[]{:S(2)}) copy-start(s32[2]{0:T(128)} %pad_add_fusion.info) | copy-start | bytes 28
  78.9 17.0 %collective-permute-start.3 = (bf16[384,768]{1,0:T(8,128)(2,1)}, bf16[384,768]{1,0:T(8,128)(2,1)S(1)}, u32[]{:S(2)}, u32[]{:S(2)}) collective-permute-start(bf16[384,768]{1,0:T(8,128)(2,1)} %get-tuple-element.123), channel_id=1, source_target_pairs={{0,16},{16,0},{1,17},{17,1},{2,18},{18,2},{3,19},{19,3},{4,20},{20... | collective-permute-start | bytes 1769480 | tf_op jit(solution)/shard_map/ppermute | solution.py:630
  79.3 16.6 %collective-permute-start.1 = (bf16[1536,768]{1,0:T(8,128)(2,1)}, bf16[1536,768]{1,0:T(8,128)(2,1)S(1)}, u32[]{:S(2)}, u32[]{:S(2)}) collective-permute-start(bf16[1536,768]{1,0:T(8,128)(2,1)} %get-tuple-element.117), channel_id=1, source_target_pairs={{0,16},{16,0},{1,17},{17,1},{2,18},{18,2},{3,19},{19,3},{4,20},{20... | collective-permute-start | bytes 7077896 | tf_op jit(solution)/shard_map/ppermute | solution.py:630
  79.5 16.5 %collective-permute-start.2 = (bf16[1536,768]{1,0:T(8,128)(2,1)}, bf16[1536,768]{1,0:T(8,128)(2,1)S(1)}, u32[]{:S(2)}, u32[]{:S(2)}) collective-permute-start(bf16[1536,768]{1,0:T(8,128)(2,1)} %get-tuple-element.120), channel_id=1, source_target_pairs={{0,16},{16,0},{1,17},{17,1},{2,18},{18,2},{3,19},{19,3},{4,20},{20... | collective-permute-start | bytes 7077896 | tf_op jit(solution)/shard_map/ppermute | solution.py:630
  80.7 15.3 %copy-start = (bf16[1536,768]{1,0:T(8,128)(2,1)S(1)}, bf16[1536,768]{1,0:T(8,128)(2,1)}, u32[]{:S(2)}) copy-start(bf16[1536,768]{1,0:T(8,128)(2,1)} %get-tuple-element.119) | copy-start | bytes 7077892
  80.7 15.3 %copy-start.1 = (bf16[1536,768]{1,0:T(8,128)(2,1)S(1)}, bf16[1536,768]{1,0:T(8,128)(2,1)}, u32[]{:S(2)}) copy-start(bf16[1536,768]{1,0:T(8,128)(2,1)} %get-tuple-element.116) | copy-start | bytes 7077892
  80.7 15.3 %copy-start.2 = (bf16[384,768]{1,0:T(8,128)(2,1)S(1)}, bf16[384,768]{1,0:T(8,128)(2,1)}, u32[]{:S(2)}) copy-start(bf16[384,768]{1,0:T(8,128)(2,1)} %get-tuple-element.122) | copy-start | bytes 1769476
  94.6 34.7 %collective-permute-start.7 = (bf16[2,1024,384]{2,1,0:T(8,128)(2,1)S(1)}, bf16[2,1024,384]{2,1,0:T(8,128)(2,1)S(1)}, u32[]{:S(2)}, u32[]{:S(2)}) collective-permute-start(bf16[2,1024,384]{2,1,0:T(8,128)(2,1)S(1)} %get-tuple-element.137), channel_id=1, source_target_pairs={{16,0},{17,1},{18,2},{19,3},{20,4},{21,5},{22,6},{23,7},{24,8},{25... | collective-permute-start | bytes 4718600 | tf_op jit(solution)/shard_map/ppermute | solution.py:881
  100.0 26.1 %collective-permute-start.4 = (bf16[8,72,768]{2,1,0:T(8,128)(2,1)S(1)}, bf16[8,72,768]{2,1,0:T(8,128)(2,1)S(1)}, u32[]{:S(2)}, u32[]{:S(2)}) collective-permute-start(bf16[8,72,768]{2,1,0:T(8,128)(2,1)S(1)} %get-tuple-element.127), channel_id=1, source_target_pairs={{0,1},{1,0},{2,3},{3,2},{4,5},{5,4},{6,7},{7,6},{8,9},{9,8},{10,11... | collective-permute-start | bytes 2654216 | tf_op jit(solution)/shard_map/ppermute | solution.py:630
  102.4 22.5 %collective-permute-start.5 = (bf16[8,72,768]{2,1,0:T(8,128)(2,1)S(1)}, bf16[8,72,768]{2,1,0:T(8,128)(2,1)S(1)}, u32[]{:S(2)}, u32[]{:S(2)}) collective-permute-start(bf16[8,72,768]{2,1,0:T(8,128)(2,1)S(1)} %get-tuple-element.133), channel_id=1, source_target_pairs={{0,2},{1,3},{2,0},{3,1},{4,6},{5,7},{6,4},{7,5},{8,10},{9,11},{10,... | collective-permute-start | bytes 2654216 | tf_op jit(solution)/shard_map/ppermute | solution.py:630
  103.9 22.2 %collective-permute-start.6 = (bf16[8,72,768]{2,1,0:T(8,128)(2,1)S(1)}, bf16[8,72,768]{2,1,0:T(8,128)(2,1)S(1)}, u32[]{:S(2)}, u32[]{:S(2)}) collective-permute-start(bf16[8,72,768]{2,1,0:T(8,128)(2,1)S(1)} %get-tuple-element.134), channel_id=1, source_target_pairs={{0,4},{1,5},{2,6},{3,7},{4,0},{5,1},{6,2},{7,3},{8,12},{9,13},{10,... | collective-permute-start | bytes 2654216 | tf_op jit(solution)/shard_map/ppermute | solution.py:630
  119.3 10.1 %copy-start.4 = (bf16[768,2304]{1,0:T(8,128)(2,1)S(1)}, bf16[768,2304]{1,0:T(8,128)(2,1)}, u32[]{:S(2)}) copy-start(bf16[768,2304]{1,0:T(8,128)(2,1)} %wqkv.5) | copy-start | bytes 10616836
  119.4 13.8 %collective-permute-start.8 = (bf16[2,1024,384]{2,1,0:T(8,128)(2,1)S(1)}, bf16[2,1024,384]{2,1,0:T(8,128)(2,1)S(1)}, u32[]{:S(2)}, u32[]{:S(2)}) collective-permute-start(bf16[2,1024,384]{2,1,0:T(8,128)(2,1)S(1)} %get-tuple-element.145), channel_id=1, source_target_pairs={{16,0},{17,1},{18,2},{19,3},{20,4},{21,5},{22,6},{23,7},{24,8},{25... | collective-permute-start | bytes 4718600 | tf_op jit(solution)/shard_map/ppermute | solution.py:892
  126.7 13.5 %collective-permute-start.9 = (bf16[4,72,768]{2,1,0:T(8,128)(2,1)S(1)}, bf16[4,72,768]{2,1,0:T(8,128)(2,1)S(1)}, u32[]{:S(2)}, u32[]{:S(2)}) collective-permute-start(bf16[4,72,768]{2,1,0:T(8,128)(2,1)S(1)} %get-tuple-element.135), channel_id=1, source_target_pairs={{0,2},{1,3},{2,0},{3,1},{4,6},{5,7},{6,4},{7,5},{8,10},{9,11},{10,... | collective-permute-start | bytes 1327112 | tf_op jit(solution)/shard_map/ppermute | solution.py:630
  127.3 11.6 %collective-permute-start.10 = (bf16[4,72,768]{2,1,0:T(8,128)(2,1)S(1)}, bf16[4,72,768]{2,1,0:T(8,128)(2,1)S(1)}, u32[]{:S(2)}, u32[]{:S(2)}) collective-permute-start(bf16[4,72,768]{2,1,0:T(8,128)(2,1)S(1)} %get-tuple-element.151), channel_id=1, source_target_pairs={{0,4},{1,5},{2,6},{3,7},{4,0},{5,1},{6,2},{7,3},{8,12},{9,13},{10,... | collective-permute-start | bytes 1327112 | tf_op jit(solution)/shard_map/ppermute | solution.py:630
  128.9 11.4 %collective-permute-start.11 = (bf16[4,72,768]{2,1,0:T(8,128)(2,1)S(1)}, bf16[4,72,768]{2,1,0:T(8,128)(2,1)S(1)}, u32[]{:S(2)}, u32[]{:S(2)}) collective-permute-start(bf16[4,72,768]{2,1,0:T(8,128)(2,1)S(1)} %get-tuple-element.152), channel_id=1, source_target_pairs={{0,1},{1,0},{2,3},{3,2},{4,5},{5,4},{6,7},{7,6},{8,9},{9,8},{10,11... | collective-permute-start | bytes 1327112 | tf_op jit(solution)/shard_map/ppermute | solution.py:630
  133.1 10.0 %collective-permute-start.12 = (bf16[3,384,384]{2,1,0:T(8,128)(2,1)S(1)}, bf16[3,384,384]{2,1,0:T(8,128)(2,1)S(1)}, u32[]{:S(2)}, u32[]{:S(2)}) collective-permute-start(bf16[3,384,384]{2,1,0:T(8,128)(2,1)S(1)} %get-tuple-element.155), channel_id=1, source_target_pairs={{0,16},{16,0},{1,17},{17,1},{2,18},{18,2},{3,19},{19,3},{4,20},{20... | collective-permute-start | bytes 2654216 | tf_op jit(solution)/shard_map/ppermute | solution.py:630
  136.8 4.8 %collective-permute-start.14 = (f32[8,768]{1,0:T(8,128)S(1)}, f32[8,768]{1,0:T(8,128)S(1)}, u32[]{:S(2)}, u32[]{:S(2)}) collective-permute-start(f32[8,768]{1,0:T(8,128)S(1)} %get-tuple-element.159.refs_4_), channel_id=1, source_target_pairs={{0,16},{16,0},{1,17},{17,1},{2,18},{18,2},{3,19},{19,3},{4,20},{20... | collective-permute-start | bytes 73736 | tf_op jit(solution)/shard_map/ppermute | solution.py:630
  138.9 4.2 %collective-permute-start.13 = (bf16[3,384,384]{2,1,0:T(8,128)(2,1)S(1)}, bf16[3,384,384]{2,1,0:T(8,128)(2,1)S(1)}, u32[]{:S(2)}, u32[]{:S(2)}) collective-permute-start(bf16[3,384,384]{2,1,0:T(8,128)(2,1)S(1)} %get-tuple-element.158), channel_id=1, source_target_pairs={{0,16},{16,0},{1,17},{17,1},{2,18},{18,2},{3,19},{19,3},{4,20},{20... | collective-permute-start | bytes 2654216 | tf_op jit(solution)/shard_map/ppermute | solution.py:630
  140.5 18.6 %collective-permute-start.17 = (bf16[2,72,768]{2,1,0:T(8,128)(2,1)S(1)}, bf16[2,72,768]{2,1,0:T(8,128)(2,1)S(1)}, u32[]{:S(2)}, u32[]{:S(2)}) collective-permute-start(bf16[2,72,768]{2,1,0:T(8,128)(2,1)S(1)} %get-tuple-element.153), channel_id=1, source_target_pairs={{0,4},{1,5},{2,6},{3,7},{4,0},{5,1},{6,2},{7,3},{8,12},{9,13},{10,... | collective-permute-start | bytes 663560 | tf_op jit(solution)/shard_map/ppermute | solution.py:630
  141.1 18.1 %collective-permute-start.18 = (bf16[2,72,768]{2,1,0:T(8,128)(2,1)S(1)}, bf16[2,72,768]{2,1,0:T(8,128)(2,1)S(1)}, u32[]{:S(2)}, u32[]{:S(2)}) collective-permute-start(bf16[2,72,768]{2,1,0:T(8,128)(2,1)S(1)} %get-tuple-element.173), channel_id=1, source_target_pairs={{0,1},{1,0},{2,3},{3,2},{4,5},{5,4},{6,7},{7,6},{8,9},{9,8},{10,11... | collective-permute-start | bytes 663560 | tf_op jit(solution)/shard_map/ppermute | solution.py:630
  141.6 17.5 %collective-permute-start.19 = (bf16[2,72,768]{2,1,0:T(8,128)(2,1)S(1)}, bf16[2,72,768]{2,1,0:T(8,128)(2,1)S(1)}, u32[]{:S(2)}, u32[]{:S(2)}) collective-permute-start(bf16[2,72,768]{2,1,0:T(8,128)(2,1)S(1)} %get-tuple-element.174), channel_id=1, source_target_pairs={{0,2},{1,3},{2,0},{3,1},{4,6},{5,7},{6,4},{7,5},{8,10},{9,11},{10,... | collective-permute-start | bytes 663560 | tf_op jit(solution)/shard_map/ppermute | solution.py:630
  143.8 15.3 %collective-permute-start.15 = (bf16[9,72,384]{2,1,0:T(8,128)(2,1)S(1)}, bf16[9,72,384]{2,1,0:T(8,128)(2,1)S(1)}, u32[]{:S(2)}, u32[]{:S(2)}) collective-permute-start(bf16[9,72,384]{2,1,0:T(8,128)(2,1)S(1)} %get-tuple-element.160), channel_id=1, source_target_pairs={{0,1},{1,0},{2,3},{3,2},{4,5},{5,4},{6,7},{7,6},{8,9},{9,8},{10,11... | collective-permute-start | bytes 1493000 | tf_op jit(solution)/shard_map/ppermute | solution.py:630
  145.4 12.8 %collective-permute-start.16 = (bf16[8,72,384]{2,1,0:T(8,128)(2,1)S(1)}, bf16[8,72,384]{2,1,0:T(8,128)(2,1)S(1)}, u32[]{:S(2)}, u32[]{:S(2)}) collective-permute-start(bf16[8,72,384]{2,1,0:T(8,128)(2,1)S(1)} %get-tuple-element.169), channel_id=1, source_target_pairs={{0,2},{1,3},{2,0},{3,1},{4,6},{5,7},{6,4},{7,5},{8,10},{9,11},{10,... | collective-permute-start | bytes 1327112 | tf_op jit(solution)/shard_map/ppermute | solution.py:630
  159.5 7.8 %collective-permute-start.20 = (bf16[5,72,384]{2,1,0:T(8,128)(2,1)S(1)}, bf16[5,72,384]{2,1,0:T(8,128)(2,1)S(1)}, u32[]{:S(2)}, u32[]{:S(2)}) collective-permute-start(bf16[5,72,384]{2,1,0:T(8,128)(2,1)S(1)} %get-tuple-element.181), channel_id=1, source_target_pairs={{0,2},{1,3},{2,0},{3,1},{4,6},{5,7},{6,4},{7,5},{8,10},{9,11},{10,... | collective-permute-start | bytes 829448 | tf_op jit(solution)/shard_map/ppermute | solution.py:630
  161.1 6.3 %collective-permute-start.21 = (bf16[4,72,384]{2,1,0:T(8,128)(2,1)S(1)}, bf16[4,72,384]{2,1,0:T(8,128)(2,1)S(1)}, u32[]{:S(2)}, u32[]{:S(2)}) collective-permute-start(bf16[4,72,384]{2,1,0:T(8,128)(2,1)S(1)} %get-tuple-element.182), channel_id=1, source_target_pairs={{0,1},{1,0},{2,3},{3,2},{4,5},{5,4},{6,7},{7,6},{8,9},{9,8},{10,11... | collective-permute-start | bytes 663560 | tf_op jit(solution)/shard_map/ppermute | solution.py:630
  161.6 15.2 %collective-permute-start.22 = (bf16[1,216,768]{2,1,0:T(8,128)(2,1)S(1)}, bf16[1,216,768]{2,1,0:T(8,128)(2,1)S(1)}, u32[]{:S(2)}, u32[]{:S(2)}) collective-permute-start(bf16[1,216,768]{2,1,0:T(8,128)(2,1)S(1)} %get-tuple-element.175), channel_id=1, source_target_pairs={{0,8},{1,9},{2,10},{3,11},{4,12},{5,13},{6,14},{7,15},{8,0},{9,1},... | collective-permute-start | bytes 995336 | tf_op jit(solution)/shard_map/ppermute | solution.py:630
  167.5 15.1 %collective-permute-start.23 = (bf16[3,144,384]{2,1,0:T(8,128)(2,1)S(1)}, bf16[3,144,384]{2,1,0:T(8,128)(2,1)S(1)}, u32[]{:S(2)}, u32[]{:S(2)}) collective-permute-start(bf16[3,144,384]{2,1,0:T(8,128)(2,1)S(1)} %get-tuple-element.186), channel_id=1, source_target_pairs={{0,4},{1,5},{2,6},{3,7},{4,0},{5,1},{6,2},{7,3},{8,12},{9,13},{10,... | collective-permute-start | bytes 995336 | tf_op jit(solution)/shard_map/ppermute | solution.py:630
  182.7 10.7 %collective-permute-start.24 = (bf16[2,144,384]{2,1,0:T(8,128)(2,1)S(1)}, bf16[2,144,384]{2,1,0:T(8,128)(2,1)S(1)}, u32[]{:S(2)}, u32[]{:S(2)}) collective-permute-start(bf16[2,144,384]{2,1,0:T(8,128)(2,1)S(1)} %get-tuple-element.189), channel_id=1, source_target_pairs={{0,8},{1,9},{2,10},{3,11},{4,12},{5,13},{6,14},{7,15},{8,0},{9,1},... | collective-permute-start | bytes 663560 | tf_op jit(solution)/shard_map/ppermute | solution.py:630
  (10 other events, 63.1 us)

commit v5 on v4

--- a/solution.py
+++ b/solution.py
@@ -581,10 +581,9 @@
     )(info, dq, keep, got, *tables, h1t, wqkv, sums)
 
 
-def finish_kernel(parts, x, dx2, wqkv, gain_line, *refs):
+def finish_kernel(parts, tiles, x, dx2, wqkv, gain_line, *refs):
     dx_any, dx, sem = refs[-3:]
     dqs, dkvs = refs[:parts], refs[parts : 2 * parts]
-    tiles = sem.shape[0]
     gain = gain_line[...].reshape(1, x.shape[1])
 
     def store(t):
@@ -600,22 +599,25 @@
         store(t).start()
         return carry
 
-    lax.fori_loop(0, tiles, some_rows, 0)
-    for t in range(tiles):
+    lax.fori_loop(*tiles, some_rows, 0)
+    for t in range(*tiles):
         store(t).wait()
 
 
-def finish(x, dx2, dqs, dkvs, weight, gain):
+def finish(tiles, x, dx2, dqs, dkvs, weight, gain, before):
+    anywhere = pl.BlockSpec(memory_space=pl.ANY)
+    ins = 4 + len(dqs) + len(dkvs)
     return pl.pallas_call(
-        functools.partial(finish_kernel, len(dqs)),
-        in_specs=[IN_VMEM] * (4 + len(dqs) + len(dkvs)),
-        out_specs=pl.BlockSpec(memory_space=pl.ANY),
+        functools.partial(finish_kernel, len(dqs), tiles),
+        in_specs=[IN_VMEM] * ins + [anywhere] * len(before),
+        out_specs=anywhere,
         out_shape=shape(x.shape, bf16),
         scratch_shapes=[pltpu.VMEM(x.shape, bf16), pltpu.SemaphoreType.DMA((x.shape[0] // R,))],
+        input_output_aliases={ins: 0} if before else {},
         compiler_params=params(24),
-        cost_estimate=LONG,
+        cost_estimate=COST if before else LONG,
         name="finish",
-    )(x, dx2, weight, gain, *dqs, *dkvs)
+    )(x, dx2, weight, gain, *dqs, *dkvs, *before)
 
 
 def bit_orders(count, groups):
@@ -760,7 +762,7 @@
         out_specs=[IN_VMEM] * (len(sums) + len(small[:1])),
         out_shape=sums + [shape(a.shape, f32) for a in small[:1]],
         compiler_params=params(16),
-        cost_estimate=COST if small else LONG,
+        cost_estimate=COST if small or half == 1 else LONG,
         name="step_sum",
     )(*args)
     return list(outs[0 : len(sums) : 2]), list(outs[1 : len(sums) : 2]), list(outs[len(sums) :])
@@ -909,13 +911,16 @@
         [small, small_got],
         rides,
     )
-    token, came = next(late)
-    dx = finish(after(x, token), dx2, [dq1, dq2], [dkv1, dkv2], qkv_weight, attn_gain)
-    early_out = early.send((dx, came))
-    late_out = late.send(early_out[0])
+    token = next(late)[0]
+    ends = [dq1, dq2], [dkv1, dkv2], qkv_weight, attn_gain
+    tiles = seq // R
+    dx = finish((0, tiles // 2), after(x, token), dx2, *ends, [])
+    early_out = early.send(dx)
+    dx = finish((tiles // 2, tiles), x, after(dx2, early_out[0]), *ends, [dx])
+    late.send(dx)
+    late_out = late.send(early_out[1])
     while len(late_out) == 2:
-        last = late_out[0].shape[0] <= 3
-        late_out = late.send(early_out[1] if last and len(early_out) == 2 else None)
+        late_out = late.send(None)
     while len(early_out) == 2:
         early_out = early.send(None)
     up_cols = down_keep.shape[0] // count

time: 195 us -> 189 us (0.969)
  waiting for transfers between devices: 43.6 us -> 35.2 us
    ppermute x22, waiting for transfers between devices: 41.7 us -> 33.3 us  [exchange(): return lax.ppermute(value, axis, [(i, i ^ bit) for i in range(size)])]
    pallas_call x1 -> x2, Pallas kernels: 6.34 us -> 7.05 us  [finish(): pl.pallas_call(functools.partial(finish_kernel, len(dqs), tiles), in_spec...]
  transfers between devices with their start and end apart: 25 -> 25, of which waited for: 11 -> 12; matrix products, arithmetic and copies ran while one was open for 1% -> 1% of each run, Pallas kernels for 25% -> 26%
where the time goes in v5:
time: 189 us
  Pallas kernels  121 us (64%)
  waiting for transfers between devices  35.2 us (19%)
  starting transfers between devices  26.5 us (14%)
  local copies, waits for them, and re-layouts  3.51 us (2%)
    pallas_call x1, Pallas kernels, layer(): pl.pallas_call(layer_kernel, in_specs=[SMEM, IN_VMEM, IN_VMEM] + [anywher...  71.5 us
    ppermute x22, waiting for transfers between devices, exchange(): return lax.ppermute(value, axis, [(i, i ^ bit) for i in range(size)])  33.3 us
    pallas_call x2, Pallas kernels, attend_back(): pl.pallas_call(attend_back_kernel, grid=(pairs,), in_specs=[SMEM] + [head...  27.8 us
    ppermute x22, starting transfers between devices, exchange(): return lax.ppermute(value, axis, [(i, i ^ bit) for i in range(size)])  20.9 us
    pallas_call x2, Pallas kernels, weigh(): pl.pallas_call(functools.partial(weigh_kernel, first), in_specs=[SMEM] +...  7.28 us
    pallas_call x2, Pallas kernels, finish(): pl.pallas_call(functools.partial(finish_kernel, len(dqs), tiles), in_spec...  7.05 us
    pallas_call x2, Pallas kernels, start_sum(): pl.pallas_call(functools.partial(start_kernel, orders, sources, mode), co...  4.66 us
  transfers between devices with their start and end apart: 25, of which 12 were waited for; matrix products, arithmetic and copies ran while one was open for 1% of the time, Pallas kernels for 26%

profile of v5, /device:TPU:0, one launch (start us, length us, event | category | flops | bytes accessed | tf_op | source)
XLA Modules:
  0.0 188.8 jit_solution(12119628459990444733)
XLA Ops:
  0.6 2.5 %collective-permute-start = (bf16[1024,768]{1,0:T(8,128)(2,1)}, bf16[1024,768]{1,0:T(8,128)(2,1)S(1)}, u32[]{:S(2)}, u32[]{:S(2)}) collective-permute-start(bf16[1024,768]{1,0:T(8,128)(2,1)} %bitcast.20), channel_id=1, source_target_pairs={{0,16},{1,17},{2,18},{3,19},{4,20},{5,21},{6,22},{7,23},{8,24},{9,... | collective-permute-start | bytes 4718600 | tf_op jit(solution)/shard_map/ppermute | solution.py:868
  4.3 1.9 %collective-permute-done.received_any = bf16[1024,768]{1,0:T(8,128)(2,1)S(1)} collective-permute-done((bf16[1024,768]{1,0:T(8,128)(2,1)}, bf16[1024,768]{1,0:T(8,128)(2,1)S(1)}, u32[]{:S(2)}, u32[]{:S(2)}) %collective-permute-start) | collective-permute-done | bytes 1572896 | tf_op jit(solution)/shard_map/ppermute | solution.py:868
  6.2 1.1 copy-done.16
  7.4 71.5 %layer.1 = (bf16[6,1024,128]{2,1,0:T(8,128)(2,1)}, bf16[6,1024,128]{2,1,0:T(8,128)(2,1)}, bf16[6,1024,128]{2,1,0:T(8,128)(2,1)}, bf16[6,1024,128]{2,1,0:T(8,128)...) custom-call(s32[2]{0:T(128)} %pad_add_fusion.info, ...), custom_call_target="tpu_custom_call" | custom-call | flops 34359738368 | bytes 67108864 | tf_op jit(solution)/shard_map/layer/pallas_call | solution.py:517
  80.7 14.0 %attend_back.2 = (bf16[1024,384]{1,0:T(8,128)(2,1)S(1)}, bf16[2,1024,384]{2,1,0:T(8,128)(2,1)S(1)}, bf16[2,1024,384]{2,1,0:T(8,128)(2,1)S(1)}) custom-call(s32[2]{0:T(128)S(1)} %copy-done.11, bf16[6,1024,128]{2,1,0:T(8,128)(2,1)} %get-tuple-element.109.q, bf16[6,1024,128]{2,1,0:T(8,128)(2,1)} %get-tuple-element.110.ko, ...), custom_call_target="tpu_custom_call" | custom-call | flops 34359738368 | bytes 67108864 | tf_op jit(solution)/shard_map/attend_back/pallas_call | solution.py:272
  94.7 1.3 collective-permute-start.8
  96.0 3.9 %start_sum.2 = (bf16[8,72,768]{2,1,0:T(8,128)(2,1)S(1)}, bf16[8,72,768]{2,1,0:T(8,128)(2,1)S(1)}, bf16[8,72,768]{2,1,0:T(8,128)(2,1)S(1)}, bf16[8,72,768]{2,1,0:...) custom-call(s32[1]{0:T(128)} %bitcast.4.me, bf16[48,32,768]{2,1,0:T(8,128)(2,1)S(1)} %bitcast.17, ...), custom_call_target="tpu_custom_call" | custom-call | flops 1048576 | bytes 65536 | tf_op jit(solution)/shard_map/start_sum/pallas_call | solution.py:719
  100.0 2.4 %collective-permute-start.4 = (bf16[8,72,768]{2,1,0:T(8,128)(2,1)S(1)}, bf16[8,72,768]{2,1,0:T(8,128)(2,1)S(1)}, u32[]{:S(2)}, u32[]{:S(2)}) collective-permute-start(bf16[8,72,768]{2,1,0:T(8,128)(2,1)S(1)} %get-tuple-element.129), channel_id=1, source_target_pairs={{0,1},{1,0},{2,3},{3,2},{4,5},{5,4},{6,7},{7,6},{8,9},{9,8},{10,11... | collective-permute-start | bytes 2654216 | tf_op jit(solution)/shard_map/ppermute | solution.py:632
  102.4 1.5 collective-permute-start.5
  103.9 1.6 collective-permute-start.6
  105.5 13.9 %attend_back.3 = (bf16[1024,384]{1,0:T(8,128)(2,1)S(1)}, bf16[2,1024,384]{2,1,0:T(8,128)(2,1)S(1)}, bf16[2,1024,384]{2,1,0:T(8,128)(2,1)S(1)}) custom-call(s32[2]{0:T(128)S(1)} %copy-done.11, bf16[6,1024,128]{2,1,0:T(8,128)(2,1)} %get-tuple-element.109.q, bf16[6,1024,128]{2,1,0:T(8,128)(2,1)} %get-tuple-element.110.ko, ...), custom_call_target="tpu_custom_call" | custom-call | flops 34359738368 | bytes 67108864 | tf_op jit(solution)/shard_map/attend_back/pallas_call | solution.py:272
  119.4 1.8 collective-permute-start.7
  121.2 3.7 %collective-permute-done.5.refs_4_ = bf16[8,72,768]{2,1,0:T(8,128)(2,1)S(1)} collective-permute-done((bf16[8,72,768]{2,1,0:T(8,128)(2,1)S(1)}, bf16[8,72,768]{2,1,0:T(8,128)(2,1)S(1)}, u32[]{:S(2)}, u32[]{:S(2)}) %collective-permute-start.5) | collective-permute-done | bytes 884768 | tf_op jit(solution)/shard_map/ppermute | solution.py:632
  124.9 1.2 collective-permute-done.6.refs_5_
  127.3 1.6 collective-permute-start.10
  129.4 3.6 %weigh.2 = (bf16[2,1024,384]{2,1,0:T(8,128)(2,1)S(1)}, bf16[3,384,384]{2,1,0:T(8,128)(2,1)S(1)}, bf16[3,384,384]{2,1,0:T(8,128)(2,1)S(1)}, f32[8,768]{1,0:T(8,128)S(1)}) custom-call(s32[2]{0:T(128)S(1)} %copy-done.11, bf16[1024,384]{1,0:T(8,128)(2,1)S(1)} %get-tuple-element.117.dq.refs_0_, bf16[2,1024,384]{2,1,0:T(8,128)(2,1)S(1)} %get-tuple-element.145.keep, ...), custom_call_target="tpu_custom_call" | custom-call | flops 34359738368 | bytes 67108864 | tf_op jit(solution)/shard_map/weigh/pallas_call | solution.py:571
  133.1 3.7 %weigh.3 = (bf16[2,1024,384]{2,1,0:T(8,128)(2,1)S(1)}, bf16[3,384,384]{2,1,0:T(8,128)(2,1)S(1)}, bf16[3,384,384]{2,1,0:T(8,128)(2,1)S(1)}, f32[8,768]{1,0:T(8,128)S(1)}) custom-call(s32[2]{0:T(128)S(1)} %copy-done.11, bf16[1024,384]{1,0:T(8,128)(2,1)S(1)} %get-tuple-element.131.dq.refs_1_, bf16[2,1024,384]{2,1,0:T(8,128)(2,1)S(1)} %get-tuple-element.140.keep, ...), custom_call_target="tpu_custom_call" | custom-call | flops 34359738368 | bytes 67108864 | tf_op jit(solution)/shard_map/weigh/pallas_call | solution.py:571
  137.3 1.6 collective-permute-done.10.refs_4_
  138.9 1.3 collective-permute-done.11.refs_5_
  141.7 1.4 collective-permute-start.17
  143.8 1.6 collective-permute-start.18
  146.0 3.5 %finish.2.refs_4_ = bf16[1024,768]{1,0:T(8,128)(2,1)} custom-call(bf16[1024,768]{1,0:T(8,128)(2,1)S(1)} %bitcast.22, f32[1024,768]{1,0:T(8,128)S(1)} %copy-done.1, bf16[768,2304]{1,0:T(8,128)(2,1)S(1)} %copy-done, f32[768]{0:T(1024)S(1)} %copy-done.6, bf16[1024,384]{1,0:T(8,128)(2,1)S(1)} %get-tuple-element.117.dq.refs_0_, ...), custom_call_target="tpu_custom_call" | custom-call | flops 34359738368 | bytes 67108864 | tf_op jit(solution)/shard_map/finish/pallas_call | solution.py:610
  150.2 2.6 %collective-permute-start.20 = (bf16[1,216,768]{2,1,0:T(8,128)(2,1)S(1)}, bf16[1,216,768]{2,1,0:T(8,128)(2,1)S(1)}, u32[]{:S(2)}, u32[]{:S(2)}) collective-permute-start(bf16[1,216,768]{2,1,0:T(8,128)(2,1)S(1)} %get-tuple-element.174), channel_id=1, source_target_pairs={{0,8},{1,9},{2,10},{3,11},{4,12},{5,13},{6,14},{7,15},{8,0},{9,1},... | collective-permute-start | bytes 995336 | tf_op jit(solution)/shard_map/ppermute | solution.py:632
  152.7 3.5 %finish.3 = bf16[1024,768]{1,0:T(8,128)(2,1)} custom-call(bf16[1024,768]{1,0:T(8,128)(2,1)S(1)} %bitcast.23, f32[1024,768]{1,0:T(8,128)S(1)} %copy-done.1, bf16[768,2304]{1,0:T(8,128)(2,1)S(1)} %copy-done, f32[768]{0:T(1024)S(1)} %copy-done.6, bf16[1024,384]{1,0:T(8,128)(2,1)S(1)} %get-tuple-element.117.dq.refs_0_, ...), custom_call_target="tpu_custom_call", output_to_operand_aliasing={{}: (8, {})} | custom-call | flops 1048576 | bytes 65536 | tf_op jit(solution)/shard_map/finish/pallas_call | solution.py:610
  156.3 1.9 %collective-permute-done.19.refs_3_ = bf16[8,72,384]{2,1,0:T(8,128)(2,1)S(1)} collective-permute-done((bf16[8,72,384]{2,1,0:T(8,128)(2,1)S(1)}, bf16[8,72,384]{2,1,0:T(8,128)(2,1)S(1)}, u32[]{:S(2)}, u32[]{:S(2)}) %collective-permute-start.19) | collective-permute-done | bytes 442400 | tf_op jit(solution)/shard_map/ppermute | solution.py:632
  158.2 0.9 collective-permute-done.18.refs_2_
  159.4 1.5 collective-permute-start.21
  161.5 4.8 %collective-permute-done.20.got = bf16[1,216,768]{2,1,0:T(8,128)(2,1)S(1)} collective-permute-done((bf16[1,216,768]{2,1,0:T(8,128)(2,1)S(1)}, bf16[1,216,768]{2,1,0:T(8,128)(2,1)S(1)}, u32[]{:S(2)}, u32[]{:S(2)}) %collective-permute-start.20) | collective-permute-done | bytes 331808 | tf_op jit(solution)/shard_map/ppermute | solution.py:632
  166.3 0.9 collective-permute-done.22.refs_3_
  167.5 8.7 %collective-permute-done.23.refs_1_ = bf16[3,144,384]{2,1,0:T(8,128)(2,1)S(1)} collective-permute-done((bf16[3,144,384]{2,1,0:T(8,128)(2,1)S(1)}, bf16[3,144,384]{2,1,0:T(8,128)(2,1)S(1)}, u32[]{:S(2)}, u32[]{:S(2)}) %collective-permute-start.23) | collective-permute-done | bytes 331808 | tf_op jit(solution)/shard_map/ppermute | solution.py:632
  176.3 1.8 collective-permute-start.24
  179.8 7.7 %collective-permute-done.24.got = bf16[2,144,384]{2,1,0:T(8,128)(2,1)S(1)} collective-permute-done((bf16[2,144,384]{2,1,0:T(8,128)(2,1)S(1)}, bf16[2,144,384]{2,1,0:T(8,128)(2,1)S(1)}, u32[]{:S(2)}, u32[]{:S(2)}) %collective-permute-start.24) | collective-permute-done | bytes 221216 | tf_op jit(solution)/shard_map/ppermute | solution.py:632
  (72 shorter events, 12.3 us)
Async XLA Ops:
  0.6 5.6 %collective-permute-start = (bf16[1024,768]{1,0:T(8,128)(2,1)}, bf16[1024,768]{1,0:T(8,128)(2,1)S(1)}, u32[]{:S(2)}, u32[]{:S(2)}) collective-permute-start(bf16[1024,768]{1,0:T(8,128)(2,1)} %bitcast.20), channel_id=1, source_target_pairs={{0,16},{1,17},{2,18},{3,19},{4,20},{5,21},{6,22},{7,23},{8,24},{9,... | collective-permute-start | bytes 4718600 | tf_op jit(solution)/shard_map/ppermute | solution.py:868
  7.4 72.5 %copy-start.9 = (f32[32,1024]{1,0:T(8,128)S(1)}, f32[32,1024]{1,0:T(8,128)}, u32[]{:S(2)}) copy-start(f32[32,1024]{1,0:T(8,128)} %constant.20.clone.sine) | copy-start | bytes 393220
  7.4 72.5 %copy-start.10 = (f32[32,1024]{1,0:T(8,128)S(1)}, f32[32,1024]{1,0:T(8,128)}, u32[]{:S(2)}) copy-start(f32[32,1024]{1,0:T(8,128)} %constant.19.clone.cosine) | copy-start | bytes 393220
  7.4 72.5 %copy-start.11 = (s32[2]{0:T(128)S(1)}, s32[2]{0:T(128)}, u32[]{:S(2)}) copy-start(s32[2]{0:T(128)} %pad_add_fusion.info) | copy-start | bytes 28
  78.9 17.1 %collective-permute-start.3 = (bf16[384,768]{1,0:T(8,128)(2,1)}, bf16[384,768]{1,0:T(8,128)(2,1)S(1)}, u32[]{:S(2)}, u32[]{:S(2)}) collective-permute-start(bf16[384,768]{1,0:T(8,128)(2,1)} %get-tuple-element.125), channel_id=1, source_target_pairs={{0,16},{16,0},{1,17},{17,1},{2,18},{18,2},{3,19},{19,3},{4,20},{20... | collective-permute-start | bytes 1769480 | tf_op jit(solution)/shard_map/ppermute | solution.py:632
  79.3 16.6 %collective-permute-start.1 = (bf16[1536,768]{1,0:T(8,128)(2,1)}, bf16[1536,768]{1,0:T(8,128)(2,1)S(1)}, u32[]{:S(2)}, u32[]{:S(2)}) collective-permute-start(bf16[1536,768]{1,0:T(8,128)(2,1)} %get-tuple-element.119), channel_id=1, source_target_pairs={{0,16},{16,0},{1,17},{17,1},{2,18},{18,2},{3,19},{19,3},{4,20},{20... | collective-permute-start | bytes 7077896 | tf_op jit(solution)/shard_map/ppermute | solution.py:632
  79.5 16.5 %collective-permute-start.2 = (bf16[1536,768]{1,0:T(8,128)(2,1)}, bf16[1536,768]{1,0:T(8,128)(2,1)S(1)}, u32[]{:S(2)}, u32[]{:S(2)}) collective-permute-start(bf16[1536,768]{1,0:T(8,128)(2,1)} %get-tuple-element.122), channel_id=1, source_target_pairs={{0,16},{16,0},{1,17},{17,1},{2,18},{18,2},{3,19},{19,3},{4,20},{20... | collective-permute-start | bytes 7077896 | tf_op jit(solution)/shard_map/ppermute | solution.py:632
  80.7 15.3 %copy-start.2 = (bf16[1536,768]{1,0:T(8,128)(2,1)S(1)}, bf16[1536,768]{1,0:T(8,128)(2,1)}, u32[]{:S(2)}) copy-start(bf16[1536,768]{1,0:T(8,128)(2,1)} %get-tuple-element.121) | copy-start | bytes 7077892
  80.7 15.3 %copy-start.3 = (bf16[1536,768]{1,0:T(8,128)(2,1)S(1)}, bf16[1536,768]{1,0:T(8,128)(2,1)}, u32[]{:S(2)}) copy-start(bf16[1536,768]{1,0:T(8,128)(2,1)} %get-tuple-element.118) | copy-start | bytes 7077892
  80.7 15.4 %copy-start.5 = (bf16[384,768]{1,0:T(8,128)(2,1)S(1)}, bf16[384,768]{1,0:T(8,128)(2,1)}, u32[]{:S(2)}) copy-start(bf16[384,768]{1,0:T(8,128)(2,1)} %get-tuple-element.124) | copy-start | bytes 1769476
  94.7 34.7 %collective-permute-start.8 = (bf16[2,1024,384]{2,1,0:T(8,128)(2,1)S(1)}, bf16[2,1024,384]{2,1,0:T(8,128)(2,1)S(1)}, u32[]{:S(2)}, u32[]{:S(2)}) collective-permute-start(bf16[2,1024,384]{2,1,0:T(8,128)(2,1)S(1)} %get-tuple-element.146), channel_id=1, source_target_pairs={{16,0},{17,1},{18,2},{19,3},{20,4},{21,5},{22,6},{23,7},{24,8},{25... | collective-permute-start | bytes 4718600 | tf_op jit(solution)/shard_map/ppermute | solution.py:883
  100.0 26.1 %collective-permute-start.4 = (bf16[8,72,768]{2,1,0:T(8,128)(2,1)S(1)}, bf16[8,72,768]{2,1,0:T(8,128)(2,1)S(1)}, u32[]{:S(2)}, u32[]{:S(2)}) collective-permute-start(bf16[8,72,768]{2,1,0:T(8,128)(2,1)S(1)} %get-tuple-element.129), channel_id=1, source_target_pairs={{0,1},{1,0},{2,3},{3,2},{4,5},{5,4},{6,7},{7,6},{8,9},{9,8},{10,11... | collective-permute-start | bytes 2654216 | tf_op jit(solution)/shard_map/ppermute | solution.py:632
  102.4 22.5 %collective-permute-start.5 = (bf16[8,72,768]{2,1,0:T(8,128)(2,1)S(1)}, bf16[8,72,768]{2,1,0:T(8,128)(2,1)S(1)}, u32[]{:S(2)}, u32[]{:S(2)}) collective-permute-start(bf16[8,72,768]{2,1,0:T(8,128)(2,1)S(1)} %get-tuple-element.135), channel_id=1, source_target_pairs={{0,2},{1,3},{2,0},{3,1},{4,6},{5,7},{6,4},{7,5},{8,10},{9,11},{10,... | collective-permute-start | bytes 2654216 | tf_op jit(solution)/shard_map/ppermute | solution.py:632
  103.9 22.2 %collective-permute-start.6 = (bf16[8,72,768]{2,1,0:T(8,128)(2,1)S(1)}, bf16[8,72,768]{2,1,0:T(8,128)(2,1)S(1)}, u32[]{:S(2)}, u32[]{:S(2)}) collective-permute-start(bf16[8,72,768]{2,1,0:T(8,128)(2,1)S(1)} %get-tuple-element.136), channel_id=1, source_target_pairs={{0,4},{1,5},{2,6},{3,7},{4,0},{5,1},{6,2},{7,3},{8,12},{9,13},{10,... | collective-permute-start | bytes 2654216 | tf_op jit(solution)/shard_map/ppermute | solution.py:632
  119.3 10.0 %copy-start = (bf16[768,2304]{1,0:T(8,128)(2,1)S(1)}, bf16[768,2304]{1,0:T(8,128)(2,1)}, u32[]{:S(2)}) copy-start(bf16[768,2304]{1,0:T(8,128)(2,1)} %wqkv.7) | copy-start | bytes 10616836
  119.4 13.7 %collective-permute-start.7 = (bf16[2,1024,384]{2,1,0:T(8,128)(2,1)S(1)}, bf16[2,1024,384]{2,1,0:T(8,128)(2,1)S(1)}, u32[]{:S(2)}, u32[]{:S(2)}) collective-permute-start(bf16[2,1024,384]{2,1,0:T(8,128)(2,1)S(1)} %get-tuple-element.141), channel_id=1, source_target_pairs={{16,0},{17,1},{18,2},{19,3},{20,4},{21,5},{22,6},{23,7},{24,8},{25... | collective-permute-start | bytes 4718600 | tf_op jit(solution)/shard_map/ppermute | solution.py:894
  126.7 13.5 %collective-permute-start.9 = (bf16[4,72,768]{2,1,0:T(8,128)(2,1)S(1)}, bf16[4,72,768]{2,1,0:T(8,128)(2,1)S(1)}, u32[]{:S(2)}, u32[]{:S(2)}) collective-permute-start(bf16[4,72,768]{2,1,0:T(8,128)(2,1)S(1)} %get-tuple-element.144), channel_id=1, source_target_pairs={{0,2},{1,3},{2,0},{3,1},{4,6},{5,7},{6,4},{7,5},{8,10},{9,11},{10,... | collective-permute-start | bytes 1327112 | tf_op jit(solution)/shard_map/ppermute | solution.py:632
  127.3 11.6 %collective-permute-start.10 = (bf16[4,72,768]{2,1,0:T(8,128)(2,1)S(1)}, bf16[4,72,768]{2,1,0:T(8,128)(2,1)S(1)}, u32[]{:S(2)}, u32[]{:S(2)}) collective-permute-start(bf16[4,72,768]{2,1,0:T(8,128)(2,1)S(1)} %get-tuple-element.153), channel_id=1, source_target_pairs={{0,4},{1,5},{2,6},{3,7},{4,0},{5,1},{6,2},{7,3},{8,12},{9,13},{10,... | collective-permute-start | bytes 1327112 | tf_op jit(solution)/shard_map/ppermute | solution.py:632
  128.9 11.4 %collective-permute-start.11 = (bf16[4,72,768]{2,1,0:T(8,128)(2,1)S(1)}, bf16[4,72,768]{2,1,0:T(8,128)(2,1)S(1)}, u32[]{:S(2)}, u32[]{:S(2)}) collective-permute-start(bf16[4,72,768]{2,1,0:T(8,128)(2,1)S(1)} %get-tuple-element.154), channel_id=1, source_target_pairs={{0,1},{1,0},{2,3},{3,2},{4,5},{5,4},{6,7},{7,6},{8,9},{9,8},{10,11... | collective-permute-start | bytes 1327112 | tf_op jit(solution)/shard_map/ppermute | solution.py:632
  133.0 10.1 %collective-permute-start.12 = (bf16[3,384,384]{2,1,0:T(8,128)(2,1)S(1)}, bf16[3,384,384]{2,1,0:T(8,128)(2,1)S(1)}, u32[]{:S(2)}, u32[]{:S(2)}) collective-permute-start(bf16[3,384,384]{2,1,0:T(8,128)(2,1)S(1)} %get-tuple-element.161), channel_id=1, source_target_pairs={{0,16},{16,0},{1,17},{17,1},{2,18},{18,2},{3,19},{19,3},{4,20},{20... | collective-permute-start | bytes 2654216 | tf_op jit(solution)/shard_map/ppermute | solution.py:632
  136.8 4.9 %collective-permute-start.14 = (f32[8,768]{1,0:T(8,128)S(1)}, f32[8,768]{1,0:T(8,128)S(1)}, u32[]{:S(2)}, u32[]{:S(2)}) collective-permute-start(f32[8,768]{1,0:T(8,128)S(1)} %get-tuple-element.165.refs_4_), channel_id=1, source_target_pairs={{0,16},{16,0},{1,17},{17,1},{2,18},{18,2},{3,19},{19,3},{4,20},{20... | collective-permute-start | bytes 73736 | tf_op jit(solution)/shard_map/ppermute | solution.py:632
  138.9 4.2 %collective-permute-start.13 = (bf16[3,384,384]{2,1,0:T(8,128)(2,1)S(1)}, bf16[3,384,384]{2,1,0:T(8,128)(2,1)S(1)}, u32[]{:S(2)}, u32[]{:S(2)}) collective-permute-start(bf16[3,384,384]{2,1,0:T(8,128)(2,1)S(1)} %get-tuple-element.164), channel_id=1, source_target_pairs={{0,16},{16,0},{1,17},{17,1},{2,18},{18,2},{3,19},{19,3},{4,20},{20... | collective-permute-start | bytes 2654216 | tf_op jit(solution)/shard_map/ppermute | solution.py:632
  140.6 9.4 %collective-permute-start.15 = (bf16[2,72,768]{2,1,0:T(8,128)(2,1)S(1)}, bf16[2,72,768]{2,1,0:T(8,128)(2,1)S(1)}, u32[]{:S(2)}, u32[]{:S(2)}) collective-permute-start(bf16[2,72,768]{2,1,0:T(8,128)(2,1)S(1)} %get-tuple-element.159), channel_id=1, source_target_pairs={{0,4},{1,5},{2,6},{3,7},{4,0},{5,1},{6,2},{7,3},{8,12},{9,13},{10,... | collective-permute-start | bytes 663560 | tf_op jit(solution)/shard_map/ppermute | solution.py:632
  141.1 8.4 %collective-permute-start.16 = (bf16[2,72,768]{2,1,0:T(8,128)(2,1)S(1)}, bf16[2,72,768]{2,1,0:T(8,128)(2,1)S(1)}, u32[]{:S(2)}, u32[]{:S(2)}) collective-permute-start(bf16[2,72,768]{2,1,0:T(8,128)(2,1)S(1)} %get-tuple-element.172), channel_id=1, source_target_pairs={{0,1},{1,0},{2,3},{3,2},{4,5},{5,4},{6,7},{7,6},{8,9},{9,8},{10,11... | collective-permute-start | bytes 663560 | tf_op jit(solution)/shard_map/ppermute | solution.py:632
  141.7 8.3 %collective-permute-start.17 = (bf16[2,72,768]{2,1,0:T(8,128)(2,1)S(1)}, bf16[2,72,768]{2,1,0:T(8,128)(2,1)S(1)}, u32[]{:S(2)}, u32[]{:S(2)}) collective-permute-start(bf16[2,72,768]{2,1,0:T(8,128)(2,1)S(1)} %get-tuple-element.173), channel_id=1, source_target_pairs={{0,2},{1,3},{2,0},{3,1},{4,6},{5,7},{6,4},{7,5},{8,10},{9,11},{10,... | collective-permute-start | bytes 663560 | tf_op jit(solution)/shard_map/ppermute | solution.py:632
  143.8 15.3 %collective-permute-start.18 = (bf16[9,72,384]{2,1,0:T(8,128)(2,1)S(1)}, bf16[9,72,384]{2,1,0:T(8,128)(2,1)S(1)}, u32[]{:S(2)}, u32[]{:S(2)}) collective-permute-start(bf16[9,72,384]{2,1,0:T(8,128)(2,1)S(1)} %get-tuple-element.166), channel_id=1, source_target_pairs={{0,1},{1,0},{2,3},{3,2},{4,5},{5,4},{6,7},{7,6},{8,9},{9,8},{10,11... | collective-permute-start | bytes 1493000 | tf_op jit(solution)/shard_map/ppermute | solution.py:632
  145.4 12.8 %collective-permute-start.19 = (bf16[8,72,384]{2,1,0:T(8,128)(2,1)S(1)}, bf16[8,72,384]{2,1,0:T(8,128)(2,1)S(1)}, u32[]{:S(2)}, u32[]{:S(2)}) collective-permute-start(bf16[8,72,384]{2,1,0:T(8,128)(2,1)S(1)} %get-tuple-element.180), channel_id=1, source_target_pairs={{0,2},{1,3},{2,0},{3,1},{4,6},{5,7},{6,4},{7,5},{8,10},{9,11},{10,... | collective-permute-start | bytes 1327112 | tf_op jit(solution)/shard_map/ppermute | solution.py:632
  150.2 16.1 %collective-permute-start.20 = (bf16[1,216,768]{2,1,0:T(8,128)(2,1)S(1)}, bf16[1,216,768]{2,1,0:T(8,128)(2,1)S(1)}, u32[]{:S(2)}, u32[]{:S(2)}) collective-permute-start(bf16[1,216,768]{2,1,0:T(8,128)(2,1)S(1)} %get-tuple-element.174), channel_id=1, source_target_pairs={{0,8},{1,9},{2,10},{3,11},{4,12},{5,13},{6,14},{7,15},{8,0},{9,1},... | collective-permute-start | bytes 995336 | tf_op jit(solution)/shard_map/ppermute | solution.py:632
  159.4 7.8 %collective-permute-start.21 = (bf16[5,72,384]{2,1,0:T(8,128)(2,1)S(1)}, bf16[5,72,384]{2,1,0:T(8,128)(2,1)S(1)}, u32[]{:S(2)}, u32[]{:S(2)}) collective-permute-start(bf16[5,72,384]{2,1,0:T(8,128)(2,1)S(1)} %get-tuple-element.186), channel_id=1, source_target_pairs={{0,2},{1,3},{2,0},{3,1},{4,6},{5,7},{6,4},{7,5},{8,10},{9,11},{10,... | collective-permute-start | bytes 829448 | tf_op jit(solution)/shard_map/ppermute | solution.py:632
  160.9 6.3 %collective-permute-start.22 = (bf16[4,72,384]{2,1,0:T(8,128)(2,1)S(1)}, bf16[4,72,384]{2,1,0:T(8,128)(2,1)S(1)}, u32[]{:S(2)}, u32[]{:S(2)}) collective-permute-start(bf16[4,72,384]{2,1,0:T(8,128)(2,1)S(1)} %get-tuple-element.187), channel_id=1, source_target_pairs={{0,1},{1,0},{2,3},{3,2},{4,5},{5,4},{6,7},{7,6},{8,9},{9,8},{10,11... | collective-permute-start | bytes 663560 | tf_op jit(solution)/shard_map/ppermute | solution.py:632
  167.3 8.9 %collective-permute-start.23 = (bf16[3,144,384]{2,1,0:T(8,128)(2,1)S(1)}, bf16[3,144,384]{2,1,0:T(8,128)(2,1)S(1)}, u32[]{:S(2)}, u32[]{:S(2)}) collective-permute-start(bf16[3,144,384]{2,1,0:T(8,128)(2,1)S(1)} %get-tuple-element.190), channel_id=1, source_target_pairs={{0,4},{1,5},{2,6},{3,7},{4,0},{5,1},{6,2},{7,3},{8,12},{9,13},{10,... | collective-permute-start | bytes 995336 | tf_op jit(solution)/shard_map/ppermute | solution.py:632
  176.3 11.2 %collective-permute-start.24 = (bf16[2,144,384]{2,1,0:T(8,128)(2,1)S(1)}, bf16[2,144,384]{2,1,0:T(8,128)(2,1)S(1)}, u32[]{:S(2)}, u32[]{:S(2)}) collective-permute-start(bf16[2,144,384]{2,1,0:T(8,128)(2,1)S(1)} %get-tuple-element.193), channel_id=1, source_target_pairs={{0,8},{1,9},{2,10},{3,11},{4,12},{5,13},{6,14},{7,15},{8,0},{9,1},... | collective-permute-start | bytes 663560 | tf_op jit(solution)/shard_map/ppermute | solution.py:632
  (10 other events, 63.0 us)

commit v6 on v5

--- a/solution.py
+++ b/solution.py
@@ -668,13 +668,18 @@
 
             def one(r, carry, g=g, order=order, side=side):
                 part = me[0] ^ distance(order, r + side * half)
+                out = outs[2 * g + side]
                 row = 0
                 for a, where in sources[g]:
                     kept, got = ins[2 * a : 2 * a + 2]
                     place = where(part)
                     size = kept.shape[1]
                     total = kept[place].astype(f32) + got[place].astype(f32)
-                    outs[2 * g + side][r, row : row + size, :] = total.astype(bf16)
+                    if len(out.shape) == 3:
+                        out[r, row : row + size, :] = total.astype(bf16)
+                    else:
+                        start = pl.multiple_of(r * outs[0].shape[1] + row, 8)
+                        out[pl.ds(start, size), :] = total.astype(bf16)
                     row += size
                 return carry
 
@@ -685,9 +690,13 @@
         if small == "rides":
             wide = total.shape[1] // 2
             total = jnp.concatenate([total[:, :wide], total[:, wide:]], axis=0)
-            put_sums(total, kept, outs[1].at[half])
+            put_sums(total, kept, outs[1].at[pl.ds(half * outs[0].shape[1], 2 * LINES), :])
         else:
             kept[...] = total
+
+
+def travelling(count, rows, width, rides):
+    return shape((count * rows + 2 * LINES, width) if rides else (count, rows, width), bf16)
 
 
 def start_sum(me, kept, got, sources, orders, small, rides):
@@ -699,7 +708,7 @@
     args = [a for pair in zip(kept, got, strict=True) for a in pair]
     sums = []
     for g in range(len(orders)):
-        sums += [shape((half, rows[g], width), bf16), shape((half + (rides and g == 0), rows[g], width), bf16)]
+        sums += [shape((half, rows[g], width), bf16), travelling(half, rows[g], width, rides and g == 0)]
     mode = "rides" if rides else "alone" if small else ""
     if small:
         lines = (LINES, width) if rides else small[0].shape
@@ -734,15 +743,22 @@
     half = count // 2
     row = 0
     for g in range(groups):
-        total = (kept[g][...].astype(f32) + got[g][:count].astype(f32)).astype(bf16)
         keep, send = outs[:2] if merge else outs[2 * g : 2 * g + 2]
-        size = total.shape[1]
-        keep[:, row : row + size, :] = total[:half]
-        send[:half, row : row + size, :] = total[half:]
+        size = kept[g].shape[1]
+        for r in range(count):
+            there = got[g][r] if len(got[g].shape) == 3 else got[g][r * size : (r + 1) * size]
+            total = (kept[g][r].astype(f32) + there.astype(f32)).astype(bf16)
+            if r < half:
+                keep[r, row : row + size, :] = total
+            elif len(send.shape) == 3:
+                send[r - half, row : row + size, :] = total
+            else:
+                start = (r - half) * keep.shape[1] + row
+                send[start : start + size, :] = total
         row += size if merge else 0
     if mode == "rides":
-        total = refs[2 * groups][...] + got_sums(got[0].at[count])
-        put_sums(total, outs[-1], outs[1].at[half])
+        total = refs[2 * groups][...] + got_sums(got[0][count * kept[0].shape[1] :])
+        put_sums(total, outs[-1], outs[1].at[pl.ds(half * outs[0].shape[1], 2 * LINES), :])
     elif mode:
         outs[-1][...] = refs[2 * groups][...] + refs[2 * groups + 1][...]
 
@@ -755,7 +771,7 @@
     args = [*kept, *got, *small]
     sums = []
     for g, r in enumerate([sum(rows)] if merge else rows):
-        sums += [shape((half, r, width), bf16), shape((half + (rides and g == 0), r, width), bf16)]
+        sums += [shape((half, r, width), bf16), travelling(half, r, width, rides and g == 0)]
     outs = pl.pallas_call(
         functools.partial(step_kernel, groups, merge, "rides" if rides else "alone" if small else ""),
         in_specs=[IN_VMEM] * len(args),
@@ -798,13 +814,14 @@
     tall = out.shape[0]
     width = gain1.shape[0]
     cols = kept.shape[2]
-    total = kept[0].astype(f32) + got[0].astype(f32)
+    there = got[: kept.shape[1]] if rides else got[0]
+    total = kept[0].astype(f32) + there.astype(f32)
     for i in range(total.shape[0] // tall):
         part, third = i // 3, i % 3
         at = third * width + part * cols
         out[:, at : at + cols] = total[i * tall : (i + 1) * tall]
     if rides:
-        sums = refs[0][...] + got_sums(got.at[1])
+        sums = refs[0][...] + got_sums(got[kept.shape[1] :])
         sums = jnp.concatenate([sums[: LINES // 2], sums[LINES // 2 :]], axis=1)
     else:
         sums = refs[0][...] + refs[1][...]

time: 189 us -> 184 us (0.974)
  waiting for transfers between devices: 35.2 us -> 30.4 us
    ppermute x22, waiting for transfers between devices: 33.3 us -> 28.5 us  [exchange(): return lax.ppermute(value, axis, [(i, i ^ bit) for i in range(size)])]
  transfers between devices with their start and end apart: 25 -> 25, of which waited for: 12 -> 12; matrix products, arithmetic and copies ran while one was open for 1% -> 1% of each run, Pallas kernels for 26% -> 27%
where the time goes in v6:
time: 184 us
  Pallas kernels  121 us (66%)
  waiting for transfers between devices  30.4 us (17%)
  starting transfers between devices  26.5 us (14%)
  local copies, waits for them, and re-layouts  3.51 us (2%)
    pallas_call x1, Pallas kernels, layer(): pl.pallas_call(layer_kernel, in_specs=[SMEM, IN_VMEM, IN_VMEM] + [anywher...  71.5 us
    ppermute x22, waiting for transfers between devices, exchange(): return lax.ppermute(value, axis, [(i, i ^ bit) for i in range(size)])  28.5 us
    pallas_call x2, Pallas kernels, attend_back(): pl.pallas_call(attend_back_kernel, grid=(pairs,), in_specs=[SMEM] + [head...  27.8 us
    ppermute x22, starting transfers between devices, exchange(): return lax.ppermute(value, axis, [(i, i ^ bit) for i in range(size)])  21 us
    pallas_call x2, Pallas kernels, weigh(): pl.pallas_call(functools.partial(weigh_kernel, first), in_specs=[SMEM] +...  7.28 us
    pallas_call x2, Pallas kernels, finish(): pl.pallas_call(functools.partial(finish_kernel, len(dqs), tiles), in_spec...  7.05 us
    pallas_call x2, Pallas kernels, start_sum(): pl.pallas_call(functools.partial(start_kernel, orders, sources, mode), co...  4.67 us
  transfers between devices with their start and end apart: 25, of which 12 were waited for; matrix products, arithmetic and copies ran while one was open for 1% of the time, Pallas kernels for 27%

profile of v6, /device:TPU:0, one launch (start us, length us, event | category | flops | bytes accessed | tf_op | source)
XLA Modules:
  0.0 184.0 jit_solution(5386492842799070295)
XLA Ops:
  0.6 2.5 %collective-permute-start = (bf16[1024,768]{1,0:T(8,128)(2,1)}, bf16[1024,768]{1,0:T(8,128)(2,1)S(1)}, u32[]{:S(2)}, u32[]{:S(2)}) collective-permute-start(bf16[1024,768]{1,0:T(8,128)(2,1)} %bitcast.20), channel_id=1, source_target_pairs={{0,16},{1,17},{2,18},{3,19},{4,20},{5,21},{6,22},{7,23},{8,24},{9,... | collective-permute-start | bytes 4718600 | tf_op jit(solution)/shard_map/ppermute | solution.py:885
  4.3 1.9 %collective-permute-done.received_any = bf16[1024,768]{1,0:T(8,128)(2,1)S(1)} collective-permute-done((bf16[1024,768]{1,0:T(8,128)(2,1)}, bf16[1024,768]{1,0:T(8,128)(2,1)S(1)}, u32[]{:S(2)}, u32[]{:S(2)}) %collective-permute-start) | collective-permute-done | bytes 1572896 | tf_op jit(solution)/shard_map/ppermute | solution.py:885
  6.2 1.1 copy-done.16
  7.4 71.5 %layer.1 = (bf16[6,1024,128]{2,1,0:T(8,128)(2,1)}, bf16[6,1024,128]{2,1,0:T(8,128)(2,1)}, bf16[6,1024,128]{2,1,0:T(8,128)(2,1)}, bf16[6,1024,128]{2,1,0:T(8,128)...) custom-call(s32[2]{0:T(128)} %pad_add_fusion.info, ...), custom_call_target="tpu_custom_call" | custom-call | flops 34359738368 | bytes 67108864 | tf_op jit(solution)/shard_map/layer/pallas_call | solution.py:517
  80.7 14.0 %attend_back.2 = (bf16[1024,384]{1,0:T(8,128)(2,1)S(1)}, bf16[2,1024,384]{2,1,0:T(8,128)(2,1)S(1)}, bf16[2,1024,384]{2,1,0:T(8,128)(2,1)S(1)}) custom-call(s32[2]{0:T(128)S(1)} %copy-done.11, bf16[6,1024,128]{2,1,0:T(8,128)(2,1)} %get-tuple-element.109.q, bf16[6,1024,128]{2,1,0:T(8,128)(2,1)} %get-tuple-element.110.ko, ...), custom_call_target="tpu_custom_call" | custom-call | flops 34359738368 | bytes 67108864 | tf_op jit(solution)/shard_map/attend_back/pallas_call | solution.py:272
  94.7 1.3 collective-permute-start.8
  96.0 3.9 %start_sum.2 = (bf16[8,72,768]{2,1,0:T(8,128)(2,1)S(1)}, bf16[8,72,768]{2,1,0:T(8,128)(2,1)S(1)}, bf16[8,72,768]{2,1,0:T(8,128)(2,1)S(1)}, bf16[8,72,768]{2,1,0:...) custom-call(s32[1]{0:T(128)} %bitcast.4.me, bf16[48,32,768]{2,1,0:T(8,128)(2,1)S(1)} %bitcast.17, ...), custom_call_target="tpu_custom_call" | custom-call | flops 1048576 | bytes 65536 | tf_op jit(solution)/shard_map/start_sum/pallas_call | solution.py:728
  100.0 2.4 %collective-permute-start.4 = (bf16[8,72,768]{2,1,0:T(8,128)(2,1)S(1)}, bf16[8,72,768]{2,1,0:T(8,128)(2,1)S(1)}, u32[]{:S(2)}, u32[]{:S(2)}) collective-permute-start(bf16[8,72,768]{2,1,0:T(8,128)(2,1)S(1)} %get-tuple-element.129), channel_id=1, source_target_pairs={{0,1},{1,0},{2,3},{3,2},{4,5},{5,4},{6,7},{7,6},{8,9},{9,8},{10,11... | collective-permute-start | bytes 2654216 | tf_op jit(solution)/shard_map/ppermute | solution.py:632
  102.4 1.5 collective-permute-start.5
  103.9 1.6 collective-permute-start.6
  105.5 13.9 %attend_back.3 = (bf16[1024,384]{1,0:T(8,128)(2,1)S(1)}, bf16[2,1024,384]{2,1,0:T(8,128)(2,1)S(1)}, bf16[2,1024,384]{2,1,0:T(8,128)(2,1)S(1)}) custom-call(s32[2]{0:T(128)S(1)} %copy-done.11, bf16[6,1024,128]{2,1,0:T(8,128)(2,1)} %get-tuple-element.109.q, bf16[6,1024,128]{2,1,0:T(8,128)(2,1)} %get-tuple-element.110.ko, ...), custom_call_target="tpu_custom_call" | custom-call | flops 34359738368 | bytes 67108864 | tf_op jit(solution)/shard_map/attend_back/pallas_call | solution.py:272
  119.4 1.8 collective-permute-start.7
  121.2 3.7 %collective-permute-done.5.refs_4_ = bf16[8,72,768]{2,1,0:T(8,128)(2,1)S(1)} collective-permute-done((bf16[8,72,768]{2,1,0:T(8,128)(2,1)S(1)}, bf16[8,72,768]{2,1,0:T(8,128)(2,1)S(1)}, u32[]{:S(2)}, u32[]{:S(2)}) %collective-permute-start.5) | collective-permute-done | bytes 884768 | tf_op jit(solution)/shard_map/ppermute | solution.py:632
  124.9 1.2 collective-permute-done.6.refs_5_
  127.3 1.6 collective-permute-start.10
  129.4 3.6 %weigh.2 = (bf16[2,1024,384]{2,1,0:T(8,128)(2,1)S(1)}, bf16[3,384,384]{2,1,0:T(8,128)(2,1)S(1)}, bf16[3,384,384]{2,1,0:T(8,128)(2,1)S(1)}, f32[8,768]{1,0:T(8,128)S(1)}) custom-call(s32[2]{0:T(128)S(1)} %copy-done.11, bf16[1024,384]{1,0:T(8,128)(2,1)S(1)} %get-tuple-element.117.dq.refs_0_, bf16[2,1024,384]{2,1,0:T(8,128)(2,1)S(1)} %get-tuple-element.145.keep, ...), custom_call_target="tpu_custom_call" | custom-call | flops 34359738368 | bytes 67108864 | tf_op jit(solution)/shard_map/weigh/pallas_call | solution.py:571
  133.1 3.7 %weigh.3 = (bf16[2,1024,384]{2,1,0:T(8,128)(2,1)S(1)}, bf16[3,384,384]{2,1,0:T(8,128)(2,1)S(1)}, bf16[3,384,384]{2,1,0:T(8,128)(2,1)S(1)}, f32[8,768]{1,0:T(8,128)S(1)}) custom-call(s32[2]{0:T(128)S(1)} %copy-done.11, bf16[1024,384]{1,0:T(8,128)(2,1)S(1)} %get-tuple-element.131.dq.refs_1_, bf16[2,1024,384]{2,1,0:T(8,128)(2,1)S(1)} %get-tuple-element.140.keep, ...), custom_call_target="tpu_custom_call" | custom-call | flops 34359738368 | bytes 67108864 | tf_op jit(solution)/shard_map/weigh/pallas_call | solution.py:571
  137.3 1.6 collective-permute-done.10.refs_4_
  138.9 1.3 collective-permute-done.11.refs_5_
  141.7 1.4 collective-permute-start.17
  143.8 1.6 collective-permute-start.18
  146.0 3.5 %finish.2.refs_4_ = bf16[1024,768]{1,0:T(8,128)(2,1)} custom-call(bf16[1024,768]{1,0:T(8,128)(2,1)S(1)} %bitcast.22, f32[1024,768]{1,0:T(8,128)S(1)} %copy-done.1, bf16[768,2304]{1,0:T(8,128)(2,1)S(1)} %copy-done, f32[768]{0:T(1024)S(1)} %copy-done.6, bf16[1024,384]{1,0:T(8,128)(2,1)S(1)} %get-tuple-element.117.dq.refs_0_, ...), custom_call_target="tpu_custom_call" | custom-call | flops 34359738368 | bytes 67108864 | tf_op jit(solution)/shard_map/finish/pallas_call | solution.py:610
  150.2 2.6 %collective-permute-start.20 = (bf16[1,216,768]{2,1,0:T(8,128)(2,1)S(1)}, bf16[1,216,768]{2,1,0:T(8,128)(2,1)S(1)}, u32[]{:S(2)}, u32[]{:S(2)}) collective-permute-start(bf16[1,216,768]{2,1,0:T(8,128)(2,1)S(1)} %get-tuple-element.174), channel_id=1, source_target_pairs={{0,8},{1,9},{2,10},{3,11},{4,12},{5,13},{6,14},{7,15},{8,0},{9,1},... | collective-permute-start | bytes 995336 | tf_op jit(solution)/shard_map/ppermute | solution.py:632
  152.7 3.5 %finish.3 = bf16[1024,768]{1,0:T(8,128)(2,1)} custom-call(bf16[1024,768]{1,0:T(8,128)(2,1)S(1)} %bitcast.23, f32[1024,768]{1,0:T(8,128)S(1)} %copy-done.1, bf16[768,2304]{1,0:T(8,128)(2,1)S(1)} %copy-done, f32[768]{0:T(1024)S(1)} %copy-done.6, bf16[1024,384]{1,0:T(8,128)(2,1)S(1)} %get-tuple-element.117.dq.refs_0_, ...), custom_call_target="tpu_custom_call", output_to_operand_aliasing={{}: (8, {})} | custom-call | flops 1048576 | bytes 65536 | tf_op jit(solution)/shard_map/finish/pallas_call | solution.py:610
  156.3 1.9 %collective-permute-done.19.refs_3_ = bf16[8,72,384]{2,1,0:T(8,128)(2,1)S(1)} collective-permute-done((bf16[8,72,384]{2,1,0:T(8,128)(2,1)S(1)}, bf16[8,72,384]{2,1,0:T(8,128)(2,1)S(1)}, u32[]{:S(2)}, u32[]{:S(2)}) %collective-permute-start.19) | collective-permute-done | bytes 442400 | tf_op jit(solution)/shard_map/ppermute | solution.py:632
  158.7 1.5 collective-permute-start.21
  160.2 1.2 collective-permute-start.22
  161.5 4.8 %collective-permute-done.20.got = bf16[1,216,768]{2,1,0:T(8,128)(2,1)S(1)} collective-permute-done((bf16[1,216,768]{2,1,0:T(8,128)(2,1)S(1)}, bf16[1,216,768]{2,1,0:T(8,128)(2,1)S(1)}, u32[]{:S(2)}, u32[]{:S(2)}) %collective-permute-start.20) | collective-permute-done | bytes 331808 | tf_op jit(solution)/shard_map/ppermute | solution.py:632
  166.8 7.6 %collective-permute-done.23.refs_1_ = bf16[320,384]{1,0:T(8,128)(2,1)S(1)} collective-permute-done((bf16[320,384]{1,0:T(8,128)(2,1)S(1)}, bf16[320,384]{1,0:T(8,128)(2,1)S(1)}, u32[]{:S(2)}, u32[]{:S(2)}) %collective-permute-start.23) | collective-permute-done | bytes 245792 | tf_op jit(solution)/shard_map/ppermute | solution.py:632
  174.4 1.2 collective-permute-start.24
  175.6 0.9 feed_end.1
  177.4 5.3 %collective-permute-done.24.got = bf16[176,384]{1,0:T(8,128)(2,1)S(1)} collective-permute-done((bf16[176,384]{1,0:T(8,128)(2,1)S(1)}, bf16[176,384]{1,0:T(8,128)(2,1)S(1)}, u32[]{:S(2)}, u32[]{:S(2)}) %collective-permute-start.24) | collective-permute-done | bytes 135200 | tf_op jit(solution)/shard_map/ppermute | solution.py:632
  (72 shorter events, 11.4 us)
Async XLA Ops:
  0.6 5.6 %collective-permute-start = (bf16[1024,768]{1,0:T(8,128)(2,1)}, bf16[1024,768]{1,0:T(8,128)(2,1)S(1)}, u32[]{:S(2)}, u32[]{:S(2)}) collective-permute-start(bf16[1024,768]{1,0:T(8,128)(2,1)} %bitcast.20), channel_id=1, source_target_pairs={{0,16},{1,17},{2,18},{3,19},{4,20},{5,21},{6,22},{7,23},{8,24},{9,... | collective-permute-start | bytes 4718600 | tf_op jit(solution)/shard_map/ppermute | solution.py:885
  7.4 72.5 %copy-start.9 = (f32[32,1024]{1,0:T(8,128)S(1)}, f32[32,1024]{1,0:T(8,128)}, u32[]{:S(2)}) copy-start(f32[32,1024]{1,0:T(8,128)} %constant.20.clone.sine) | copy-start | bytes 393220
  7.4 72.5 %copy-start.10 = (f32[32,1024]{1,0:T(8,128)S(1)}, f32[32,1024]{1,0:T(8,128)}, u32[]{:S(2)}) copy-start(f32[32,1024]{1,0:T(8,128)} %constant.19.clone.cosine) | copy-start | bytes 393220
  7.4 72.5 %copy-start.11 = (s32[2]{0:T(128)S(1)}, s32[2]{0:T(128)}, u32[]{:S(2)}) copy-start(s32[2]{0:T(128)} %pad_add_fusion.info) | copy-start | bytes 28
  78.9 17.1 %collective-permute-start.3 = (bf16[384,768]{1,0:T(8,128)(2,1)}, bf16[384,768]{1,0:T(8,128)(2,1)S(1)}, u32[]{:S(2)}, u32[]{:S(2)}) collective-permute-start(bf16[384,768]{1,0:T(8,128)(2,1)} %get-tuple-element.125), channel_id=1, source_target_pairs={{0,16},{16,0},{1,17},{17,1},{2,18},{18,2},{3,19},{19,3},{4,20},{20... | collective-permute-start | bytes 1769480 | tf_op jit(solution)/shard_map/ppermute | solution.py:632
  79.3 16.6 %collective-permute-start.1 = (bf16[1536,768]{1,0:T(8,128)(2,1)}, bf16[1536,768]{1,0:T(8,128)(2,1)S(1)}, u32[]{:S(2)}, u32[]{:S(2)}) collective-permute-start(bf16[1536,768]{1,0:T(8,128)(2,1)} %get-tuple-element.119), channel_id=1, source_target_pairs={{0,16},{16,0},{1,17},{17,1},{2,18},{18,2},{3,19},{19,3},{4,20},{20... | collective-permute-start | bytes 7077896 | tf_op jit(solution)/shard_map/ppermute | solution.py:632
  79.5 16.5 %collective-permute-start.2 = (bf16[1536,768]{1,0:T(8,128)(2,1)}, bf16[1536,768]{1,0:T(8,128)(2,1)S(1)}, u32[]{:S(2)}, u32[]{:S(2)}) collective-permute-start(bf16[1536,768]{1,0:T(8,128)(2,1)} %get-tuple-element.122), channel_id=1, source_target_pairs={{0,16},{16,0},{1,17},{17,1},{2,18},{18,2},{3,19},{19,3},{4,20},{20... | collective-permute-start | bytes 7077896 | tf_op jit(solution)/shard_map/ppermute | solution.py:632
  80.7 15.3 %copy-start.2 = (bf16[1536,768]{1,0:T(8,128)(2,1)S(1)}, bf16[1536,768]{1,0:T(8,128)(2,1)}, u32[]{:S(2)}) copy-start(bf16[1536,768]{1,0:T(8,128)(2,1)} %get-tuple-element.121) | copy-start | bytes 7077892
  80.7 15.3 %copy-start.3 = (bf16[1536,768]{1,0:T(8,128)(2,1)S(1)}, bf16[1536,768]{1,0:T(8,128)(2,1)}, u32[]{:S(2)}) copy-start(bf16[1536,768]{1,0:T(8,128)(2,1)} %get-tuple-element.118) | copy-start | bytes 7077892
  80.7 15.4 %copy-start.5 = (bf16[384,768]{1,0:T(8,128)(2,1)S(1)}, bf16[384,768]{1,0:T(8,128)(2,1)}, u32[]{:S(2)}) copy-start(bf16[384,768]{1,0:T(8,128)(2,1)} %get-tuple-element.124) | copy-start | bytes 1769476
  94.7 34.7 %collective-permute-start.8 = (bf16[2,1024,384]{2,1,0:T(8,128)(2,1)S(1)}, bf16[2,1024,384]{2,1,0:T(8,128)(2,1)S(1)}, u32[]{:S(2)}, u32[]{:S(2)}) collective-permute-start(bf16[2,1024,384]{2,1,0:T(8,128)(2,1)S(1)} %get-tuple-element.146), channel_id=1, source_target_pairs={{16,0},{17,1},{18,2},{19,3},{20,4},{21,5},{22,6},{23,7},{24,8},{25... | collective-permute-start | bytes 4718600 | tf_op jit(solution)/shard_map/ppermute | solution.py:900
  100.0 26.1 %collective-permute-start.4 = (bf16[8,72,768]{2,1,0:T(8,128)(2,1)S(1)}, bf16[8,72,768]{2,1,0:T(8,128)(2,1)S(1)}, u32[]{:S(2)}, u32[]{:S(2)}) collective-permute-start(bf16[8,72,768]{2,1,0:T(8,128)(2,1)S(1)} %get-tuple-element.129), channel_id=1, source_target_pairs={{0,1},{1,0},{2,3},{3,2},{4,5},{5,4},{6,7},{7,6},{8,9},{9,8},{10,11... | collective-permute-start | bytes 2654216 | tf_op jit(solution)/shard_map/ppermute | solution.py:632
  102.4 22.5 %collective-permute-start.5 = (bf16[8,72,768]{2,1,0:T(8,128)(2,1)S(1)}, bf16[8,72,768]{2,1,0:T(8,128)(2,1)S(1)}, u32[]{:S(2)}, u32[]{:S(2)}) collective-permute-start(bf16[8,72,768]{2,1,0:T(8,128)(2,1)S(1)} %get-tuple-element.135), channel_id=1, source_target_pairs={{0,2},{1,3},{2,0},{3,1},{4,6},{5,7},{6,4},{7,5},{8,10},{9,11},{10,... | collective-permute-start | bytes 2654216 | tf_op jit(solution)/shard_map/ppermute | solution.py:632
  103.9 22.2 %collective-permute-start.6 = (bf16[8,72,768]{2,1,0:T(8,128)(2,1)S(1)}, bf16[8,72,768]{2,1,0:T(8,128)(2,1)S(1)}, u32[]{:S(2)}, u32[]{:S(2)}) collective-permute-start(bf16[8,72,768]{2,1,0:T(8,128)(2,1)S(1)} %get-tuple-element.136), channel_id=1, source_target_pairs={{0,4},{1,5},{2,6},{3,7},{4,0},{5,1},{6,2},{7,3},{8,12},{9,13},{10,... | collective-permute-start | bytes 2654216 | tf_op jit(solution)/shard_map/ppermute | solution.py:632
  119.3 10.0 %copy-start = (bf16[768,2304]{1,0:T(8,128)(2,1)S(1)}, bf16[768,2304]{1,0:T(8,128)(2,1)}, u32[]{:S(2)}) copy-start(bf16[768,2304]{1,0:T(8,128)(2,1)} %wqkv.7) | copy-start | bytes 10616836
  119.4 13.7 %collective-permute-start.7 = (bf16[2,1024,384]{2,1,0:T(8,128)(2,1)S(1)}, bf16[2,1024,384]{2,1,0:T(8,128)(2,1)S(1)}, u32[]{:S(2)}, u32[]{:S(2)}) collective-permute-start(bf16[2,1024,384]{2,1,0:T(8,128)(2,1)S(1)} %get-tuple-element.141), channel_id=1, source_target_pairs={{16,0},{17,1},{18,2},{19,3},{20,4},{21,5},{22,6},{23,7},{24,8},{25... | collective-permute-start | bytes 4718600 | tf_op jit(solution)/shard_map/ppermute | solution.py:911
  126.7 13.5 %collective-permute-start.9 = (bf16[4,72,768]{2,1,0:T(8,128)(2,1)S(1)}, bf16[4,72,768]{2,1,0:T(8,128)(2,1)S(1)}, u32[]{:S(2)}, u32[]{:S(2)}) collective-permute-start(bf16[4,72,768]{2,1,0:T(8,128)(2,1)S(1)} %get-tuple-element.144), channel_id=1, source_target_pairs={{0,2},{1,3},{2,0},{3,1},{4,6},{5,7},{6,4},{7,5},{8,10},{9,11},{10,... | collective-permute-start | bytes 1327112 | tf_op jit(solution)/shard_map/ppermute | solution.py:632
  127.3 11.6 %collective-permute-start.10 = (bf16[4,72,768]{2,1,0:T(8,128)(2,1)S(1)}, bf16[4,72,768]{2,1,0:T(8,128)(2,1)S(1)}, u32[]{:S(2)}, u32[]{:S(2)}) collective-permute-start(bf16[4,72,768]{2,1,0:T(8,128)(2,1)S(1)} %get-tuple-element.153), channel_id=1, source_target_pairs={{0,4},{1,5},{2,6},{3,7},{4,0},{5,1},{6,2},{7,3},{8,12},{9,13},{10,... | collective-permute-start | bytes 1327112 | tf_op jit(solution)/shard_map/ppermute | solution.py:632
  128.9 11.4 %collective-permute-start.11 = (bf16[4,72,768]{2,1,0:T(8,128)(2,1)S(1)}, bf16[4,72,768]{2,1,0:T(8,128)(2,1)S(1)}, u32[]{:S(2)}, u32[]{:S(2)}) collective-permute-start(bf16[4,72,768]{2,1,0:T(8,128)(2,1)S(1)} %get-tuple-element.154), channel_id=1, source_target_pairs={{0,1},{1,0},{2,3},{3,2},{4,5},{5,4},{6,7},{7,6},{8,9},{9,8},{10,11... | collective-permute-start | bytes 1327112 | tf_op jit(solution)/shard_map/ppermute | solution.py:632
  133.0 10.1 %collective-permute-start.12 = (bf16[3,384,384]{2,1,0:T(8,128)(2,1)S(1)}, bf16[3,384,384]{2,1,0:T(8,128)(2,1)S(1)}, u32[]{:S(2)}, u32[]{:S(2)}) collective-permute-start(bf16[3,384,384]{2,1,0:T(8,128)(2,1)S(1)} %get-tuple-element.161), channel_id=1, source_target_pairs={{0,16},{16,0},{1,17},{17,1},{2,18},{18,2},{3,19},{19,3},{4,20},{20... | collective-permute-start | bytes 2654216 | tf_op jit(solution)/shard_map/ppermute | solution.py:632
  136.8 4.9 %collective-permute-start.14 = (f32[8,768]{1,0:T(8,128)S(1)}, f32[8,768]{1,0:T(8,128)S(1)}, u32[]{:S(2)}, u32[]{:S(2)}) collective-permute-start(f32[8,768]{1,0:T(8,128)S(1)} %get-tuple-element.165.refs_4_), channel_id=1, source_target_pairs={{0,16},{16,0},{1,17},{17,1},{2,18},{18,2},{3,19},{19,3},{4,20},{20... | collective-permute-start | bytes 73736 | tf_op jit(solution)/shard_map/ppermute | solution.py:632
  138.9 4.2 %collective-permute-start.13 = (bf16[3,384,384]{2,1,0:T(8,128)(2,1)S(1)}, bf16[3,384,384]{2,1,0:T(8,128)(2,1)S(1)}, u32[]{:S(2)}, u32[]{:S(2)}) collective-permute-start(bf16[3,384,384]{2,1,0:T(8,128)(2,1)S(1)} %get-tuple-element.164), channel_id=1, source_target_pairs={{0,16},{16,0},{1,17},{17,1},{2,18},{18,2},{3,19},{19,3},{4,20},{20... | collective-permute-start | bytes 2654216 | tf_op jit(solution)/shard_map/ppermute | solution.py:632
  140.6 9.4 %collective-permute-start.15 = (bf16[2,72,768]{2,1,0:T(8,128)(2,1)S(1)}, bf16[2,72,768]{2,1,0:T(8,128)(2,1)S(1)}, u32[]{:S(2)}, u32[]{:S(2)}) collective-permute-start(bf16[2,72,768]{2,1,0:T(8,128)(2,1)S(1)} %get-tuple-element.159), channel_id=1, source_target_pairs={{0,4},{1,5},{2,6},{3,7},{4,0},{5,1},{6,2},{7,3},{8,12},{9,13},{10,... | collective-permute-start | bytes 663560 | tf_op jit(solution)/shard_map/ppermute | solution.py:632
  141.1 8.4 %collective-permute-start.16 = (bf16[2,72,768]{2,1,0:T(8,128)(2,1)S(1)}, bf16[2,72,768]{2,1,0:T(8,128)(2,1)S(1)}, u32[]{:S(2)}, u32[]{:S(2)}) collective-permute-start(bf16[2,72,768]{2,1,0:T(8,128)(2,1)S(1)} %get-tuple-element.172), channel_id=1, source_target_pairs={{0,1},{1,0},{2,3},{3,2},{4,5},{5,4},{6,7},{7,6},{8,9},{9,8},{10,11... | collective-permute-start | bytes 663560 | tf_op jit(solution)/shard_map/ppermute | solution.py:632
  141.7 8.3 %collective-permute-start.17 = (bf16[2,72,768]{2,1,0:T(8,128)(2,1)S(1)}, bf16[2,72,768]{2,1,0:T(8,128)(2,1)S(1)}, u32[]{:S(2)}, u32[]{:S(2)}) collective-permute-start(bf16[2,72,768]{2,1,0:T(8,128)(2,1)S(1)} %get-tuple-element.173), channel_id=1, source_target_pairs={{0,2},{1,3},{2,0},{3,1},{4,6},{5,7},{6,4},{7,5},{8,10},{9,11},{10,... | collective-permute-start | bytes 663560 | tf_op jit(solution)/shard_map/ppermute | solution.py:632
  143.8 14.6 %collective-permute-start.18 = (bf16[608,384]{1,0:T(8,128)(2,1)S(1)}, bf16[608,384]{1,0:T(8,128)(2,1)S(1)}, u32[]{:S(2)}, u32[]{:S(2)}) collective-permute-start(bf16[608,384]{1,0:T(8,128)(2,1)S(1)} %get-tuple-element.166), channel_id=1, source_target_pairs={{0,1},{1,0},{2,3},{3,2},{4,5},{5,4},{6,7},{7,6},{8,9},{9,8},{10,11... | collective-permute-start | bytes 1400840 | tf_op jit(solution)/shard_map/ppermute | solution.py:632
  145.4 12.8 %collective-permute-start.19 = (bf16[8,72,384]{2,1,0:T(8,128)(2,1)S(1)}, bf16[8,72,384]{2,1,0:T(8,128)(2,1)S(1)}, u32[]{:S(2)}, u32[]{:S(2)}) collective-permute-start(bf16[8,72,384]{2,1,0:T(8,128)(2,1)S(1)} %get-tuple-element.180), channel_id=1, source_target_pairs={{0,2},{1,3},{2,0},{3,1},{4,6},{5,7},{6,4},{7,5},{8,10},{9,11},{10,... | collective-permute-start | bytes 1327112 | tf_op jit(solution)/shard_map/ppermute | solution.py:632
  150.2 16.1 %collective-permute-start.20 = (bf16[1,216,768]{2,1,0:T(8,128)(2,1)S(1)}, bf16[1,216,768]{2,1,0:T(8,128)(2,1)S(1)}, u32[]{:S(2)}, u32[]{:S(2)}) collective-permute-start(bf16[1,216,768]{2,1,0:T(8,128)(2,1)S(1)} %get-tuple-element.174), channel_id=1, source_target_pairs={{0,8},{1,9},{2,10},{3,11},{4,12},{5,13},{6,14},{7,15},{8,0},{9,1},... | collective-permute-start | bytes 995336 | tf_op jit(solution)/shard_map/ppermute | solution.py:632
  158.7 7.8 %collective-permute-start.21 = (bf16[320,384]{1,0:T(8,128)(2,1)S(1)}, bf16[320,384]{1,0:T(8,128)(2,1)S(1)}, u32[]{:S(2)}, u32[]{:S(2)}) collective-permute-start(bf16[320,384]{1,0:T(8,128)(2,1)S(1)} %get-tuple-element.186), channel_id=1, source_target_pairs={{0,2},{1,3},{2,0},{3,1},{4,6},{5,7},{6,4},{7,5},{8,10},{9,11},{10,... | collective-permute-start | bytes 737288 | tf_op jit(solution)/shard_map/ppermute | solution.py:632
  160.2 6.3 %collective-permute-start.22 = (bf16[4,72,384]{2,1,0:T(8,128)(2,1)S(1)}, bf16[4,72,384]{2,1,0:T(8,128)(2,1)S(1)}, u32[]{:S(2)}, u32[]{:S(2)}) collective-permute-start(bf16[4,72,384]{2,1,0:T(8,128)(2,1)S(1)} %get-tuple-element.187), channel_id=1, source_target_pairs={{0,1},{1,0},{2,3},{3,2},{4,5},{5,4},{6,7},{7,6},{8,9},{9,8},{10,11... | collective-permute-start | bytes 663560 | tf_op jit(solution)/shard_map/ppermute | solution.py:632
  166.7 7.7 %collective-permute-start.23 = (bf16[320,384]{1,0:T(8,128)(2,1)S(1)}, bf16[320,384]{1,0:T(8,128)(2,1)S(1)}, u32[]{:S(2)}, u32[]{:S(2)}) collective-permute-start(bf16[320,384]{1,0:T(8,128)(2,1)S(1)} %get-tuple-element.190), channel_id=1, source_target_pairs={{0,4},{1,5},{2,6},{3,7},{4,0},{5,1},{6,2},{7,3},{8,12},{9,13},{10,... | collective-permute-start | bytes 737288 | tf_op jit(solution)/shard_map/ppermute | solution.py:632
  174.4 8.2 %collective-permute-start.24 = (bf16[176,384]{1,0:T(8,128)(2,1)S(1)}, bf16[176,384]{1,0:T(8,128)(2,1)S(1)}, u32[]{:S(2)}, u32[]{:S(2)}) collective-permute-start(bf16[176,384]{1,0:T(8,128)(2,1)S(1)} %get-tuple-element.193), channel_id=1, source_target_pairs={{0,8},{1,9},{2,10},{3,11},{4,12},{5,13},{6,14},{7,15},{8,0},{9,1},... | collective-permute-start | bytes 405512 | tf_op jit(solution)/shard_map/ppermute | solution.py:632
  (10 other events, 63.0 us)
